TPU v7x, 512 devices: a whole 4x8x8 slice. The times are simulated.
512 devices in a mesh: rows: 64 (over x, z, core), cols: 8 (over y).
Axes of the slice: x: 4, y: 8, z: 8, core: 2. Of those that a mesh axis runs over, the one named last changes fastest.
Arguments:
- columns: float32 [65536, 3072], P('rows', 'cols'), may hold values from -4 to 4
- row_bases: float32 [4, 65536, 128], P(None, 'rows'), may hold values from -6 to 6
- order: int32 [64, 1024], P('rows'), may hold values from 0 to 1023, each once within a row
Outputs:
- solved: float32 [65536, 2560], P('rows', 'cols')
Inputs may be any that keep to these rules, and one draw needn't show every extreme that they name: Each row of order is a permutation of 0 to 1023.
All inputs are finite; a program needn't handle non-finite values.
Results may differ from a plain program's by a relative error of at most 0.01.
Values sent between devices are 32-bit elements; how exact they have to be, the bound alone decides.
No kernel may reach another device: no remote copies, remote signals or barrier semaphores. Data moves between devices by JAX's collectives and lax.ppermute only.
A program may use at most 64 MiB of HBM per device.

v0:
```python
import math

import jax
import jax.numpy as jnp
from jax import lax
from jax.sharding import PartitionSpec as P

R = 128
LEVELS = 4
TGT_DEV = 320


HIGH = lax.Precision.HIGHEST


def partner(block, axis, apart):
    count = lax.axis_size(axis)
    route = []
    for low in range(count):
        high = low | 1 << apart
        if high != low and high < count:
            route += [(low, high), (high, low)]
    return lax.ppermute(block, axis, route)


def from_everyone(shard, axis):
    devices = lax.axis_size(axis)
    return lax.all_to_all(
        jnp.broadcast_to(shard[None], (devices, *shard.shape)), axis, 0, 0, tiled=True
    )


def joined_along(tiles, dim):
    lengths = list(tiles.shape[1:])
    lengths[dim] *= tiles.shape[0]
    return jnp.moveaxis(tiles, 0, dim).reshape(lengths)


def gather_directly(shard, axis, dim):
    tiles = from_everyone(shard, axis)
    return joined_along(tiles, dim)


def gather_turned(arrays, axis, dims):
    turned = [jnp.moveaxis(a, dim, 0) for a, dim in zip(arrays, dims)]
    widths = [t[0].size for t in turned]
    both = jnp.concatenate([t.reshape(-1, w) for t, w in zip(turned, widths)], axis=1)
    result = lax.all_gather(both, axis, axis=0, tiled=True)
    tiles = jnp.split(result, [sum(widths[:k]) for k in range(1, len(widths))], axis=1)
    return tuple(
        (
            jnp.moveaxis(b.reshape(-1, *t.shape[1:]), 0, dim)
            for b, t, dim in zip(tiles, turned, dims)
        )
    )


def solve_system(coupled, right_side):
    gram = jnp.einsum("ki,kj->ij", coupled, coupled, precision=HIGH)
    factor = jnp.linalg.cholesky(gram)
    projected = jnp.einsum("ki,kq->iq", coupled, right_side, precision=HIGH)
    middle = lax.linalg.triangular_solve(factor, projected, left_side=True, lower=True)
    return lax.linalg.triangular_solve(factor, middle, left_side=True, lower=True, transpose_a=True)


def whole_sums(partial_value, bits):
    for step in range(bits):
        partial_value = partial_value + partner(partial_value, "rows", step)
    return (partial_value, partner(partial_value, "rows", bits))


def on_device(columns, row_bases, order):
    rows_dev = columns.shape[0]
    row_count = lax.axis_size("rows")
    col_count = lax.axis_size("cols")
    width_block = R // col_count
    depth = row_count.bit_length() - 1
    position = lax.axis_index("rows")
    places = order[0]
    tree = jnp.take(columns, places, axis=0)
    for level in range(LEVELS):
        bits = depth - LEVELS + level
        scale = 0.55 / math.sqrt(R * rows_dev * (1 << bits))
        start = TGT_DEV + (LEVELS - 1 - level) * width_block
        upper = tree[:, :start]
        basis = gather_directly(tree[:, start : start + width_block], "cols", 1)
        feats = row_bases[level]
        partial_value = scale * jnp.einsum(
            "cr,cq->rq", feats, tree[:, : start + width_block], precision=HIGH
        )
        own_sum, sibling = whole_sums(partial_value, bits)
        own_proj, sibling_proj = (own_sum[:, :start], sibling[:, :start])
        own_couple, sibling_couple = (own_sum[:, start:], sibling[:, start:])
        own_couple, sibling_couple = gather_turned((own_couple, sibling_couple), "cols", (1, 1))
        first_child = position >> bits & 1 == 0
        couple_a = jnp.where(first_child, own_couple, sibling_couple)
        couple_b = jnp.where(first_child, sibling_couple, own_couple)
        proj_a = jnp.where(first_child, own_proj, sibling_proj)
        proj_b = jnp.where(first_child, sibling_proj, own_proj)
        ident = jnp.eye(R, dtype=couple_a.dtype)
        system = jnp.concatenate(
            [
                jnp.concatenate([ident, couple_b], axis=1),
                jnp.concatenate([couple_a, ident], axis=1),
            ],
            axis=0,
        )
        coeffs = solve_system(system, jnp.concatenate([proj_b, proj_a], axis=0))
        mine = jnp.where(first_child, coeffs[:R], coeffs[R:])
        upper = upper - jnp.dot(basis, mine, precision=HIGH)
        tree = jnp.concatenate([upper, tree[:, start:]], axis=1)
    targets = tree[:, :TGT_DEV]
    return jnp.zeros_like(targets).at[places].set(targets)


def solution(mesh):
    placed = (P("rows", "cols"), P(None, "rows", None), P("rows", None))
    return jax.shard_map(
        on_device, mesh=mesh, in_specs=placed, out_specs=P("rows", "cols"), check_vma=False
    )
```

profile of v0, /device:TPU:1, one launch (start us, length us, event | category | flops | bytes accessed | tf_op | source)
XLA Modules:
  0.0 599.5 jit_solution(16359245087713541908)
XLA Ops:
  1.4 3.5 gather_fusion
  8.1 2.4 fusion
  10.6 8.7 %collective-permute-start = (f32[128,384]{0,1:T(8,128)S(1)}, f32[128,384]{0,1:T(8,128)S(1)}, u32[]{:S(2)}, u32[]{:S(2)}) collective-permute-start(f32[128,384]{0,1:T(8,128)S(1)} %fusion), channel_id=1, source_target_pairs={{0,8},{8,0},{16,24},{24,16},{32,40},{40,32},{48,56},{56,48},{64,72... | collective-permute-start | bytes 589832 | tf_op jit(solution)/shard_map/ppermute | solution.py:23
  20.2 4.1 all-to-all-start
  26.4 6.5 %collective-permute-done.1 = f32[128,384]{0,1:T(8,128)S(1)} collective-permute-done((f32[128,384]{0,1:T(8,128)S(1)}, f32[128,384]{0,1:T(8,128)S(1)}, u32[]{:S(2)}, u32[]{:S(2)}) %collective-permute-start.1) | collective-permute-done | bytes 196640 | tf_op jit(solution)/shard_map/ppermute | solution.py:23
  32.9 3.8 collective-permute-start.2
  36.6 9.7 %collective-permute-done.2 = f32[128,384]{0,1:T(8,128)S(1)} collective-permute-done((f32[128,384]{0,1:T(8,128)S(1)}, f32[128,384]{0,1:T(8,128)S(1)}, u32[]{:S(2)}, u32[]{:S(2)}) %collective-permute-start.2) | collective-permute-done | bytes 196640 | tf_op jit(solution)/shard_map/ppermute | solution.py:23
  47.0 19.3 %all_gather.12 = f32[128,256]{1,0:T(8,128)S(1)} all-gather(f32[16,256]{1,0:T(8,128)S(1)} %pad_maximum_fusion.8), channel_id=1, replica_groups=mesh['rows'=64,'cols'=8] {'cols'}, dimensions={0}, use_global_device_ids=true | all-gather | bytes 147456 | tf_op jit(solution)/shard_map/all_gather | solution.py:48
  69.9 11.7 %cholesky.214 = f32[128,128]{1,0:T(8,128)S(1)} custom-call(f32[128,128]{1,0:T(8,128)S(1)} %cholesky.346), custom_call_target="Cholesky" | custom-call | tf_op jit(solution)/shard_map/jit(cholesky)/cholesky | solution.py:60
  81.7 10.4 %custom-call.35 = f32[1,128,128]{1,2,0:T(8,128)} custom-call(f32[1,128,128]{2,1,0:T(8,128)S(1)} %get-tuple-element.109), custom_call_target="InvertDiagBlocksLowerTriangular" | custom-call | tf_op jit(solution)/shard_map/jit(cholesky)/cholesky | solution.py:60
  95.0 13.2 %cholesky.231 = f32[128,128]{1,0:T(8,128)} custom-call(f32[128,128]{1,0:T(8,128)} %convolution_subtract_fusion.14), custom_call_target="Cholesky" | custom-call | tf_op jit(solution)/shard_map/jit(cholesky)/cholesky | solution.py:60
  112.7 5.7 while.4
  118.4 21.1 %custom-call.28 = f32[2,128,128]{1,2,0:T(8,128)} custom-call(f32[2,128,128]{2,1,0:T(8,128)} %get-tuple-element.13), custom_call_target="InvertDiagBlocksLowerTriangular" | custom-call | tf_op jit(solution)/shard_map/triangular_solve | solution.py:63
  144.1 2.4 slice_subtract_fusion
  146.5 2.8 fusion.1
  149.3 9.1 %collective-permute-start.3 = (f32[128,368]{0,1:T(8,128)S(1)}, f32[128,368]{0,1:T(8,128)S(1)}, u32[]{:S(2)}, u32[]{:S(2)}) collective-permute-start(f32[128,368]{0,1:T(8,128)S(1)} %fusion.1), channel_id=1, source_target_pairs={{0,8},{8,0},{16,24},{24,16},{32,40},{40,32},{48,56},{56,48},{64,72... | collective-permute-start | bytes 565256 | tf_op jit(solution)/shard_map/ppermute | solution.py:23
  161.4 5.8 collective-permute-done.4
  167.3 3.9 collective-permute-start.5
  172.9 5.5 all-to-all-start.1
  180.3 7.6 %collective-permute-start.6 = (f32[128,368]{0,1:T(8,128)S(1)}, f32[128,368]{0,1:T(8,128)S(1)}, u32[]{:S(2)}, u32[]{:S(2)}) collective-permute-start(f32[128,368]{0,1:T(8,128)S(1)} %add.105), channel_id=1, source_target_pairs={{0,64},{64,0},{8,72},{72,8},{16,80},{80,16},{24,88},{88,24},{32,96... | collective-permute-start | bytes 565256 | tf_op jit(solution)/shard_map/ppermute | solution.py:23
  187.9 7.0 %collective-permute-done.6 = f32[128,368]{0,1:T(8,128)S(1)} collective-permute-done((f32[128,368]{0,1:T(8,128)S(1)}, f32[128,368]{0,1:T(8,128)S(1)}, u32[]{:S(2)}, u32[]{:S(2)}) %collective-permute-start.6) | collective-permute-done | bytes 188448 | tf_op jit(solution)/shard_map/ppermute | solution.py:23
  195.6 18.8 %all_gather.13 = f32[128,256]{1,0:T(8,128)S(1)} all-gather(f32[16,256]{1,0:T(8,128)S(1)} %pad_maximum_fusion.9), channel_id=1, replica_groups=mesh['rows'=64,'cols'=8] {'cols'}, dimensions={0}, use_global_device_ids=true | all-gather | bytes 147456 | tf_op jit(solution)/shard_map/all_gather | solution.py:48
  215.0 11.7 %cholesky.248 = f32[128,128]{1,0:T(8,128)S(1)} custom-call(f32[128,128]{1,0:T(8,128)S(1)} %cholesky.349), custom_call_target="Cholesky" | custom-call | tf_op jit(solution)/shard_map/jit(cholesky)/cholesky | solution.py:60
  226.8 9.8 %custom-call.36 = f32[1,128,128]{1,2,0:T(8,128)S(1)} custom-call(f32[1,128,128]{2,1,0:T(8,128)S(1)} %get-tuple-element.105), custom_call_target="InvertDiagBlocksLowerTriangular" | custom-call | tf_op jit(solution)/shard_map/jit(cholesky)/cholesky | solution.py:60
  237.1 11.7 %cholesky.265 = f32[128,128]{1,0:T(8,128)S(1)} custom-call(f32[128,128]{1,0:T(8,128)S(1)} %convolution_subtract_fusion.13), custom_call_target="Cholesky" | custom-call | tf_op jit(solution)/shard_map/jit(cholesky)/cholesky | solution.py:60
  251.3 3.8 while.5
  255.1 20.3 %custom-call.29 = f32[2,128,128]{1,2,0:T(8,128)} custom-call(f32[2,128,128]{2,1,0:T(8,128)S(1)} %get-tuple-element.21), custom_call_target="InvertDiagBlocksLowerTriangular" | custom-call | tf_op jit(solution)/shard_map/triangular_solve | solution.py:63
  278.5 2.3 convolution_subtract_fusion
  280.9 2.7 fusion.2
  283.6 9.5 %collective-permute-start.7 = (f32[128,352]{0,1:T(8,128)S(1)}, f32[128,352]{0,1:T(8,128)S(1)}, u32[]{:S(2)}, u32[]{:S(2)}) collective-permute-start(f32[128,352]{0,1:T(8,128)S(1)} %fusion.2), channel_id=1, source_target_pairs={{0,8},{8,0},{16,24},{24,16},{32,40},{40,32},{48,56},{56,48},{64,72... | collective-permute-start | bytes 540680 | tf_op jit(solution)/shard_map/ppermute | solution.py:23
  294.1 3.6 collective-permute-start.8
  297.7 4.5 collective-permute-done.8
  302.2 4.4 collective-permute-start.9
  306.6 7.9 %collective-permute-done.9 = f32[128,352]{0,1:T(8,128)S(1)} collective-permute-done((f32[128,352]{0,1:T(8,128)S(1)}, f32[128,352]{0,1:T(8,128)S(1)}, u32[]{:S(2)}, u32[]{:S(2)}) %collective-permute-start.9) | collective-permute-done | bytes 180256 | tf_op jit(solution)/shard_map/ppermute | solution.py:23
  314.6 8.1 %collective-permute-start.10 = (f32[128,352]{0,1:T(8,128)S(1)}, f32[128,352]{0,1:T(8,128)S(1)}, u32[]{:S(2)}, u32[]{:S(2)}) collective-permute-start(f32[128,352]{0,1:T(8,128)S(1)} %add.108), channel_id=1, source_target_pairs={{0,64},{64,0},{8,72},{72,8},{16,80},{80,16},{24,88},{88,24},{32,96... | collective-permute-start | bytes 540680 | tf_op jit(solution)/shard_map/ppermute | solution.py:23
  324.3 5.5 all-to-all-start.2
  329.8 3.1 collective-permute-start.11
  332.9 3.4 collective-permute-done.11
  337.0 21.1 %all_gather.14 = f32[128,256]{1,0:T(8,128)S(1)} all-gather(f32[16,256]{1,0:T(8,128)S(1)} %pad_maximum_fusion.10), channel_id=1, replica_groups=mesh['rows'=64,'cols'=8] {'cols'}, dimensions={0}, use_global_device_ids=true | all-gather | bytes 147456 | tf_op jit(solution)/shard_map/all_gather | solution.py:48
  358.7 11.7 %cholesky.282 = f32[128,128]{1,0:T(8,128)S(1)} custom-call(f32[128,128]{1,0:T(8,128)S(1)} %cholesky.352), custom_call_target="Cholesky" | custom-call | tf_op jit(solution)/shard_map/jit(cholesky)/cholesky | solution.py:60
  370.5 9.8 %custom-call.37 = f32[1,128,128]{1,2,0:T(8,128)S(1)} custom-call(f32[1,128,128]{2,1,0:T(8,128)S(1)} %get-tuple-element.101), custom_call_target="InvertDiagBlocksLowerTriangular" | custom-call | tf_op jit(solution)/shard_map/jit(cholesky)/cholesky | solution.py:60
  380.8 11.7 %cholesky.299 = f32[128,128]{1,0:T(8,128)S(1)} custom-call(f32[128,128]{1,0:T(8,128)S(1)} %convolution_subtract_fusion.12), custom_call_target="Cholesky" | custom-call | tf_op jit(solution)/shard_map/jit(cholesky)/cholesky | solution.py:60
  395.4 4.3 while.6
  399.7 20.3 %custom-call.30 = f32[2,128,128]{1,2,0:T(8,128)} custom-call(f32[2,128,128]{2,1,0:T(8,128)S(1)} %get-tuple-element.29), custom_call_target="InvertDiagBlocksLowerTriangular" | custom-call | tf_op jit(solution)/shard_map/triangular_solve | solution.py:63
  429.1 2.7 fusion.3
  431.8 10.3 %collective-permute-start.12 = (f32[128,336]{0,1:T(8,128)S(1)}, f32[128,336]{0,1:T(8,128)S(1)}, u32[]{:S(2)}, u32[]{:S(2)}) collective-permute-start(f32[128,336]{0,1:T(8,128)S(1)} %fusion.3), channel_id=1, source_target_pairs={{0,8},{8,0},{16,24},{24,16},{32,40},{40,32},{48,56},{56,48},{64,72... | collective-permute-start | bytes 516104 | tf_op jit(solution)/shard_map/ppermute | solution.py:23
  445.1 5.5 collective-permute-done.13
  450.6 3.2 collective-permute-start.14
  453.9 9.5 %collective-permute-done.14 = f32[128,336]{0,1:T(8,128)S(1)} collective-permute-done((f32[128,336]{0,1:T(8,128)S(1)}, f32[128,336]{0,1:T(8,128)S(1)}, u32[]{:S(2)}, u32[]{:S(2)}) %collective-permute-start.14) | collective-permute-done | bytes 172064 | tf_op jit(solution)/shard_map/ppermute | solution.py:23
  463.4 3.2 collective-permute-start.15
  466.6 10.8 %collective-permute-done.15 = f32[128,336]{0,1:T(8,128)S(1)} collective-permute-done((f32[128,336]{0,1:T(8,128)S(1)}, f32[128,336]{0,1:T(8,128)S(1)}, u32[]{:S(2)}, u32[]{:S(2)}) %collective-permute-start.15) | collective-permute-done | bytes 172064 | tf_op jit(solution)/shard_map/ppermute | solution.py:23
  477.4 3.1 collective-permute-start.16
  482.2 5.0 all-to-all-start.3
  487.3 4.3 collective-permute-start.17
  491.6 3.8 collective-permute-done.17
  496.1 20.4 %all_gather.15 = f32[128,256]{1,0:T(8,128)S(1)} all-gather(f32[16,256]{1,0:T(8,128)S(1)} %pad_maximum_fusion.11), channel_id=1, replica_groups=mesh['rows'=64,'cols'=8] {'cols'}, dimensions={0}, use_global_device_ids=true | all-gather | bytes 147456 | tf_op jit(solution)/shard_map/all_gather | solution.py:48
  517.2 11.7 %cholesky.316 = f32[128,128]{1,0:T(8,128)S(1)} custom-call(f32[128,128]{1,0:T(8,128)S(1)} %cholesky.355), custom_call_target="Cholesky" | custom-call | tf_op jit(solution)/shard_map/jit(cholesky)/cholesky | solution.py:60
  529.0 9.8 %custom-call.38 = f32[1,128,128]{1,2,0:T(8,128)S(1)} custom-call(f32[1,128,128]{2,1,0:T(8,128)S(1)} %get-tuple-element.97), custom_call_target="InvertDiagBlocksLowerTriangular" | custom-call | tf_op jit(solution)/shard_map/jit(cholesky)/cholesky | solution.py:60
  539.3 11.7 %cholesky.333 = f32[128,128]{1,0:T(8,128)S(1)} custom-call(f32[128,128]{1,0:T(8,128)S(1)} %convolution_subtract_fusion.11), custom_call_target="Cholesky" | custom-call | tf_op jit(solution)/shard_map/jit(cholesky)/cholesky | solution.py:60
  553.7 4.1 while.7
  557.8 20.3 %custom-call.31 = f32[2,128,128]{1,2,0:T(8,128)} custom-call(f32[2,128,128]{2,1,0:T(8,128)S(1)} %get-tuple-element.37), custom_call_target="InvertDiagBlocksLowerTriangular" | custom-call | tf_op jit(solution)/shard_map/triangular_solve | solution.py:63
  585.9 3.2 convolution_subtract_fusion.2
  589.0 3.0 copy.18
  592.0 5.8 scatter_custom_fusion
  (229 shorter events, 84.2 us)
Async XLA Ops:
  0.0 1.4 copy-start
  4.9 1.7 copy-start.29
  10.6 13.8 %collective-permute-start = (f32[128,384]{0,1:T(8,128)S(1)}, f32[128,384]{0,1:T(8,128)S(1)}, u32[]{:S(2)}, u32[]{:S(2)}) collective-permute-start(f32[128,384]{0,1:T(8,128)S(1)} %fusion), channel_id=1, source_target_pairs={{0,8},{8,0},{16,24},{24,16},{32,40},{40,32},{48,56},{56,48},{64,72... | collective-permute-start | bytes 589832 | tf_op jit(solution)/shard_map/ppermute | solution.py:23
  20.2 123.9 %all-to-all-start = ((f32[8,1024,16]{1,2,0:T(8,128)}), f32[8,1024,16]{1,2,0:T(8,128)}, u32[]{:S(2)}, u32[]{:S(2)}) async-start(f32[8,1024,16]{1,2,0:T(8,128)} %broadcast_in_dim.24), calls=%async_computation | async-start | bytes 1048576 | tf_op jit(solution)/shard_map/all_to_all | solution.py:28
  24.4 8.4 %collective-permute-start.1 = (f32[128,384]{0,1:T(8,128)S(1)}, f32[128,384]{0,1:T(8,128)S(1)}, u32[]{:S(2)}, u32[]{:S(2)}) collective-permute-start(f32[128,384]{0,1:T(8,128)S(1)} %add.101), channel_id=1, source_target_pairs={{0,16},{16,0},{8,24},{24,8},{32,48},{48,32},{40,56},{56,40},{64,80... | collective-permute-start | bytes 589832 | tf_op jit(solution)/shard_map/ppermute | solution.py:23
  26.3 249.1 %copy-start.9 = (f32[128,128]{0,1:T(8,128)}, f32[128,128]{0,1:T(8,128)S(1)}, u32[]{:S(2)}) copy-start(f32[128,128]{0,1:T(8,128)S(1)} %fusion.70) | copy-start | bytes 196612
  32.9 33.5 %copy-start.14 = (f32[128,384]{0,1:T(8,128)}, f32[128,384]{0,1:T(8,128)S(1)}, u32[]{:S(2)}) copy-start(f32[128,384]{0,1:T(8,128)S(1)} %add.102) | copy-start | bytes 589828
  32.9 13.4 %collective-permute-start.2 = (f32[128,384]{0,1:T(8,128)S(1)}, f32[128,384]{0,1:T(8,128)S(1)}, u32[]{:S(2)}, u32[]{:S(2)}) collective-permute-start(f32[128,384]{0,1:T(8,128)S(1)} %add.102), channel_id=1, source_target_pairs={{0,32},{32,0},{8,40},{40,8},{16,48},{48,16},{24,56},{56,24},{64,96... | collective-permute-start | bytes 589832 | tf_op jit(solution)/shard_map/ppermute | solution.py:23
  46.3 0.7 copy-start.24
  66.3 0.6 copy-start.21
  66.3 0.6 copy-start.23
  69.2 0.7 copy-start.13
  92.1 48.4 %copy-start.22 = (f32[128,128]{0,1:T(8,128)S(1)}, f32[128,128]{0,1:T(8,128)}, u32[]{:S(2)}) copy-start(f32[128,128]{0,1:T(8,128)} %copy-done.21) | copy-start | bytes 196612
  109.0 1.9 copy-start.12
  139.4 2.4 copy-start.15
  146.5 20.8 %copy-start.1 = (f32[1024,368]{0,1:T(8,128)}, f32[1024,368]{0,1:T(8,128)S(1)}, u32[]{:S(2)}) copy-start(f32[1024,368]{0,1:T(8,128)S(1)} %slice_subtract_fusion) | copy-start | bytes 4521988
  149.3 10.1 %collective-permute-start.3 = (f32[128,368]{0,1:T(8,128)S(1)}, f32[128,368]{0,1:T(8,128)S(1)}, u32[]{:S(2)}, u32[]{:S(2)}) collective-permute-start(f32[128,368]{0,1:T(8,128)S(1)} %fusion.1), channel_id=1, source_target_pairs={{0,8},{8,0},{16,24},{24,16},{32,40},{40,32},{48,56},{56,48},{64,72... | collective-permute-start | bytes 565256 | tf_op jit(solution)/shard_map/ppermute | solution.py:23
  159.5 7.8 %collective-permute-start.4 = (f32[128,368]{0,1:T(8,128)S(1)}, f32[128,368]{0,1:T(8,128)S(1)}, u32[]{:S(2)}, u32[]{:S(2)}) collective-permute-start(f32[128,368]{0,1:T(8,128)S(1)} %add.103), channel_id=1, source_target_pairs={{0,16},{16,0},{8,24},{24,8},{32,48},{48,32},{40,56},{56,40},{64,80... | collective-permute-start | bytes 565256 | tf_op jit(solution)/shard_map/ppermute | solution.py:23
  167.3 13.0 %collective-permute-start.5 = (f32[128,368]{0,1:T(8,128)S(1)}, f32[128,368]{0,1:T(8,128)S(1)}, u32[]{:S(2)}, u32[]{:S(2)}) collective-permute-start(f32[128,368]{0,1:T(8,128)S(1)} %add.104), channel_id=1, source_target_pairs={{0,32},{32,0},{8,40},{40,8},{16,48},{48,16},{24,56},{56,24},{64,96... | collective-permute-start | bytes 565256 | tf_op jit(solution)/shard_map/ppermute | solution.py:23
  172.9 105.6 %all-to-all-start.1 = ((f32[8,1024,16]{1,2,0:T(8,128)}), f32[8,1024,16]{1,2,0:T(8,128)}, u32[]{:S(2)}, u32[]{:S(2)}) async-start(f32[8,1024,16]{1,2,0:T(8,128)} %broadcast_in_dim.25), calls=%async_computation.1 | async-start | bytes 1048576 | tf_op jit(solution)/shard_map/all_to_all | solution.py:28
  180.3 14.6 %collective-permute-start.6 = (f32[128,368]{0,1:T(8,128)S(1)}, f32[128,368]{0,1:T(8,128)S(1)}, u32[]{:S(2)}, u32[]{:S(2)}) collective-permute-start(f32[128,368]{0,1:T(8,128)S(1)} %add.105), channel_id=1, source_target_pairs={{0,64},{64,0},{8,72},{72,8},{16,80},{80,16},{24,88},{88,24},{32,96... | collective-permute-start | bytes 565256 | tf_op jit(solution)/shard_map/ppermute | solution.py:23
  194.9 0.7 copy-start.25
  215.0 60.4 %copy-start.26 = (f32[128,368]{0,1:T(8,128)S(1)}, f32[128,368]{0,1:T(8,128)}, u32[]{:S(2)}) copy-start(f32[128,368]{0,1:T(8,128)} %copy-done.25) | copy-start | bytes 565252
  275.4 0.9 copy-start.17
  276.3 2.2 copy-start.2
  280.9 21.3 %copy-start.3 = (f32[1024,352]{0,1:T(8,128)}, f32[1024,352]{0,1:T(8,128)S(1)}, u32[]{:S(2)}) copy-start(f32[1024,352]{0,1:T(8,128)S(1)} %convolution_subtract_fusion) | copy-start | bytes 4325380
  283.6 10.5 %collective-permute-start.7 = (f32[128,352]{0,1:T(8,128)S(1)}, f32[128,352]{0,1:T(8,128)S(1)}, u32[]{:S(2)}, u32[]{:S(2)}) collective-permute-start(f32[128,352]{0,1:T(8,128)S(1)} %fusion.2), channel_id=1, source_target_pairs={{0,8},{8,0},{16,24},{24,16},{32,40},{40,32},{48,56},{56,48},{64,72... | collective-permute-start | bytes 540680 | tf_op jit(solution)/shard_map/ppermute | solution.py:23
  294.1 8.0 %collective-permute-start.8 = (f32[128,352]{0,1:T(8,128)S(1)}, f32[128,352]{0,1:T(8,128)S(1)}, u32[]{:S(2)}, u32[]{:S(2)}) collective-permute-start(f32[128,352]{0,1:T(8,128)S(1)} %add.106), channel_id=1, source_target_pairs={{0,16},{16,0},{8,24},{24,8},{32,48},{48,32},{40,56},{56,40},{64,80... | collective-permute-start | bytes 540680 | tf_op jit(solution)/shard_map/ppermute | solution.py:23
  302.2 56.0 %copy-start.10 = (f32[128,128]{0,1:T(8,128)S(1)}, f32[128,128]{0,1:T(8,128)}, u32[]{:S(2)}) copy-start(f32[128,128]{0,1:T(8,128)} %copy-done.9) | copy-start | bytes 196612
  302.2 12.4 %collective-permute-start.9 = (f32[128,352]{0,1:T(8,128)S(1)}, f32[128,352]{0,1:T(8,128)S(1)}, u32[]{:S(2)}, u32[]{:S(2)}) collective-permute-start(f32[128,352]{0,1:T(8,128)S(1)} %add.107), channel_id=1, source_target_pairs={{0,32},{32,0},{8,40},{40,8},{16,48},{48,16},{24,56},{56,24},{64,96... | collective-permute-start | bytes 540680 | tf_op jit(solution)/shard_map/ppermute | solution.py:23
  314.6 15.2 %collective-permute-start.10 = (f32[128,352]{0,1:T(8,128)S(1)}, f32[128,352]{0,1:T(8,128)S(1)}, u32[]{:S(2)}, u32[]{:S(2)}) collective-permute-start(f32[128,352]{0,1:T(8,128)S(1)} %add.108), channel_id=1, source_target_pairs={{0,64},{64,0},{8,72},{72,8},{16,80},{80,16},{24,88},{88,24},{32,96... | collective-permute-start | bytes 540680 | tf_op jit(solution)/shard_map/ppermute | solution.py:23
  324.3 102.6 %all-to-all-start.2 = ((f32[8,1024,16]{1,2,0:T(8,128)}), f32[8,1024,16]{1,2,0:T(8,128)S(1)}, u32[]{:S(2)}, u32[]{:S(2)}) async-start(f32[8,1024,16]{1,2,0:T(8,128)} %broadcast_in_dim.44), calls=%async_computation.2 | async-start | bytes 1048576 | tf_op jit(solution)/shard_map/all_to_all | solution.py:28
  329.8 6.5 %collective-permute-start.11 = (f32[128,352]{0,1:T(8,128)S(1)}, f32[128,352]{0,1:T(8,128)S(1)}, u32[]{:S(2)}, u32[]{:S(2)}) collective-permute-start(f32[128,352]{0,1:T(8,128)S(1)} %add.109), channel_id=1, source_target_pairs={{0,128},{128,0},{8,136},{136,8},{16,144},{144,16},{24,152},{152,24... | collective-permute-start | bytes 540680 | tf_op jit(solution)/shard_map/ppermute | solution.py:23
  336.4 0.7 copy-start.27
  358.1 37.2 %copy-start.19 = (f32[128,128]{0,1:T(8,128)}, f32[128,128]{0,1:T(8,128)S(1)}, u32[]{:S(2)}) copy-start(f32[128,128]{0,1:T(8,128)S(1)} %get-tuple-element.89) | copy-start | bytes 196612
  399.7 21.3 %copy-start.8 = (f32[256,256]{1,0:T(8,128)}, f32[256,256]{1,0:T(8,128)S(1)}, u32[]{:S(2)}) copy-start(f32[256,256]{1,0:T(8,128)S(1)} %get-tuple-element.303) | copy-start | bytes 786436
  420.0 2.3 copy-start.18
  422.3 4.6 copy-start.4
  429.1 34.3 %copy-start.5 = (f32[1024,336]{0,1:T(8,128)}, f32[1024,336]{0,1:T(8,128)S(1)}, u32[]{:S(2)}) copy-start(f32[1024,336]{0,1:T(8,128)S(1)} %convolution_subtract_fusion.1) | copy-start | bytes 4128772
  431.8 11.3 %collective-permute-start.12 = (f32[128,336]{0,1:T(8,128)S(1)}, f32[128,336]{0,1:T(8,128)S(1)}, u32[]{:S(2)}, u32[]{:S(2)}) collective-permute-start(f32[128,336]{0,1:T(8,128)S(1)} %fusion.3), channel_id=1, source_target_pairs={{0,8},{8,0},{16,24},{24,16},{32,40},{40,32},{48,56},{56,48},{64,72... | collective-permute-start | bytes 516104 | tf_op jit(solution)/shard_map/ppermute | solution.py:23
  443.2 7.5 %collective-permute-start.13 = (f32[128,336]{0,1:T(8,128)S(1)}, f32[128,336]{0,1:T(8,128)S(1)}, u32[]{:S(2)}, u32[]{:S(2)}) collective-permute-start(f32[128,336]{0,1:T(8,128)S(1)} %add.110), channel_id=1, source_target_pairs={{0,16},{16,0},{8,24},{24,8},{32,48},{48,32},{40,56},{56,40},{64,80... | collective-permute-start | bytes 516104 | tf_op jit(solution)/shard_map/ppermute | solution.py:23
  450.6 12.8 %collective-permute-start.14 = (f32[128,336]{0,1:T(8,128)S(1)}, f32[128,336]{0,1:T(8,128)S(1)}, u32[]{:S(2)}, u32[]{:S(2)}) collective-permute-start(f32[128,336]{0,1:T(8,128)S(1)} %add.111), channel_id=1, source_target_pairs={{0,32},{32,0},{8,40},{40,8},{16,48},{48,16},{24,56},{56,24},{64,96... | collective-permute-start | bytes 516104 | tf_op jit(solution)/shard_map/ppermute | solution.py:23
  463.4 53.2 %copy-start.11 = (f32[128,128]{0,1:T(8,128)S(1)}, f32[128,128]{0,1:T(8,128)}, u32[]{:S(2)}) copy-start(f32[128,128]{0,1:T(8,128)} %copy-done.9) | copy-start | bytes 196612
  463.4 13.9 %collective-permute-start.15 = (f32[128,336]{0,1:T(8,128)S(1)}, f32[128,336]{0,1:T(8,128)S(1)}, u32[]{:S(2)}, u32[]{:S(2)}) collective-permute-start(f32[128,336]{0,1:T(8,128)S(1)} %add.112), channel_id=1, source_target_pairs={{0,64},{64,0},{8,72},{72,8},{16,80},{80,16},{24,88},{88,24},{32,96... | collective-permute-start | bytes 516104 | tf_op jit(solution)/shard_map/ppermute | solution.py:23
  477.4 9.8 %collective-permute-start.16 = (f32[128,336]{0,1:T(8,128)S(1)}, f32[128,336]{0,1:T(8,128)S(1)}, u32[]{:S(2)}, u32[]{:S(2)}) collective-permute-start(f32[128,336]{0,1:T(8,128)S(1)} %add.113), channel_id=1, source_target_pairs={{0,128},{128,0},{8,136},{136,8},{16,144},{144,16},{24,152},{152,24... | collective-permute-start | bytes 516104 | tf_op jit(solution)/shard_map/ppermute | solution.py:23
  482.2 103.6 %all-to-all-start.3 = ((f32[8,1024,16]{1,2,0:T(8,128)}), f32[8,1024,16]{1,2,0:T(8,128)S(1)}, u32[]{:S(2)}, u32[]{:S(2)}) async-start(f32[8,1024,16]{1,2,0:T(8,128)} %broadcast_in_dim.45), calls=%async_computation.3 | async-start | bytes 1048576 | tf_op jit(solution)/shard_map/all_to_all | solution.py:28
  487.3 8.2 %collective-permute-start.17 = (f32[128,336]{0,1:T(8,128)S(1)}, f32[128,336]{0,1:T(8,128)S(1)}, u32[]{:S(2)}, u32[]{:S(2)}) collective-permute-start(f32[128,336]{0,1:T(8,128)S(1)} %add.114), channel_id=1, source_target_pairs={{0,256},{256,0},{8,264},{264,8},{16,272},{272,16},{24,280},{280,24... | collective-permute-start | bytes 516104 | tf_op jit(solution)/shard_map/ppermute | solution.py:23
  495.5 0.7 copy-start.28
  516.6 37.1 %copy-start.20 = (f32[128,128]{0,1:T(8,128)}, f32[128,128]{0,1:T(8,128)S(1)}, u32[]{:S(2)}) copy-start(f32[128,128]{0,1:T(8,128)S(1)} %get-tuple-element.87) | copy-start | bytes 196612
  557.8 21.3 %copy-start.7 = (f32[256,256]{1,0:T(8,128)}, f32[256,256]{1,0:T(8,128)S(1)}, u32[]{:S(2)}) copy-start(f32[256,256]{1,0:T(8,128)S(1)} %get-tuple-element.300) | copy-start | bytes 786436
  578.1 4.7 copy-start.16
  580.4 5.4 copy-start.6
where the time goes:
time: 611 us; the launch traced here: 600 us
  other arithmetic  231 us (38%)
  starting transfers between devices  112 us (18%)
  blocking collectives  79.7 us (13%)
  waiting for transfers between devices  79.4 us (13%)
  matrix products  45.2 us (7%)
  local copies, waits for them, and re-layouts  45.1 us (7%)
  between operations  6.38 us (1%)
    another operation x27, other arithmetic, solve_system(): factor = jnp.linalg.cholesky(gram)  141 us
    ppermute x18, starting transfers between devices, partner(): return lax.ppermute(block, axis, route)  91.6 us
    another operation x9, other arithmetic, solve_system(): lax.linalg.triangular_solve(factor, middle, left_side=True, lower=True, t...  83 us
    all_gather x4, blocking collectives, gather_turned(): result = lax.all_gather(both, axis, axis=0, tiled=True)  79.7 us
    ppermute x18, waiting for transfers between devices, partner(): return lax.ppermute(block, axis, route)  79.4 us
    all_to_all x4, starting transfers between devices, from_everyone(): lax.all_to_all(jnp.broadcast_to(shard[None], (devices, *shard.shape)), ax...  20.1 us
    another operation x24, local copies, waits for them, and re-layouts  16.7 us
  transfers between devices with their start and end apart: 22, of which 15 were waited for; matrix products, arithmetic and copies ran while one was open for 46% of the time, Pallas kernels for 0%

commit v1 on v0

v1 whole, which is shorter than its diff:
```python
import functools
import math

import jax
import jax.numpy as jnp
from jax import lax
from jax.experimental import pallas as pl
from jax.experimental.pallas import tpu as pltpu
from jax.sharding import Mesh, PartitionSpec as P

R = 128
LEVELS = 4
WB = 16
GROUPS = 8
ROW_AXES = ("x2", "x1", "z4", "z2", "z1", "core")
HIGH = lax.Precision.HIGHEST
F32 = jnp.float32
BF16 = jnp.bfloat16


def halves(x):
    hi = x.astype(BF16)
    return hi, (x - hi.astype(F32)).astype(BF16)


def mm(a, b):
    dot = functools.partial(jnp.dot, preferred_element_type=F32)
    return dot(a[0], b[0]) + (dot(a[0], b[1]) + dot(a[1], b[0]))


def exact(a, b, dims):
    return lax.dot_general(a, b, ((dims[0], dims[1]), ((), ())), precision=HIGH, preferred_element_type=F32)


def spd_inverse(g):
    lane = lax.broadcasted_iota(jnp.int32, (8, R), 1)
    sub = lax.broadcasted_iota(jnp.int32, (8, R), 0)
    n = R // 8
    tiles = [g[8 * i : 8 * i + 8, :] for i in range(n)]
    full = lambda v: jnp.broadcast_to(v, (8, R))
    for k in range(0, R, 4):
        p, s = k // 8, k % 8
        cols = [[full(tiles[i][:, k + j : k + j + 1]) for i in range(n)] for j in range(4)]
        panel = (lane >= k) & (lane < k + 4)
        rows = [
            jnp.where(lane == k + j, 1.0, jnp.where(panel, 0.0, full(tiles[p][s + j : s + j + 1, :])))
            for j in range(4)
        ]
        d = [[full(cols[j][p][s + i : s + i + 1, :]) for j in range(4)] for i in range(4)]
        r = 1.0 / (d[0][0] * d[1][1] - d[0][1] * d[1][0])
        p00, p01, p10, p11 = d[1][1] * r, -d[0][1] * r, -d[1][0] * r, d[0][0] * r
        e = [
            [p00 * d[0][2] + p01 * d[1][2], p00 * d[0][3] + p01 * d[1][3]],
            [p10 * d[0][2] + p11 * d[1][2], p10 * d[0][3] + p11 * d[1][3]],
        ]
        c = [
            [d[2 + i][2 + j] - (d[2 + i][0] * e[0][j] + d[2 + i][1] * e[1][j]) for j in range(2)]
            for i in range(2)
        ]
        q = 1.0 / (c[0][0] * c[1][1] - c[0][1] * c[1][0])
        t0 = p00 * rows[0] + p01 * rows[1]
        t1 = p10 * rows[0] + p11 * rows[1]
        u0 = rows[2] - (d[2][0] * t0 + d[2][1] * t1)
        u1 = rows[3] - (d[3][0] * t0 + d[3][1] * t1)
        v0 = (c[1][1] * u0 - c[0][1] * u1) * q
        v1 = (c[0][0] * u1 - c[1][0] * u0) * q
        new = [t0 - (e[0][0] * v0 + e[0][1] * v1), t1 - (e[1][0] * v0 + e[1][1] * v1), v0, v1]
        for i in range(n):
            a = jnp.where(panel, 0.0, tiles[i])
            for j in range(4):
                a = a - cols[j][i] * new[j]
            if i == p:
                for j in range(4):
                    a = jnp.where(sub == s + j, new[j], a)
            tiles[i] = a
    return jnp.concatenate(tiles, axis=0)


def pair_inverse(own, sib):
    i = lax.broadcasted_iota(jnp.int32, (R, R), 0)
    j = lax.broadcasted_iota(jnp.int32, (R, R), 1)
    m = jnp.where(i == j, 1.0, 0.0) - exact(own, sib, ((1,), (0,)))
    return exact(spd_inverse(exact(m, m, ((0,), (0,)))), m, ((1,), (1,)))


def coefficients(p_own, p_sib, a_own, a_sib, inv):
    c_own = mm(halves(p_sib - mm(halves(p_own), a_sib)), inv)
    c_own_h = halves(c_own)
    c_sib_h = halves(p_own - mm(c_own_h, a_own))
    return c_own, c_own_h, c_sib_h


def project_kernel(order_ref, x_ref, v_ref, scale, ht_ref, hw_ref):
    rows, width = x_ref.shape
    tgt = width - LEVELS * WB
    xt = x_ref[...].T
    hi, lo = halves(xt)
    at = lax.broadcasted_iota(jnp.int32, (rows, rows), 0)
    onehot = jnp.where(at == order_ref[...], 1.0, 0.0).astype(BF16)
    hi = jnp.dot(hi, onehot, preferred_element_type=F32).astype(BF16)
    lo = jnp.dot(lo, onehot, preferred_element_type=F32).astype(BF16)
    for level in range(LEVELS):
        h = mm((hi, lo), halves(v_ref[level])) * scale[level]
        ht_ref[:, R * level : R * level + R] = h[:tgt]
        for m in range(LEVELS):
            at_m = tgt + (LEVELS - 1 - m) * WB
            hw_ref[m * WB : m * WB + WB, R * level : R * level + R] = h[at_m : at_m + WB]


def block(ref, side, row, lanes):
    part = ref[side, :, row : row + WB, lanes]
    return part.reshape(GROUPS * WB, part.shape[-1])


def first_kernel(side_ref, crit_ref, inv_ref, next_ref):
    own, sib = side_ref[0], 1 - side_ref[0]
    lo, hi = slice(0, R), slice(R, 2 * R)
    a_own, a_sib = block(crit_ref, own, 0, lo), block(crit_ref, sib, 0, lo)
    inv = pair_inverse(a_own, a_sib)
    inv_ref[...] = inv
    _, c_own, c_sib = coefficients(
        block(crit_ref, own, WB, lo), block(crit_ref, sib, WB, lo), halves(a_own), halves(a_sib), halves(inv)
    )
    next_ref[...] = (block(crit_ref, own, WB, hi) + block(crit_ref, sib, WB, hi)) - (
        mm(c_own, halves(block(crit_ref, own, 0, hi))) + mm(c_sib, halves(block(crit_ref, sib, 0, hi)))
    )


def first_update_kernel(side_ref, inv_ref, crit_ref, rest_ref, t_own_ref, t_sib_ref, next_ref, c_ref):
    own, sib = side_ref[0], 1 - side_ref[0]
    lo, hi, more, deep = slice(0, R), slice(R, 2 * R), slice(0, 2 * R), slice(2 * R, 6 * R)

    def whole(side, t_ref):
        top = jnp.concatenate([block(crit_ref, side, 0, slice(0, 2 * R)), block(rest_ref, side, 0, more)], axis=1)
        second = jnp.concatenate([block(crit_ref, side, WB, slice(0, 2 * R)), block(rest_ref, side, WB, more)], axis=1)
        third, fourth = block(rest_ref, side, 0, deep), block(rest_ref, side, WB, deep)
        return top, jnp.concatenate([second, third, fourth, t_ref[...]], axis=0)

    top_own, low_own = whole(own, t_own_ref)
    top_sib, low_sib = whole(sib, t_sib_ref)
    update(top_own, low_own, top_sib, low_sib, inv_ref[...], next_ref, c_ref)


def update(top_own, low_own, top_sib, low_sib, inv, next_ref, c_ref):
    a_own, a_sib = halves(top_own[:, :R]), halves(top_sib[:, :R])
    c, c_own, c_sib = coefficients(low_own[:, :R], low_sib[:, :R], a_own, a_sib, halves(inv))
    c_ref[...] = c
    if next_ref is not None:
        next_ref[...] = (low_own[:, R:] + low_sib[:, R:]) - (
            mm(c_own, halves(top_own[:, R:])) + mm(c_sib, halves(top_sib[:, R:]))
        )


def inverse_kernel(own_ref, sib_ref, inv_ref):
    inv_ref[...] = pair_inverse(own_ref[...], sib_ref[...])


def update_kernel(inv_ref, own_ref, sib_ref, next_ref, c_ref):
    update(own_ref[:R], own_ref[R:], sib_ref[:R], sib_ref[R:], inv_ref[...], next_ref, c_ref)


def total_kernel(a_own_ref, a_sib_ref, t_own_ref, t_sib_ref, c0_ref, c1_ref, c2_ref, k_ref):
    a_own, a_sib = a_own_ref[...], a_sib_ref[...]
    inv = pair_inverse(a_own, a_sib)
    k3, k3h, _ = coefficients(t_own_ref[...], t_sib_ref[...], halves(a_own), halves(a_sib), halves(inv))
    w = lambda ref, m: halves(ref[m * R : m * R + R])
    k2 = c2_ref[R:] - mm(k3h, w(c2_ref, 0))
    k2h = halves(k2)
    k1 = c1_ref[2 * R :] - (mm(k2h, w(c1_ref, 0)) + mm(k3h, w(c1_ref, 1)))
    k1h = halves(k1)
    k0 = c0_ref[3 * R :] - (mm(k1h, w(c0_ref, 0)) + mm(k2h, w(c0_ref, 1)) + mm(k3h, w(c0_ref, 2)))
    for level, k in enumerate((k0, k1, k2, k3)):
        k_ref[:, R * level : R * level + R] = k


def final_kernel(core_ref, x_ref, w_ref, k_own_ref, k_sib_ref, out_ref):
    tgt = out_ref.shape[1]
    half = tgt // 2
    core = core_ref[0]
    rows = x_ref.shape[0]
    own, sib = k_own_ref[...], k_sib_ref[...]
    k = halves(jnp.concatenate([jnp.where(core == 0, own, sib), jnp.where(core == 0, sib, own)], axis=0))
    total = jnp.zeros((tgt, rows), F32)
    for level in range(LEVELS):
        at = (LEVELS - 1 - level) * WB
        w = halves(w_ref[:, at : at + WB, :].reshape(GROUPS * WB, rows))
        part = slice(R * level, R * level + R)
        total = total + mm((k[0][:, part], k[1][:, part]), w)
    out_ref[...] = x_ref[:, :tgt] - total.T


def call(kernel, outs, name, scalar=False):
    shapes = [jax.ShapeDtypeStruct(s, F32) for s in outs]
    single = len(shapes) == 1
    vmem = pl.BlockSpec(memory_space=pltpu.VMEM)

    def run(*args):
        specs = [vmem] * len(args)
        if scalar:
            specs[0] = pl.BlockSpec(memory_space=pltpu.SMEM)
        return pl.pallas_call(
            kernel,
            out_shape=shapes[0] if single else shapes,
            in_specs=specs,
            out_specs=vmem if single else [vmem] * len(shapes),
            name=name,
            compiler_params=pltpu.CompilerParams(vmem_limit_bytes=56 * 2**20),
        )(*args)

    return run


def swap(v, axis):
    return lax.ppermute(v, axis, [(0, 1), (1, 0)])


def gather(v, axes):
    n = lax.axis_size(axes)
    return lax.all_to_all(jnp.broadcast_to(v[None], (n, *v.shape)), axes, 0, 0, tiled=True)


def after(v, token):
    return lax.optimization_barrier((v, token))[0]


def on_device(columns, row_bases, order):
    rows, width = columns.shape
    tgt = width - LEVELS * WB
    half = tgt // 2
    scale = [0.55 / math.sqrt(R * rows * (4 << level)) for level in range(LEVELS)]
    core = lax.axis_index("core")
    side = lax.axis_index("z2").astype(jnp.int32)[None]

    def project(order_ref, x_ref, v_ref, ht_ref, hw_ref):
        project_kernel(order_ref, x_ref, v_ref, scale, ht_ref, hw_ref)

    ht, hw = call(project, [(tgt, LEVELS * R), (LEVELS * WB, LEVELS * R)], "project")(order, columns, row_bases)

    hw = hw + swap(hw, "core")
    hw = hw + swap(hw, "z1")
    crit = gather(hw[: 2 * WB, : 2 * R], ("z2", "cols")).reshape(2, GROUPS, 2 * WB, 2 * R)
    keep = lax.dynamic_slice_in_dim(ht, core * half, half, 0)
    give = lax.dynamic_slice_in_dim(ht, (1 - core) * half, half, 0)
    t_own = keep + swap(give, "core")
    t_own = t_own + swap(t_own, "z1")
    t_sib = swap(t_own, "z2")
    rest = jnp.concatenate([hw[: 2 * WB, 2 * R :], hw[2 * WB :]], axis=1)
    rest = gather(rest, ("z2", "cols")).reshape(2, GROUPS, 2 * WB, 6 * R)

    inv, a_own = call(first_kernel, [(R, R), (R, R)], "first", True)(side, crit)
    a_sib = swap(a_own, "z4")
    own, c0 = call(first_update_kernel, [(3 * R + half, 3 * R), (3 * R + half, R)], "first_update", True)(
        side, inv, crit, rest, t_own, t_sib
    )
    sib = swap(own, "z4")
    wt = after(columns[:, tgt:], inv).T
    basis = gather(wt, "cols")

    inv = call(inverse_kernel, [(R, R)], "inverse1")(a_own, a_sib)
    own, c1 = call(update_kernel, [(2 * R + half, 2 * R), (2 * R + half, R)], "update1")(inv, own, sib)
    a_own = own[:R, :R]
    a_sib = swap(a_own, "x1")
    sib = swap(own, "x1")
    inv = call(inverse_kernel, [(R, R)], "inverse2")(a_own, a_sib)
    own, c2 = call(update_kernel, [(R + half, R), (R + half, R)], "update2")(inv, own, sib)
    a_own, t_own = own[:R], own[R:]
    a_sib = swap(a_own, "x2")
    t_sib = swap(t_own, "x2")
    k = call(total_kernel, [(half, LEVELS * R)], "total")(a_own, a_sib, t_own, t_sib, c0, c1, c2)
    k_sib = swap(k, "core")
    return call(final_kernel, [(rows, tgt)], "final", True)(core.astype(jnp.int32)[None], columns, basis, k, k_sib)


def solution(mesh):
    fine = Mesh(mesh.devices.reshape(2, 2, 2, 2, 2, 2, GROUPS), (*ROW_AXES, "cols"))
    placed = (P(ROW_AXES, "cols"), P(None, ROW_AXES, None), P(ROW_AXES, None))
    return jax.shard_map(on_device, mesh=fine, in_specs=placed, out_specs=P(ROW_AXES, "cols"), check_vma=False)
```

time: 611 us -> 275 us (0.45); the launches traced: 600 us -> 274 us
  other arithmetic: 231 us -> 1.04 us
  blocking collectives: 79.7 us -> 0 us
  Pallas kernels: 0 us -> 63.2 us
  matrix products: 45.2 us -> 0 us
  waiting for transfers between devices: 79.4 us -> 118 us
  starting transfers between devices: 112 us -> 74.8 us
  local copies, waits for them, and re-layouts: 45.1 us -> 16.8 us
  between operations: 6.38 us -> 0.25 us
    another operation x36 -> x0, other arithmetic: 224 us -> none  [the longest x27 141 us: solve_system(): factor = jnp.linalg.cholesky(gram)]
    all_gather x4 -> x0, blocking collectives: 79.7 us -> none  [gather_turned(): result = lax.all_gather(both, axis, axis=0, tiled=True)]
    pallas_call x0 -> x9, Pallas kernels: none -> 63.2 us  [run(): pl.pallas_call(kernel, out_shape=shapes[0] if single else shapes, in_spec...]
    all_to_all x4 -> x3, waiting for transfers between devices: 0.01 us -> 39.8 us  [gather(): lax.all_to_all(jnp.broadcast_to(v[None], (n, *v.shape)), axes, 0, 0, tile...]
    ppermute x18 -> x12, starting transfers between devices: 91.6 us -> 53.1 us  [swap(): return lax.ppermute(v, axis, [(0, 1), (1, 0)])]
    dot_general x16 -> x0, matrix products: 26.8 us -> none  [the longest x4 10.6 us: on_device(): jnp.einsum('cr,cq->rq', feats, tree[:, :start + width_block], precision=H...]
    another operation x32 -> x0, matrix products: 18.5 us -> none  [the longest x12 7.37 us: solve_system(): lax.linalg.triangular_solve(factor, middle, left_side=True, lower=True, t...]
    another operation x33 -> x0, local copies, waits for them, and re-layouts: 16.8 us -> none
  transfers between devices with their start and end apart: 22 -> 15, of which waited for: 15 -> 11; matrix products, arithmetic and copies ran while one was open for 46% -> 2% of each run, Pallas kernels for 0% -> 18%
where the time goes in v1:
time: 275 us; the launch traced here: 274 us
  waiting for transfers between devices  118 us (43%)
  starting transfers between devices  74.8 us (27%)
  Pallas kernels  63.2 us (23%)
  local copies, waits for them, and re-layouts  16.8 us (6%)
    ppermute x12, waiting for transfers between devices, swap(): return lax.ppermute(v, axis, [(0, 1), (1, 0)])  78.1 us
    pallas_call x9, Pallas kernels, run(): pl.pallas_call(kernel, out_shape=shapes[0] if single else shapes, in_spec...  63.2 us
    ppermute x12, starting transfers between devices, swap(): return lax.ppermute(v, axis, [(0, 1), (1, 0)])  53.1 us
    all_to_all x3, waiting for transfers between devices, gather(): lax.all_to_all(jnp.broadcast_to(v[None], (n, *v.shape)), axes, 0, 0, tile...  39.8 us
    all_to_all x3, starting transfers between devices, gather(): lax.all_to_all(jnp.broadcast_to(v[None], (n, *v.shape)), axes, 0, 0, tile...  21.7 us
    unnamed x34, local copies, waits for them, and re-layouts  5.83 us
  transfers between devices with their start and end apart: 15, of which 11 were waited for; matrix products, arithmetic and copies ran while one was open for 2% of the time, Pallas kernels for 18%

profile of v1, /device:TPU:1, one launch (start us, length us, event | category | flops | bytes accessed | tf_op | source)
XLA Modules:
  0.0 273.9 jit_solution(10982370833818762626)
XLA Ops:
  0.0 7.4 %project.1 = (f32[320,512]{1,0:T(8,128)}, f32[64,512]{1,0:T(8,128)}) custom-call(s32[1,1024]{1,0:T(1,128)} %order_ref.1, f32[1024,384]{1,0:T(8,128)} %x_ref.3, f32[4,1024,128]{2,1,0:T(8,128)} %v_ref.1), custom_call_target="tpu_custom_call" | custom-call | tf_op jit(solution)/shard_map/project/pallas_call | solution.py:201
  7.4 8.7 %collective-permute-start = (f32[64,512]{1,0:T(8,128)}, f32[64,512]{1,0:T(8,128)S(1)}, u32[]{:S(2)}, u32[]{:S(2)}) collective-permute-start(f32[64,512]{1,0:T(8,128)} %get-tuple-element.16), channel_id=1, source_target_pairs={{0,8},{8,0},{1,9},{9,1},{2,10},{10,2},{3,11},{11,3},{4,12},{12,4},... | collective-permute-start | bytes 393224 | tf_op jit(solution)/shard_map/ppermute | solution.py:214
  16.1 1.2 collective-permute-done
  17.3 0.9 add.18
  18.2 1.9 collective-permute-start.1
  20.2 4.7 %collective-permute-done.1 = f32[64,512]{1,0:T(8,128)S(1)} collective-permute-done((f32[64,512]{1,0:T(8,128)S(1)}, f32[64,512]{1,0:T(8,128)S(1)}, u32[]{:S(2)}, u32[]{:S(2)}) %collective-permute-start.1) | collective-permute-done | bytes 131104 | tf_op jit(solution)/shard_map/ppermute | solution.py:214
  24.9 0.9 broadcast_in_dim.12
  25.7 6.1 %all-to-all-start = ((f32[16,32,256]{2,1,0:T(8,128)}), f32[16,32,256]{2,1,0:T(8,128)S(1)}, u32[]{:S(2)}, u32[]{:S(2)}) async-start(f32[16,32,256]{2,1,0:T(8,128)} %broadcast_in_dim.12), calls=%async_computation | async-start | bytes 1048576 | tf_op jit(solution)/shard_map/all_to_all | solution.py:219
  31.9 13.8 %all-to-all-done = f32[16,32,256]{2,1,0:T(8,128)S(1)} async-done(((f32[16,32,256]{2,1,0:T(8,128)}), f32[16,32,256]{2,1,0:T(8,128)S(1)}, u32[]{:S(2)}, u32[]{:S(2)}) %all-to-all-start) | async-done | bytes 524320 | tf_op jit(solution)/shard_map/all_to_all | solution.py:219
  45.7 1.4 broadcast_in_dim.28
  47.1 0.0 copy-done.2
  47.1 6.9 %all-to-all-start.2 = ((f32[16,32,768]{2,1,0:T(8,128)}), f32[16,32,768]{2,1,0:T(8,128)S(1)}, u32[]{:S(2)}, u32[]{:S(2)}) async-start(f32[16,32,768]{2,1,0:T(8,128)} %broadcast_in_dim.28), calls=%async_computation.2 | async-start | bytes 3145728 | tf_op jit(solution)/shard_map/all_to_all | solution.py:219
  54.0 1.2 slice.21
  55.2 10.4 %first.1 = (f32[128,128]{1,0:T(8,128)}, f32[128,128]{1,0:T(8,128)}) custom-call(s32[1]{0:T(128)} %bitcast.1.side_ref, f32[2,8,32,256]{3,2,1,0:T(8,128)} %bitcast.6), custom_call_target="tpu_custom_call" | custom-call | tf_op jit(solution)/shard_map/first/pallas_call | solution.py:201
  65.6 0.2 copy.4
  65.8 25.9 %all-to-all-done.2 = f32[16,32,768]{2,1,0:T(8,128)S(1)} async-done(((f32[16,32,768]{2,1,0:T(8,128)}), f32[16,32,768]{2,1,0:T(8,128)S(1)}, u32[]{:S(2)}, u32[]{:S(2)}) %all-to-all-start.2) | async-done | bytes 1572896 | tf_op jit(solution)/shard_map/all_to_all | solution.py:219
  91.7 1.8 broadcast_in_dim.13
  93.5 0.1 copy-done.1
  93.6 8.7 %all-to-all-start.1 = ((f32[8,64,1024]{2,1,0:T(8,128)}), f32[8,64,1024]{2,1,0:T(8,128)S(1)}, u32[]{:S(2)}, u32[]{:S(2)}) async-start(f32[8,64,1024]{2,1,0:T(8,128)} %broadcast_in_dim.13), calls=%async_computation.1 | async-start | bytes 4194304 | tf_op jit(solution)/shard_map/all_to_all | solution.py:219
  102.2 0.0 copy-done.5
  102.3 3.6 %collective-permute-start.3 = (f32[160,512]{1,0:T(8,128)S(1)}, f32[160,512]{1,0:T(8,128)S(1)}, u32[]{:S(2)}, u32[]{:S(2)}) collective-permute-start(f32[160,512]{1,0:T(8,128)S(1)} %constant_dynamic-slice_fusion), channel_id=1, source_target_pairs={{0,8},{8,0},{1,9},{9,1},{2,10},{10,2},{3,11},{11,3},{4,12},{12,4},... | collective-permute-start | bytes 983048 | tf_op jit(solution)/shard_map/ppermute | solution.py:214
  105.8 1.2 collective-permute-done.3
  107.1 4.1 %collective-permute-start.4 = (f32[160,512]{1,0:T(8,128)S(1)}, f32[160,512]{1,0:T(8,128)S(1)}, u32[]{:S(2)}, u32[]{:S(2)}) collective-permute-start(f32[160,512]{1,0:T(8,128)S(1)} %dynamic-slice_add_fusion), channel_id=1, source_target_pairs={{0,16},{16,0},{1,17},{17,1},{2,18},{18,2},{3,19},{19,3},{4,20},{20... | collective-permute-start | bytes 983048 | tf_op jit(solution)/shard_map/ppermute | solution.py:214
  111.2 7.7 %collective-permute-done.4 = f32[160,512]{1,0:T(8,128)S(1)} collective-permute-done((f32[160,512]{1,0:T(8,128)S(1)}, f32[160,512]{1,0:T(8,128)S(1)}, u32[]{:S(2)}, u32[]{:S(2)}) %collective-permute-start.4) | collective-permute-done | bytes 327712 | tf_op jit(solution)/shard_map/ppermute | solution.py:214
  119.0 5.6 %collective-permute-start.5 = (f32[160,512]{1,0:T(8,128)S(1)}, f32[160,512]{1,0:T(8,128)S(1)}, u32[]{:S(2)}, u32[]{:S(2)}) collective-permute-start(f32[160,512]{1,0:T(8,128)S(1)} %add.23.t_own_ref), channel_id=1, source_target_pairs={{0,32},{32,0},{1,33},{33,1},{2,34},{34,2},{3,35},{35,3},{4,36},{36... | collective-permute-start | bytes 983048 | tf_op jit(solution)/shard_map/ppermute | solution.py:214
  124.6 14.3 %collective-permute-done.5.t_sib_ref = f32[160,512]{1,0:T(8,128)S(1)} collective-permute-done((f32[160,512]{1,0:T(8,128)S(1)}, f32[160,512]{1,0:T(8,128)S(1)}, u32[]{:S(2)}, u32[]{:S(2)}) %collective-permute-start.5) | collective-permute-done | bytes 327712 | tf_op jit(solution)/shard_map/ppermute | solution.py:214
  138.8 0.0 copy-done.3
  138.8 0.7 copy-done.9
  139.6 4.2 %first_update.1 = (f32[544,384]{1,0:T(8,128)}, f32[544,128]{1,0:T(8,128)}) custom-call(s32[1]{0:T(128)} %bitcast.1.side_ref, f32[128,128]{1,0:T(8,128)} %get-tuple-element.17.inv_ref, f32[2,8,32,256]{3,2,1,0:T(8,128)} %bitcast.7, f32[2,8,32,768]{3,2,1,0:T(8,128)} %bitcast.5, f32[160,512]{1,0:T(8,128)} %copy-done.3, f32[160,512]{1,0:T(8,128)} %copy-done.9), custom_call_target="tpu_custom_call" | custom-call | tf_op jit(solution)/shard_map/first_update/pallas_call | solution.py:201
  143.8 8.7 %collective-permute-start.6 = (f32[544,384]{1,0:T(8,128)}, f32[544,384]{1,0:T(8,128)S(1)}, u32[]{:S(2)}, u32[]{:S(2)}) collective-permute-start(f32[544,384]{1,0:T(8,128)} %get-tuple-element.21.own_ref), channel_id=1, source_target_pairs={{0,64},{64,0},{1,65},{65,1},{2,66},{66,2},{3,67},{67,3},{4,68},{68... | collective-permute-start | bytes 2506760 | tf_op jit(solution)/shard_map/ppermute | solution.py:214
  152.5 2.1 collective-permute-start.2
  154.6 36.7 %collective-permute-done.2.sib_ref = f32[128,128]{1,0:T(8,128)S(1)} collective-permute-done((f32[128,128]{1,0:T(8,128)S(1)}, f32[128,128]{1,0:T(8,128)S(1)}, u32[]{:S(2)}, u32[]{:S(2)}) %collective-permute-start.2) | collective-permute-done | bytes 65568 | tf_op jit(solution)/shard_map/ppermute | solution.py:214
  191.4 0.6 copy-done.15
  192.0 8.9 %inverse1.1.inv_ref = f32[128,128]{1,0:T(8,128)} custom-call(f32[128,128]{1,0:T(8,128)} %get-tuple-element.19.own_ref, f32[128,128]{1,0:T(8,128)} %copy-done.15), custom_call_target="tpu_custom_call" | custom-call | tf_op jit(solution)/shard_map/inverse1/pallas_call | solution.py:201
  200.9 0.0 collective-permute-done.6.sib_ref
  200.9 0.9 copy-done.4
  201.8 3.4 %update1.1 = (f32[416,256]{1,0:T(8,128)}, f32[416,128]{1,0:T(8,128)}) custom-call(f32[128,128]{1,0:T(8,128)} %inverse1.1.inv_ref, f32[544,384]{1,0:T(8,128)} %get-tuple-element.21.own_ref, f32[544,384]{1,0:T(8,128)} %copy-done.4), custom_call_target="tpu_custom_call" | custom-call | tf_op jit(solution)/shard_map/update1/pallas_call | solution.py:201
  205.2 3.1 %collective-permute-start.8 = (f32[416,256]{1,0:T(8,128)}, f32[416,256]{1,0:T(8,128)S(1)}, u32[]{:S(2)}, u32[]{:S(2)}) collective-permute-start(f32[416,256]{1,0:T(8,128)} %get-tuple-element.22.own_ref), channel_id=1, source_target_pairs={{0,128},{128,0},{1,129},{129,1},{2,130},{130,2},{3,131},{131,3},{4... | collective-permute-start | bytes 1277960 | tf_op jit(solution)/shard_map/ppermute | solution.py:214
  208.3 0.9 slice.25.own_ref
  209.1 2.1 collective-permute-start.7
  211.3 6.7 %collective-permute-done.7.sib_ref = f32[128,128]{1,0:T(8,128)S(1)} collective-permute-done((f32[128,128]{1,0:T(8,128)S(1)}, f32[128,128]{1,0:T(8,128)S(1)}, u32[]{:S(2)}, u32[]{:S(2)}) %collective-permute-start.7) | collective-permute-done | bytes 65568 | tf_op jit(solution)/shard_map/ppermute | solution.py:214
  218.0 0.0 copy-done.11
  218.0 0.6 copy-done.16
  218.6 8.9 %inverse2.1.inv_ref = f32[128,128]{1,0:T(8,128)} custom-call(f32[128,128]{1,0:T(8,128)} %copy-done.11, f32[128,128]{1,0:T(8,128)} %copy-done.16), custom_call_target="tpu_custom_call" | custom-call | tf_op jit(solution)/shard_map/inverse2/pallas_call | solution.py:201
  227.5 0.0 collective-permute-done.8.sib_ref
  227.5 0.8 copy-done.6
  228.3 2.7 update2.1
  230.9 0.9 slice.27.t_own_ref
  231.8 4.6 %collective-permute-start.10 = (f32[160,128]{1,0:T(8,128)S(1)}, f32[160,128]{1,0:T(8,128)S(1)}, u32[]{:S(2)}, u32[]{:S(2)}) collective-permute-start(f32[160,128]{1,0:T(8,128)S(1)} %slice.27.t_own_ref), channel_id=1, source_target_pairs={{0,256},{256,0},{1,257},{257,1},{2,258},{258,2},{3,259},{259,3},{4... | collective-permute-start | bytes 245768 | tf_op jit(solution)/shard_map/ppermute | solution.py:214
  236.4 0.8 slice.26.a_own_ref
  237.3 2.4 collective-permute-start.9
  239.7 4.1 %collective-permute-done.9.a_sib_ref = f32[128,128]{1,0:T(8,128)S(1)} collective-permute-done((f32[128,128]{1,0:T(8,128)S(1)}, f32[128,128]{1,0:T(8,128)S(1)}, u32[]{:S(2)}, u32[]{:S(2)}) %collective-permute-start.9) | collective-permute-done | bytes 65568 | tf_op jit(solution)/shard_map/ppermute | solution.py:214
  243.8 0.0 collective-permute-done.10.t_sib_ref
  243.8 0.0 copy-done.8
  243.8 0.6 copy-done.14
  244.4 0.0 copy-done.12
  244.4 11.6 %total.1.k_own_ref = f32[160,512]{1,0:T(8,128)} custom-call(f32[128,128]{1,0:T(8,128)} %copy-done.10, f32[128,128]{1,0:T(8,128)} %copy-done.14, f32[160,128]{1,0:T(8,128)} %copy-done.8, f32[160,128]{1,0:T(8,128)} %copy-done.12, f32[544,128]{1,0:T(8,128)} %get-tuple-element.24.c0_ref, f32[416,128]{1,0:T(8,128)} %get-tuple-element.25.c1_ref, ...), custom_call_target="tpu_custom_call" | custom-call | tf_op jit(solution)/shard_map/total/pallas_call | solution.py:201
  256.1 6.2 %collective-permute-start.11 = (f32[160,512]{1,0:T(8,128)}, f32[160,512]{1,0:T(8,128)S(1)}, u32[]{:S(2)}, u32[]{:S(2)}) collective-permute-start(f32[160,512]{1,0:T(8,128)} %total.1.k_own_ref), channel_id=1, source_target_pairs={{0,8},{8,0},{1,9},{9,1},{2,10},{10,2},{3,11},{11,3},{4,12},{12,4},... | collective-permute-start | bytes 983048 | tf_op jit(solution)/shard_map/ppermute | solution.py:214
  262.3 1.4 collective-permute-done.11.k_sib_ref
  263.7 0.0 all-to-all-done.1.w_ref
  263.7 0.7 copy-done.7
  264.4 0.7 copy-done
  265.2 5.8 %final.1 = f32[1024,320]{1,0:T(8,128)} custom-call(s32[1]{0:T(128)} %bitcast.core_ref, f32[1024,384]{1,0:T(8,128)} %x_ref.3, f32[8,64,1024]{2,1,0:T(8,128)} %copy-done, f32[160,512]{1,0:T(8,128)} %total.1.k_own_ref, f32[160,512]{1,0:T(8,128)} %copy-done.7), custom_call_target="tpu_custom_call" | custom-call | tf_op jit(solution)/shard_map/final/pallas_call | solution.py:201
  271.0 2.9 %copy.5 = f32[1024,320]{0,1:T(8,128)} copy(f32[1024,320]{1,0:T(8,128)} %final.1) | data formatting | bytes 2621440 | tf_op jit(solution)/shard_map/final/pallas_call | solution.py:201
  (26 shorter events, 0.2 us)
Async XLA Ops:
  7.4 9.9 %collective-permute-start = (f32[64,512]{1,0:T(8,128)}, f32[64,512]{1,0:T(8,128)S(1)}, u32[]{:S(2)}, u32[]{:S(2)}) collective-permute-start(f32[64,512]{1,0:T(8,128)} %get-tuple-element.16), channel_id=1, source_target_pairs={{0,8},{8,0},{1,9},{9,1},{2,10},{10,2},{3,11},{11,3},{4,12},{12,4},... | collective-permute-start | bytes 393224 | tf_op jit(solution)/shard_map/ppermute | solution.py:214
  18.2 6.6 %collective-permute-start.1 = (f32[64,512]{1,0:T(8,128)S(1)}, f32[64,512]{1,0:T(8,128)S(1)}, u32[]{:S(2)}, u32[]{:S(2)}) collective-permute-start(f32[64,512]{1,0:T(8,128)S(1)} %add.18), channel_id=1, source_target_pairs={{0,16},{16,0},{1,17},{17,1},{2,18},{18,2},{3,19},{19,3},{4,20},{20... | collective-permute-start | bytes 393224 | tf_op jit(solution)/shard_map/ppermute | solution.py:214
  25.7 20.0 %all-to-all-start = ((f32[16,32,256]{2,1,0:T(8,128)}), f32[16,32,256]{2,1,0:T(8,128)S(1)}, u32[]{:S(2)}, u32[]{:S(2)}) async-start(f32[16,32,256]{2,1,0:T(8,128)} %broadcast_in_dim.12), calls=%async_computation | async-start | bytes 1048576 | tf_op jit(solution)/shard_map/all_to_all | solution.py:219
  45.7 1.4 copy-start.2
  47.1 44.7 %all-to-all-start.2 = ((f32[16,32,768]{2,1,0:T(8,128)}), f32[16,32,768]{2,1,0:T(8,128)S(1)}, u32[]{:S(2)}, u32[]{:S(2)}) async-start(f32[16,32,768]{2,1,0:T(8,128)} %broadcast_in_dim.28), calls=%async_computation.2 | async-start | bytes 3145728 | tf_op jit(solution)/shard_map/all_to_all | solution.py:219
  91.7 1.8 copy-start.1
  93.5 8.7 %copy-start.5 = (f32[320,512]{1,0:T(8,128)S(1)}, f32[320,512]{1,0:T(8,128)}, u32[]{:S(2)}) copy-start(f32[320,512]{1,0:T(8,128)} %get-tuple-element.20) | copy-start | bytes 1966084
  93.6 170.2 %all-to-all-start.1 = ((f32[8,64,1024]{2,1,0:T(8,128)}), f32[8,64,1024]{2,1,0:T(8,128)S(1)}, u32[]{:S(2)}, u32[]{:S(2)}) async-start(f32[8,64,1024]{2,1,0:T(8,128)} %broadcast_in_dim.13), calls=%async_computation.1 | async-start | bytes 4194304 | tf_op jit(solution)/shard_map/all_to_all | solution.py:219
  102.3 4.8 %collective-permute-start.3 = (f32[160,512]{1,0:T(8,128)S(1)}, f32[160,512]{1,0:T(8,128)S(1)}, u32[]{:S(2)}, u32[]{:S(2)}) collective-permute-start(f32[160,512]{1,0:T(8,128)S(1)} %constant_dynamic-slice_fusion), channel_id=1, source_target_pairs={{0,8},{8,0},{1,9},{9,1},{2,10},{10,2},{3,11},{11,3},{4,12},{12,4},... | collective-permute-start | bytes 983048 | tf_op jit(solution)/shard_map/ppermute | solution.py:214
  107.1 11.8 %collective-permute-start.4 = (f32[160,512]{1,0:T(8,128)S(1)}, f32[160,512]{1,0:T(8,128)S(1)}, u32[]{:S(2)}, u32[]{:S(2)}) collective-permute-start(f32[160,512]{1,0:T(8,128)S(1)} %dynamic-slice_add_fusion), channel_id=1, source_target_pairs={{0,16},{16,0},{1,17},{17,1},{2,18},{18,2},{3,19},{19,3},{4,20},{20... | collective-permute-start | bytes 983048 | tf_op jit(solution)/shard_map/ppermute | solution.py:214
  119.0 19.9 %copy-start.3 = (f32[160,512]{1,0:T(8,128)}, f32[160,512]{1,0:T(8,128)S(1)}, u32[]{:S(2)}) copy-start(f32[160,512]{1,0:T(8,128)S(1)} %add.23.t_own_ref) | copy-start | bytes 983044
  119.0 33.5 %copy-start.13 = (f32[128,128]{1,0:T(8,128)S(1)}, f32[128,128]{1,0:T(8,128)}, u32[]{:S(2)}) copy-start(f32[128,128]{1,0:T(8,128)} %get-tuple-element.19.own_ref) | copy-start | bytes 196612
  119.0 19.9 %collective-permute-start.5 = (f32[160,512]{1,0:T(8,128)S(1)}, f32[160,512]{1,0:T(8,128)S(1)}, u32[]{:S(2)}, u32[]{:S(2)}) collective-permute-start(f32[160,512]{1,0:T(8,128)S(1)} %add.23.t_own_ref), channel_id=1, source_target_pairs={{0,32},{32,0},{1,33},{33,1},{2,34},{34,2},{3,35},{35,3},{4,36},{36... | collective-permute-start | bytes 983048 | tf_op jit(solution)/shard_map/ppermute | solution.py:214
  138.8 0.7 copy-start.9
  143.8 57.1 %collective-permute-start.6 = (f32[544,384]{1,0:T(8,128)}, f32[544,384]{1,0:T(8,128)S(1)}, u32[]{:S(2)}, u32[]{:S(2)}) collective-permute-start(f32[544,384]{1,0:T(8,128)} %get-tuple-element.21.own_ref), channel_id=1, source_target_pairs={{0,64},{64,0},{1,65},{65,1},{2,66},{66,2},{3,67},{67,3},{4,68},{68... | collective-permute-start | bytes 2506760 | tf_op jit(solution)/shard_map/ppermute | solution.py:214
  152.5 38.9 %collective-permute-start.2 = (f32[128,128]{1,0:T(8,128)S(1)}, f32[128,128]{1,0:T(8,128)S(1)}, u32[]{:S(2)}, u32[]{:S(2)}) collective-permute-start(f32[128,128]{1,0:T(8,128)S(1)} %copy-done.13), channel_id=1, source_target_pairs={{0,64},{64,0},{1,65},{65,1},{2,66},{66,2},{3,67},{67,3},{4,68},{68... | collective-permute-start | bytes 196616 | tf_op jit(solution)/shard_map/ppermute | solution.py:214
  191.4 0.6 copy-start.15
  200.9 0.9 copy-start.4
  205.2 22.4 %collective-permute-start.8 = (f32[416,256]{1,0:T(8,128)}, f32[416,256]{1,0:T(8,128)S(1)}, u32[]{:S(2)}, u32[]{:S(2)}) collective-permute-start(f32[416,256]{1,0:T(8,128)} %get-tuple-element.22.own_ref), channel_id=1, source_target_pairs={{0,128},{128,0},{1,129},{129,1},{2,130},{130,2},{3,131},{131,3},{4... | collective-permute-start | bytes 1277960 | tf_op jit(solution)/shard_map/ppermute | solution.py:214
  209.1 8.9 %copy-start.11 = (f32[128,128]{1,0:T(8,128)}, f32[128,128]{1,0:T(8,128)S(1)}, u32[]{:S(2)}) copy-start(f32[128,128]{1,0:T(8,128)S(1)} %slice.25.own_ref) | copy-start | bytes 196612
  209.1 8.9 %collective-permute-start.7 = (f32[128,128]{1,0:T(8,128)S(1)}, f32[128,128]{1,0:T(8,128)S(1)}, u32[]{:S(2)}, u32[]{:S(2)}) collective-permute-start(f32[128,128]{1,0:T(8,128)S(1)} %slice.25.own_ref), channel_id=1, source_target_pairs={{0,128},{128,0},{1,129},{129,1},{2,130},{130,2},{3,131},{131,3},{4... | collective-permute-start | bytes 196616 | tf_op jit(solution)/shard_map/ppermute | solution.py:214
  218.0 0.6 copy-start.16
  227.5 0.8 copy-start.6
  231.8 12.0 %copy-start.8 = (f32[160,128]{1,0:T(8,128)}, f32[160,128]{1,0:T(8,128)S(1)}, u32[]{:S(2)}) copy-start(f32[160,128]{1,0:T(8,128)S(1)} %slice.27.t_own_ref) | copy-start | bytes 245764
  231.8 12.0 %collective-permute-start.10 = (f32[160,128]{1,0:T(8,128)S(1)}, f32[160,128]{1,0:T(8,128)S(1)}, u32[]{:S(2)}, u32[]{:S(2)}) collective-permute-start(f32[160,128]{1,0:T(8,128)S(1)} %slice.27.t_own_ref), channel_id=1, source_target_pairs={{0,256},{256,0},{1,257},{257,1},{2,258},{258,2},{3,259},{259,3},{4... | collective-permute-start | bytes 245768 | tf_op jit(solution)/shard_map/ppermute | solution.py:214
  237.3 6.5 %copy-start.10 = (f32[128,128]{1,0:T(8,128)}, f32[128,128]{1,0:T(8,128)S(1)}, u32[]{:S(2)}) copy-start(f32[128,128]{1,0:T(8,128)S(1)} %slice.26.a_own_ref) | copy-start | bytes 196612
  237.3 6.5 %collective-permute-start.9 = (f32[128,128]{1,0:T(8,128)S(1)}, f32[128,128]{1,0:T(8,128)S(1)}, u32[]{:S(2)}, u32[]{:S(2)}) collective-permute-start(f32[128,128]{1,0:T(8,128)S(1)} %slice.26.a_own_ref), channel_id=1, source_target_pairs={{0,256},{256,0},{1,257},{257,1},{2,258},{258,2},{3,259},{259,3},{4... | collective-permute-start | bytes 196616 | tf_op jit(solution)/shard_map/ppermute | solution.py:214
  243.8 0.6 copy-start.14
  243.8 0.6 copy-start.12
  256.1 7.7 %collective-permute-start.11 = (f32[160,512]{1,0:T(8,128)}, f32[160,512]{1,0:T(8,128)S(1)}, u32[]{:S(2)}, u32[]{:S(2)}) collective-permute-start(f32[160,512]{1,0:T(8,128)} %total.1.k_own_ref), channel_id=1, source_target_pairs={{0,8},{8,0},{1,9},{9,1},{2,10},{10,2},{3,11},{11,3},{4,12},{12,4},... | collective-permute-start | bytes 983048 | tf_op jit(solution)/shard_map/ppermute | solution.py:214
  263.7 0.7 copy-start.7
  263.7 1.4 copy-start

commit v2 on v1

v2 whole, which is shorter than its diff:
```python
import functools
import math

import jax
import jax.numpy as jnp
from jax import lax
from jax.experimental import pallas as pl
from jax.experimental.pallas import tpu as pltpu
from jax.sharding import Mesh, PartitionSpec as P


R = 128
LEVELS = 4
WB = 16
GROUPS = 8
ROW_AXES = ("x2", "x1", "z4", "z2", "z1", "core")
HIGH = lax.Precision.HIGHEST
F32 = jnp.float32
BF16 = jnp.bfloat16


def halves(x):
    hi = x.astype(BF16)
    return hi, (x - hi.astype(F32)).astype(BF16)


def mm(a, b):
    dot = functools.partial(jnp.dot, preferred_element_type=F32)
    return dot(a[0], b[0]) + (dot(a[0], b[1]) + dot(a[1], b[0]))


def exact(a, b, dims):
    return lax.dot_general(a, b, ((dims[0], dims[1]), ((), ())), precision=HIGH, preferred_element_type=F32)


def spd_inverse(g):
    lane = lax.broadcasted_iota(jnp.int32, (8, R), 1)
    sub = lax.broadcasted_iota(jnp.int32, (8, R), 0)
    n = R // 8
    tiles = [g[8 * i : 8 * i + 8, :] for i in range(n)]
    full = lambda v: jnp.broadcast_to(v, (8, R))
    for k in range(0, R, 4):
        p, s = k // 8, k % 8
        cols = [[full(tiles[i][:, k + j : k + j + 1]) for i in range(n)] for j in range(4)]
        panel = (lane >= k) & (lane < k + 4)
        rows = [
            jnp.where(lane == k + j, 1.0, jnp.where(panel, 0.0, full(tiles[p][s + j : s + j + 1, :])))
            for j in range(4)
        ]
        d = [[full(cols[j][p][s + i : s + i + 1, :]) for j in range(4)] for i in range(4)]
        r = 1.0 / (d[0][0] * d[1][1] - d[0][1] * d[1][0])
        p00, p01, p10, p11 = d[1][1] * r, -d[0][1] * r, -d[1][0] * r, d[0][0] * r
        e = [
            [p00 * d[0][2] + p01 * d[1][2], p00 * d[0][3] + p01 * d[1][3]],
            [p10 * d[0][2] + p11 * d[1][2], p10 * d[0][3] + p11 * d[1][3]],
        ]
        c = [
            [d[2 + i][2 + j] - (d[2 + i][0] * e[0][j] + d[2 + i][1] * e[1][j]) for j in range(2)]
            for i in range(2)
        ]
        q = 1.0 / (c[0][0] * c[1][1] - c[0][1] * c[1][0])
        t0 = p00 * rows[0] + p01 * rows[1]
        t1 = p10 * rows[0] + p11 * rows[1]
        u0 = rows[2] - (d[2][0] * t0 + d[2][1] * t1)
        u1 = rows[3] - (d[3][0] * t0 + d[3][1] * t1)
        v0 = (c[1][1] * u0 - c[0][1] * u1) * q
        v1 = (c[0][0] * u1 - c[1][0] * u0) * q
        new = [t0 - (e[0][0] * v0 + e[0][1] * v1), t1 - (e[1][0] * v0 + e[1][1] * v1), v0, v1]
        for i in range(n):
            a = jnp.where(panel, 0.0, tiles[i])
            for j in range(4):
                a = a - cols[j][i] * new[j]
            if i == p:
                for j in range(4):
                    a = jnp.where(sub == s + j, new[j], a)
            tiles[i] = a
    return jnp.concatenate(tiles, axis=0)


def pair_inverse(own, sib):
    i = lax.broadcasted_iota(jnp.int32, (R, R), 0)
    j = lax.broadcasted_iota(jnp.int32, (R, R), 1)
    m = jnp.where(i == j, 1.0, 0.0) - exact(own, sib, ((1,), (0,)))
    return exact(spd_inverse(exact(m, m, ((0,), (0,)))), m, ((1,), (1,)))


def coefficients(p_own, p_sib, a_own, a_sib, inv):
    c_own = mm(halves(p_sib - mm(halves(p_own), a_sib)), inv)
    c_own_h = halves(c_own)
    c_sib_h = halves(p_own - mm(c_own_h, a_own))
    return c_own, c_own_h, c_sib_h


def project_kernel(core_ref, order_ref, x_ref, v_ref, scale, xt_ref, w0_ref, keep_ref, give_ref):
    rows, width = x_ref.shape
    tgt = width - LEVELS * WB
    half = tgt // 2
    core = core_ref[0]
    xt = x_ref[...].T
    xt_ref[...] = xt
    hi, lo = halves(xt)
    at = lax.broadcasted_iota(jnp.int32, (rows, rows), 0)
    onehot = jnp.where(at == order_ref[...], 1.0, 0.0).astype(BF16)
    hi = jnp.dot(hi, onehot, preferred_element_type=F32).astype(BF16)
    lo = jnp.dot(lo, onehot, preferred_element_type=F32).astype(BF16)
    later = slice(tgt, width - WB)
    for level in range(LEVELS):
        lanes = slice(R * level, R * level + R)
        h = mm((hi, lo), halves(v_ref[level])) * scale[level]
        keep_ref[:half, lanes] = jnp.where(core == 0, h[:half], h[half:tgt])
        give_ref[:half, lanes] = jnp.where(core == 0, h[half:tgt], h[:half])
        keep_ref[half:, lanes] = h[later]
        give_ref[half:, lanes] = h[later]
        w0_ref[:, :, lanes] = jnp.broadcast_to(h[width - WB :][None], (w0_ref.shape[0], WB, R))


def leaf_sum_kernel(parts_ref, out_ref):
    total = (parts_ref[0] + parts_ref[1]) + (parts_ref[2] + parts_ref[3])
    out_ref[...] = jnp.broadcast_to(total[None], out_ref.shape)


def block(ref, side, rows, lanes):
    part = ref[side, :, rows, lanes]
    return part.reshape(GROUPS * WB, part.shape[-1])


def inverse_kernel(side_ref, g_ref, inv_ref):
    own = side_ref[0]
    rows = g_ref.shape[2]
    last = slice(rows - WB, rows)
    inv_ref[...] = pair_inverse(block(g_ref, own, last, slice(0, R)), block(g_ref, 1 - own, last, slice(0, R)))


def advance(top_own, top_sib, low_own, low_sib, inv):
    a_own, a_sib = halves(top_own[:, :R]), halves(top_sib[:, :R])
    c, c_own, c_sib = coefficients(low_own[:, :R], low_sib[:, :R], a_own, a_sib, halves(inv))
    return c, (low_own[:, R:] + low_sib[:, R:]) - (
        mm(c_own, halves(top_own[:, R:])) + mm(c_sib, halves(top_sib[:, R:]))
    )


def update0_kernel(side_ref, inv_ref, g_ref, q_own_ref, q_sib_ref, q_ref, c_ref, send_ref):
    own, sib = side_ref[0], 1 - side_ref[0]
    every, whole = slice(0, WB), slice(0, LEVELS * R)
    c, q = advance(
        block(g_ref, own, every, whole), block(g_ref, sib, every, whole), q_own_ref[...], q_sib_ref[...], inv_ref[...]
    )
    left = q_ref.shape[0]
    q_ref[...] = q[:left]
    c_ref[...] = c[:left]
    send = jnp.concatenate([q[left:], c[left:]], axis=1)
    send_ref[...] = jnp.broadcast_to(send[None], send_ref.shape)


def update1_kernel(side_ref, inv_ref, g_ref, q_own_ref, q_sib_ref, q_ref, c_ref):
    own, sib = side_ref[0], 1 - side_ref[0]
    lanes = slice(0, q_own_ref.shape[1])
    at = lambda side, m: block(g_ref, side, slice((3 - m) * WB, (4 - m) * WB), lanes)
    low_own = jnp.concatenate([at(own, 2), at(own, 3), q_own_ref[...]], axis=0)
    low_sib = jnp.concatenate([at(sib, 2), at(sib, 3), q_sib_ref[...]], axis=0)
    c_ref[...], q_ref[...] = advance(at(own, 1), at(sib, 1), low_own, low_sib, inv_ref[...])


def level2_kernel(own_ref, sib_ref, q_ref, c_ref):
    own, sib = own_ref[...], sib_ref[...]
    inv = pair_inverse(own[:R, :R], sib[:R, :R])
    c_ref[...], q_ref[...] = advance(own[:R], sib[:R], own[R:], sib[R:], inv)


def total_kernel(side_ref, own_ref, sib_ref, c0_ref, c1_ref, c2_ref, g_ref, k_ref):
    a_own, a_sib = own_ref[:R], sib_ref[:R]
    inv = pair_inverse(a_own, a_sib)
    k3, k3h, _ = coefficients(own_ref[R:], sib_ref[R:], halves(a_own), halves(a_sib), halves(inv))
    w0 = lambda m: halves(block(g_ref, side_ref[0], slice((3 - m) * WB, (4 - m) * WB), slice(3 * R, 4 * R)))
    k2 = c2_ref[R:] - mm(k3h, halves(c2_ref[:R]))
    k2h = halves(k2)
    k1 = c1_ref[2 * R :] - (mm(k2h, halves(c1_ref[:R])) + mm(k3h, halves(c1_ref[R : 2 * R])))
    k1h = halves(k1)
    k0 = c0_ref[...] - (mm(k1h, w0(1)) + mm(k2h, w0(2)) + mm(k3h, w0(3)))
    for level, k in enumerate((k0, k1, k2, k3)):
        k_ref[:, R * level : R * level + R] = k


def final_kernel(core_ref, xt_ref, w_ref, k_own_ref, k_sib_ref, out_ref):
    tgt, rows = out_ref.shape
    core = core_ref[0]
    own, sib = k_own_ref[...], k_sib_ref[...]
    k = halves(jnp.concatenate([jnp.where(core == 0, own, sib), jnp.where(core == 0, sib, own)], axis=0))
    at = [(LEVELS - 1 - level) * WB for level in range(LEVELS)]
    w = halves(jnp.concatenate([w_ref[:, a : a + WB, :].reshape(GROUPS * WB, rows) for a in at], axis=0))
    out_ref[...] = xt_ref[:tgt] - mm(k, w)


def call(kernel, outs, scalars=0):
    shapes = [jax.ShapeDtypeStruct(s, F32) for s in outs]
    single = len(shapes) == 1
    vmem, smem = pl.BlockSpec(memory_space=pltpu.VMEM), pl.BlockSpec(memory_space=pltpu.SMEM)

    def run(*args):
        return pl.pallas_call(
            kernel,
            out_shape=shapes[0] if single else shapes,
            in_specs=[smem] * scalars + [vmem] * (len(args) - scalars),
            out_specs=vmem if single else [vmem] * len(shapes),
            compiler_params=pltpu.CompilerParams(vmem_limit_bytes=56 * 2**20),
        )(*args)

    return run


def swap(v, axis):
    return lax.ppermute(v, axis, [(0, 1), (1, 0)])


def mirror(v, axes):
    n = lax.axis_size(axes)
    return lax.ppermute(v, axes, [(i, n - 1 - i) for i in range(n)])


def exchange(v, axes):
    return lax.all_to_all(v, axes, 0, 0, tiled=True).reshape(2, GROUPS, *v.shape[1:])


def mirror_exchange(v, axes):
    n = lax.axis_size(axes)
    pairs = [[p * GROUPS + y for p in (a, n - 1 - a) for y in range(GROUPS)] for a in range(n // 2)]
    out = lax.all_to_all(v, (*axes, "cols"), 0, 0, tiled=True, axis_index_groups=pairs)
    return out.reshape(2, GROUPS, *v.shape[1:])


Z, X = ("z4", "z2", "z1"), ("x2", "x1")


def sweep(columns, row_bases, order):
    rows, width = columns.shape
    tgt = width - LEVELS * WB
    half = tgt // 2
    wide = LEVELS * R
    scale = [0.55 / math.sqrt(R * rows * (4 << level)) for level in range(LEVELS)]
    index = lambda axis: lax.axis_index(axis).astype(jnp.int32)[None]
    core = index("core")
    sides = [index(axis) for axis in ("z2", "z4")]

    def project(core_ref, order_ref, x_ref, v_ref, *outs):
        project_kernel(core_ref, order_ref, x_ref, v_ref, scale, *outs)

    early = half + (LEVELS - 1) * WB
    xt, w0, keep, give = call(
        project, [(width, rows), (4, WB, wide), (early, wide), (early, wide)], 1
    )(core, order, columns, row_bases)

    q = keep + swap(give, "core")
    w0 = lax.all_to_all(lax.optimization_barrier((w0, q))[0], ("z1", "core"), 0, 0, tiled=True)
    send = call(leaf_sum_kernel, [(2 * GROUPS, WB, wide)])(w0)
    g = exchange(send, ("z2", "cols"))
    q = q + swap(q, "z1")
    q_sib = swap(q, "z2")
    basis = lax.all_to_all(
        jnp.broadcast_to(xt[None, tgt:], (GROUPS, LEVELS * WB, rows)), "cols", 0, 0, tiled=True
    )

    inv = call(inverse_kernel, [(R, R)], 1)(sides[0], g)
    q, c0, send = call(
        update0_kernel, [(half, 3 * R), (half, R), (2 * GROUPS, (LEVELS - 1) * WB, wide)], 1
    )(sides[0], inv, g, q, q_sib)
    g = mirror_exchange(send, Z)
    q_sib = mirror(q, Z)

    inv = call(inverse_kernel, [(R, R)], 1)(sides[1], g)
    q, c1 = call(update1_kernel, [(2 * R + half, 2 * R), (2 * R + half, R)], 1)(sides[1], inv, g, q, q_sib)
    q_sib = swap(q, "x1")
    q, c2 = call(level2_kernel, [(R + half, R), (R + half, R)])(q, q_sib)
    q_sib = mirror(q, X)
    k = call(total_kernel, [(half, wide)], 1)(sides[1], q, q_sib, c0, c1, c2, g)
    k_sib = swap(k, "core")
    return call(final_kernel, [(tgt, rows)], 1)(core, xt, basis, k, k_sib).T


def solution(mesh):
    fine = Mesh(mesh.devices.reshape(2, 2, 2, 2, 2, 2, GROUPS), (*ROW_AXES, "cols"))
    placed = (P(ROW_AXES, "cols"), P(None, ROW_AXES, None), P(ROW_AXES, None))
    return jax.shard_map(sweep, mesh=fine, in_specs=placed, out_specs=P(ROW_AXES, "cols"), check_vma=False)
```

time: 275 us -> 215 us (0.78)
  waiting for transfers between devices: 118 us -> 81 us
  starting transfers between devices: 74.8 us -> 54.6 us
  local copies, waits for them, and re-layouts: 16.8 us -> 7.15 us
  blocking collectives: 0 us -> 7.95 us
    ppermute x12 -> x5, waiting for transfers between devices: 78.1 us -> 37.6 us  [swap(): return lax.ppermute(v, axis, [(0, 1), (1, 0)])]
    ppermute x12 -> x5, starting transfers between devices: 53.1 us -> 22.3 us  [swap(): return lax.ppermute(v, axis, [(0, 1), (1, 0)])]
    ppermute x0 -> x2, starting transfers between devices: none -> 9.41 us  [mirror(): return lax.ppermute(v, axes, [(i, n - 1 - i) for i in range(n)])]
    all_to_all x0 -> x1, blocking collectives: none -> 7.95 us  [sweep(): lax.all_to_all(lax.optimization_barrier((w0, q))[0], ('z1', 'core'), 0, 0...]
    ppermute x0 -> x2, waiting for transfers between devices: none -> 3.49 us  [mirror(): return lax.ppermute(v, axes, [(i, n - 1 - i) for i in range(n)])]
    pallas_call x1 -> x0, local copies, waits for them, and re-layouts: 2.92 us -> none  [run(): pl.pallas_call(kernel, out_shape=shapes[0] if single else shapes, in_spec...]
    slice x6 -> x1, local copies, waits for them, and re-layouts: 3.85 us -> 0.97 us  [sweep(): xt[None, tgt:]]
    unnamed x34 -> x18, local copies, waits for them, and re-layouts: 5.83 us -> 4.46 us
  transfers between devices with their start and end apart: 15 -> 10, of which waited for: 11 -> 8; matrix products, arithmetic and copies ran while one was open for 2% -> 0% of each run, Pallas kernels for 18% -> 21%
where the time goes in v2:
time: 215 us
  waiting for transfers between devices  81 us (38%)
  Pallas kernels  62.6 us (29%)
  starting transfers between devices  54.6 us (25%)
  blocking collectives  7.95 us (4%)
  local copies, waits for them, and re-layouts  7.15 us (3%)
    pallas_call x9, Pallas kernels, run(): pl.pallas_call(kernel, out_shape=shapes[0] if single else shapes, in_spec...  62.6 us
    all_to_all x1, waiting for transfers between devices, mirror_exchange(): lax.all_to_all(v, (*axes, 'cols'), 0, 0, tiled=True, axis_index_groups=pa...  39.8 us
    ppermute x5, waiting for transfers between devices, swap(): return lax.ppermute(v, axis, [(0, 1), (1, 0)])  37.6 us
    ppermute x5, starting transfers between devices, swap(): return lax.ppermute(v, axis, [(0, 1), (1, 0)])  22.3 us
    all_to_all x1, starting transfers between devices, mirror_exchange(): lax.all_to_all(v, (*axes, 'cols'), 0, 0, tiled=True, axis_index_groups=pa...  11.7 us
    ppermute x2, starting transfers between devices, mirror(): return lax.ppermute(v, axes, [(i, n - 1 - i) for i in range(n)])  9.41 us
    all_to_all x1, blocking collectives, sweep(): lax.all_to_all(lax.optimization_barrier((w0, q))[0], ('z1', 'core'), 0, 0...  7.95 us
    all_to_all x1, starting transfers between devices, sweep(): lax.all_to_all(jnp.broadcast_to(xt[None, tgt:], (GROUPS, LEVELS * WB, row...  5.62 us
  transfers between devices with their start and end apart: 10, of which 8 were waited for; matrix products, arithmetic and copies ran while one was open for 0% of the time, Pallas kernels for 21%

profile of v2, /device:TPU:1, one launch (start us, length us, event | category | flops | bytes accessed | tf_op | source)
XLA Modules:
  0.0 214.5 jit_solution(7526558180712144969)
XLA Ops:
  0.0 7.5 %shard_map.37 = (f32[384,1024]{1,0:T(8,128)}, f32[4,16,512]{2,1,0:T(8,128)}, f32[208,512]{1,0:T(8,128)}, f32[208,512]{1,0:T(8,128)}) custom-call(s32[1]{0:T(128)} %bitcast.core_ref, s32[1,1024]{1,0:T(1,128)} %order_ref.1, f32[1024,384]{1,0:T(8,128)} %x_ref.1, f32[4,1024,128]{2,1,0:T(8,128)} %v_ref.1), custom_call_target="tpu_custom_call" | custom-call | tf_op jit(solution)/shard_map/pallas_call | solution.py:200
  7.5 8.7 %collective-permute-start = (f32[208,512]{1,0:T(8,128)}, f32[208,512]{1,0:T(8,128)S(1)}, u32[]{:S(2)}, u32[]{:S(2)}) collective-permute-start(f32[208,512]{1,0:T(8,128)} %get-tuple-element.20), channel_id=1, source_target_pairs={{0,8},{8,0},{1,9},{9,1},{2,10},{10,2},{3,11},{11,3},{4,12},{12,4},... | collective-permute-start | bytes 1277960 | tf_op jit(solution)/shard_map/ppermute | solution.py:212
  16.2 1.6 collective-permute-done
  17.8 1.1 add.6
  18.9 7.9 %all_to_all.20.parts_ref = f32[4,16,512]{2,1,0:T(8,128)} all-to-all(f32[4,16,512]{2,1,0:T(8,128)} %get-tuple-element.21), channel_id=1, replica_groups=mesh['x2'=2,'x1'=2,'z4'=2,'z2'=2,'z1'=2,'core'=2,'cols'=8] {'z1','core'}, dimensions={0} | all-to-all | bytes 262144 | tf_op jit(solution)/shard_map/all_to_all | solution.py:253
  26.8 1.8 shard_map.38
  28.6 5.6 %all-to-all-start.2 = ((f32[16,16,512]{2,1,0:T(8,128)}), f32[16,16,512]{2,1,0:T(8,128)S(1)}, u32[]{:S(2)}, u32[]{:S(2)}) async-start(f32[16,16,512]{2,1,0:T(8,128)} %shard_map.38), calls=%async_computation.2 | async-start | bytes 1048576 | tf_op jit(solution)/shard_map/all_to_all | solution.py:221
  34.2 2.1 collective-permute-start.1
  36.3 15.6 %collective-permute-done.1 = f32[208,512]{1,0:T(8,128)S(1)} collective-permute-done((f32[208,512]{1,0:T(8,128)S(1)}, f32[208,512]{1,0:T(8,128)S(1)}, u32[]{:S(2)}, u32[]{:S(2)}) %collective-permute-start.1) | collective-permute-done | bytes 426016 | tf_op jit(solution)/shard_map/ppermute | solution.py:212
  51.8 0.1 add.7.q_own_ref
  51.9 0.0 copy-start.2
  51.9 2.8 %collective-permute-start.2 = (f32[208,512]{1,0:T(8,128)S(1)}, f32[208,512]{1,0:T(8,128)S(1)}, u32[]{:S(2)}, u32[]{:S(2)}) collective-permute-start(f32[208,512]{1,0:T(8,128)S(1)} %add.7.q_own_ref), channel_id=1, source_target_pairs={{0,32},{32,0},{1,33},{33,1},{2,34},{34,2},{3,35},{35,3},{4,36},{36... | collective-permute-start | bytes 1277960 | tf_op jit(solution)/shard_map/ppermute | solution.py:212
  54.7 0.0 all-to-all-done.2
  54.7 0.0 copy-start.1
  54.8 0.8 copy-done.1
  55.5 9.1 %shard_map.39.inv_ref = f32[128,128]{1,0:T(8,128)} custom-call(s32[1]{0:T(128)} %bitcast.2.side_ref, f32[2,8,16,512]{3,2,1,0:T(8,128)} %bitcast.9), custom_call_target="tpu_custom_call" | custom-call | tf_op jit(solution)/shard_map/pallas_call | solution.py:200
  64.6 10.8 %collective-permute-done.2.q_sib_ref = f32[208,512]{1,0:T(8,128)S(1)} collective-permute-done((f32[208,512]{1,0:T(8,128)S(1)}, f32[208,512]{1,0:T(8,128)S(1)}, u32[]{:S(2)}, u32[]{:S(2)}) %collective-permute-start.2) | collective-permute-done | bytes 426016 | tf_op jit(solution)/shard_map/ppermute | solution.py:212
  75.3 0.0 copy-done.2
  75.4 0.0 copy-start.4
  75.4 0.8 copy-done.4
  76.1 3.8 %shard_map.40 = (f32[160,384]{1,0:T(8,128)}, f32[160,128]{1,0:T(8,128)}, f32[16,48,512]{2,1,0:T(8,128)}) custom-call(s32[1]{0:T(128)} %bitcast.2.side_ref, f32[128,128]{1,0:T(8,128)} %shard_map.39.inv_ref, f32[2,8,16,512]{3,2,1,0:T(8,128)} %bitcast.10, f32[208,512]{1,0:T(8,128)} %copy-done.2, f32[208,512]{1,0:T(8,128)} %copy-done.4), custom_call_target="tpu_custom_call" | custom-call | tf_op jit(solution)/shard_map/pallas_call | solution.py:200
  79.9 11.7 %all-to-all-start.3 = ((f32[16,48,512]{2,1,0:T(8,128)}), f32[16,48,512]{2,1,0:T(8,128)S(1)}, u32[]{:S(2)}, u32[]{:S(2)}) async-start(f32[16,48,512]{2,1,0:T(8,128)} %get-tuple-element.22), calls=%async_computation.3 | async-start | bytes 3145728 | tf_op jit(solution)/shard_map/all_to_all | solution.py:227
  91.6 1.0 slice.3
  92.6 39.8 %all-to-all-done.3 = f32[16,48,512]{2,1,0:T(8,128)S(1)} async-done(((f32[16,48,512]{2,1,0:T(8,128)}), f32[16,48,512]{2,1,0:T(8,128)S(1)}, u32[]{:S(2)}, u32[]{:S(2)}) %all-to-all-start.3) | async-done | bytes 1572896 | tf_op jit(solution)/shard_map/all_to_all | solution.py:227
  132.4 0.0 copy-start
  132.4 1.7 broadcast_in_dim.16
  134.2 0.0 copy-start.6
  134.2 0.1 copy-done
  134.2 5.6 %all-to-all-start = ((f32[8,64,1024]{2,1,0:T(8,128)}), f32[8,64,1024]{2,1,0:T(8,128)}, u32[]{:S(2)}, u32[]{:S(2)}) async-start(f32[8,64,1024]{2,1,0:T(8,128)} %broadcast_in_dim.16), calls=%async_computation | async-start | bytes 4194304 | tf_op jit(solution)/shard_map/all_to_all | solution.py:258
  139.9 0.0 copy-done.6
  139.9 4.9 %collective-permute-start.3 = (f32[160,384]{1,0:T(8,128)S(1)}, f32[160,384]{1,0:T(8,128)S(1)}, u32[]{:S(2)}, u32[]{:S(2)}) collective-permute-start(f32[160,384]{1,0:T(8,128)S(1)} %copy-done.6), channel_id=1, source_target_pairs={{0,112},{16,96},{32,80},{48,64},{64,48},{80,32},{96,16},{112,0},{1... | collective-permute-start | bytes 737288 | tf_op jit(solution)/shard_map/ppermute | solution.py:217
  144.8 9.4 %shard_map.41.inv_ref = f32[128,128]{1,0:T(8,128)} custom-call(s32[1]{0:T(128)} %bitcast.1.side_ref, f32[2,8,48,512]{3,2,1,0:T(8,128)} %bitcast.6), custom_call_target="tpu_custom_call" | custom-call | tf_op jit(solution)/shard_map/pallas_call | solution.py:200
  154.2 0.3 collective-permute-done.3.q_sib_ref
  154.5 0.0 copy-start.7
  154.5 0.7 copy-done.7
  155.2 3.5 %shard_map.42 = (f32[416,256]{1,0:T(8,128)}, f32[416,128]{1,0:T(8,128)}) custom-call(s32[1]{0:T(128)} %bitcast.1.side_ref, f32[128,128]{1,0:T(8,128)} %shard_map.41.inv_ref, f32[2,8,48,512]{3,2,1,0:T(8,128)} %bitcast.7, f32[160,384]{1,0:T(8,128)} %get-tuple-element.23.q_own_ref, f32[160,384]{1,0:T(8,128)} %copy-done.7), custom_call_target="tpu_custom_call" | custom-call | tf_op jit(solution)/shard_map/pallas_call | solution.py:200
  158.7 3.1 %collective-permute-start.4 = (f32[416,256]{1,0:T(8,128)}, f32[416,256]{1,0:T(8,128)S(1)}, u32[]{:S(2)}, u32[]{:S(2)}) collective-permute-start(f32[416,256]{1,0:T(8,128)} %get-tuple-element.24.own_ref), channel_id=1, source_target_pairs={{0,128},{128,0},{1,129},{129,1},{2,130},{130,2},{3,131},{131,3},{4... | collective-permute-start | bytes 1277960 | tf_op jit(solution)/shard_map/ppermute | solution.py:212
  161.8 8.3 %collective-permute-done.4.sib_ref = f32[416,256]{1,0:T(8,128)S(1)} collective-permute-done((f32[416,256]{1,0:T(8,128)}, f32[416,256]{1,0:T(8,128)S(1)}, u32[]{:S(2)}, u32[]{:S(2)}) %collective-permute-start.4) | collective-permute-done | bytes 426016 | tf_op jit(solution)/shard_map/ppermute | solution.py:212
  170.0 0.0 copy-start.3
  170.0 0.8 copy-done.3
  170.8 11.0 %shard_map.43 = (f32[288,128]{1,0:T(8,128)}, f32[288,128]{1,0:T(8,128)}) custom-call(f32[416,256]{1,0:T(8,128)} %get-tuple-element.24.own_ref, f32[416,256]{1,0:T(8,128)} %copy-done.3), custom_call_target="tpu_custom_call" | custom-call | tf_op jit(solution)/shard_map/pallas_call | solution.py:200
  181.8 4.5 %collective-permute-start.5 = (f32[288,128]{1,0:T(8,128)}, f32[288,128]{1,0:T(8,128)S(1)}, u32[]{:S(2)}, u32[]{:S(2)}) collective-permute-start(f32[288,128]{1,0:T(8,128)} %get-tuple-element.25.own_ref), channel_id=1, source_target_pairs={{0,384},{128,256},{256,128},{384,0},{1,385},{129,257},{257,129},{3... | collective-permute-start | bytes 442376 | tf_op jit(solution)/shard_map/ppermute | solution.py:217
  186.3 3.2 %collective-permute-done.5.sib_ref = f32[288,128]{1,0:T(8,128)S(1)} collective-permute-done((f32[288,128]{1,0:T(8,128)}, f32[288,128]{1,0:T(8,128)S(1)}, u32[]{:S(2)}, u32[]{:S(2)}) %collective-permute-start.5) | collective-permute-done | bytes 147488 | tf_op jit(solution)/shard_map/ppermute | solution.py:217
  189.5 0.0 copy-start.8
  189.5 0.7 copy-done.8
  190.2 12.1 %shard_map.44.k_own_ref = f32[160,512]{1,0:T(8,128)} custom-call(s32[1]{0:T(128)} %bitcast.1.side_ref, f32[288,128]{1,0:T(8,128)} %get-tuple-element.25.own_ref, f32[288,128]{1,0:T(8,128)} %copy-done.8, f32[160,128]{1,0:T(8,128)} %get-tuple-element.26.c0_ref, f32[416,128]{1,0:T(8,128)} %get-tuple-element.27.c1_ref, f32[288,128]{1,0:T(8,128)} %get-tuple-element.28.c2_ref, ...), custom_call_target="tpu_custom_call" | custom-call | tf_op jit(solution)/shard_map/pallas_call | solution.py:200
  202.3 5.6 %collective-permute-start.6 = (f32[160,512]{1,0:T(8,128)}, f32[160,512]{1,0:T(8,128)S(1)}, u32[]{:S(2)}, u32[]{:S(2)}) collective-permute-start(f32[160,512]{1,0:T(8,128)} %shard_map.44.k_own_ref), channel_id=1, source_target_pairs={{0,8},{8,0},{1,9},{9,1},{2,10},{10,2},{3,11},{11,3},{4,12},{12,4},... | collective-permute-start | bytes 983048 | tf_op jit(solution)/shard_map/ppermute | solution.py:212
  207.9 0.0 all-to-all-done.w_ref
  207.9 1.4 collective-permute-done.6.k_sib_ref
  209.4 0.0 copy-start.5
  209.4 0.7 copy-done.5
  210.1 4.4 %shard_map.45 = f32[320,1024]{1,0:T(8,128)} custom-call(s32[1]{0:T(128)} %bitcast.core_ref, f32[384,1024]{1,0:T(8,128)} %get-tuple-element.17.xt_ref, f32[8,64,1024]{2,1,0:T(8,128)} %all-to-all-done.w_ref, f32[160,512]{1,0:T(8,128)} %shard_map.44.k_own_ref, f32[160,512]{1,0:T(8,128)} %copy-done.5), custom_call_target="tpu_custom_call" | custom-call | tf_op jit(solution)/shard_map/pallas_call | solution.py:200
Async XLA Ops:
  7.5 10.3 %collective-permute-start = (f32[208,512]{1,0:T(8,128)}, f32[208,512]{1,0:T(8,128)S(1)}, u32[]{:S(2)}, u32[]{:S(2)}) collective-permute-start(f32[208,512]{1,0:T(8,128)} %get-tuple-element.20), channel_id=1, source_target_pairs={{0,8},{8,0},{1,9},{9,1},{2,10},{10,2},{3,11},{11,3},{4,12},{12,4},... | collective-permute-start | bytes 1277960 | tf_op jit(solution)/shard_map/ppermute | solution.py:212
  28.6 26.1 %all-to-all-start.2 = ((f32[16,16,512]{2,1,0:T(8,128)}), f32[16,16,512]{2,1,0:T(8,128)S(1)}, u32[]{:S(2)}, u32[]{:S(2)}) async-start(f32[16,16,512]{2,1,0:T(8,128)} %shard_map.38), calls=%async_computation.2 | async-start | bytes 1048576 | tf_op jit(solution)/shard_map/all_to_all | solution.py:221
  34.2 17.7 %collective-permute-start.1 = (f32[208,512]{1,0:T(8,128)S(1)}, f32[208,512]{1,0:T(8,128)S(1)}, u32[]{:S(2)}, u32[]{:S(2)}) collective-permute-start(f32[208,512]{1,0:T(8,128)S(1)} %add.6), channel_id=1, source_target_pairs={{0,16},{16,0},{1,17},{17,1},{2,18},{18,2},{3,19},{19,3},{4,20},{20... | collective-permute-start | bytes 1277960 | tf_op jit(solution)/shard_map/ppermute | solution.py:212
  51.9 23.4 %copy-start.2 = (f32[208,512]{1,0:T(8,128)}, f32[208,512]{1,0:T(8,128)S(1)}, u32[]{:S(2)}) copy-start(f32[208,512]{1,0:T(8,128)S(1)} %add.7.q_own_ref) | copy-start | bytes 1277956
  51.9 23.4 %collective-permute-start.2 = (f32[208,512]{1,0:T(8,128)S(1)}, f32[208,512]{1,0:T(8,128)S(1)}, u32[]{:S(2)}, u32[]{:S(2)}) collective-permute-start(f32[208,512]{1,0:T(8,128)S(1)} %add.7.q_own_ref), channel_id=1, source_target_pairs={{0,32},{32,0},{1,33},{33,1},{2,34},{34,2},{3,35},{35,3},{4,36},{36... | collective-permute-start | bytes 1277960 | tf_op jit(solution)/shard_map/ppermute | solution.py:212
  54.7 0.8 copy-start.1
  75.4 0.8 copy-start.4
  79.9 52.5 %all-to-all-start.3 = ((f32[16,48,512]{2,1,0:T(8,128)}), f32[16,48,512]{2,1,0:T(8,128)S(1)}, u32[]{:S(2)}, u32[]{:S(2)}) async-start(f32[16,48,512]{2,1,0:T(8,128)} %get-tuple-element.22), calls=%async_computation.3 | async-start | bytes 3145728 | tf_op jit(solution)/shard_map/all_to_all | solution.py:227
  132.4 1.8 copy-start
  134.2 5.7 %copy-start.6 = (f32[160,384]{1,0:T(8,128)S(1)}, f32[160,384]{1,0:T(8,128)}, u32[]{:S(2)}) copy-start(f32[160,384]{1,0:T(8,128)} %get-tuple-element.23.q_own_ref) | copy-start | bytes 737284
  134.2 73.7 %all-to-all-start = ((f32[8,64,1024]{2,1,0:T(8,128)}), f32[8,64,1024]{2,1,0:T(8,128)}, u32[]{:S(2)}, u32[]{:S(2)}) async-start(f32[8,64,1024]{2,1,0:T(8,128)} %broadcast_in_dim.16), calls=%async_computation | async-start | bytes 4194304 | tf_op jit(solution)/shard_map/all_to_all | solution.py:258
  139.9 14.7 %collective-permute-start.3 = (f32[160,384]{1,0:T(8,128)S(1)}, f32[160,384]{1,0:T(8,128)S(1)}, u32[]{:S(2)}, u32[]{:S(2)}) collective-permute-start(f32[160,384]{1,0:T(8,128)S(1)} %copy-done.6), channel_id=1, source_target_pairs={{0,112},{16,96},{32,80},{48,64},{64,48},{80,32},{96,16},{112,0},{1... | collective-permute-start | bytes 737288 | tf_op jit(solution)/shard_map/ppermute | solution.py:217
  154.5 0.7 copy-start.7
  158.7 11.3 %collective-permute-start.4 = (f32[416,256]{1,0:T(8,128)}, f32[416,256]{1,0:T(8,128)S(1)}, u32[]{:S(2)}, u32[]{:S(2)}) collective-permute-start(f32[416,256]{1,0:T(8,128)} %get-tuple-element.24.own_ref), channel_id=1, source_target_pairs={{0,128},{128,0},{1,129},{129,1},{2,130},{130,2},{3,131},{131,3},{4... | collective-permute-start | bytes 1277960 | tf_op jit(solution)/shard_map/ppermute | solution.py:212
  170.0 0.8 copy-start.3
  181.8 7.7 %collective-permute-start.5 = (f32[288,128]{1,0:T(8,128)}, f32[288,128]{1,0:T(8,128)S(1)}, u32[]{:S(2)}, u32[]{:S(2)}) collective-permute-start(f32[288,128]{1,0:T(8,128)} %get-tuple-element.25.own_ref), channel_id=1, source_target_pairs={{0,384},{128,256},{256,128},{384,0},{1,385},{129,257},{257,129},{3... | collective-permute-start | bytes 442376 | tf_op jit(solution)/shard_map/ppermute | solution.py:217
  189.5 0.7 copy-start.8
  202.3 7.1 %collective-permute-start.6 = (f32[160,512]{1,0:T(8,128)}, f32[160,512]{1,0:T(8,128)S(1)}, u32[]{:S(2)}, u32[]{:S(2)}) collective-permute-start(f32[160,512]{1,0:T(8,128)} %shard_map.44.k_own_ref), channel_id=1, source_target_pairs={{0,8},{8,0},{1,9},{9,1},{2,10},{10,2},{3,11},{11,3},{4,12},{12,4},... | collective-permute-start | bytes 983048 | tf_op jit(solution)/shard_map/ppermute | solution.py:212
  209.4 0.7 copy-start.5

commit v3 on v2

--- a/solution.py
+++ b/solution.py
@@ -13,6 +13,7 @@
 LEVELS = 4
 WB = 16
 GROUPS = 8
+RING = (1, -1, 2, -2, 3, -3, 4)
 ROW_AXES = ("x2", "x1", "z4", "z2", "z1", "core")
 HIGH = lax.Precision.HIGHEST
 F32 = jnp.float32
@@ -124,11 +125,18 @@
     return part.reshape(GROUPS * WB, part.shape[-1])
 
 
+def couple(g_ref, side, lanes):
+    rows = g_ref.shape[2]
+    return block(g_ref, side, slice(rows - WB, rows), lanes)
+
+
 def inverse_kernel(side_ref, g_ref, inv_ref):
     own = side_ref[0]
-    rows = g_ref.shape[2]
-    last = slice(rows - WB, rows)
-    inv_ref[...] = pair_inverse(block(g_ref, own, last, slice(0, R)), block(g_ref, 1 - own, last, slice(0, R)))
+    inv_ref[...] = pair_inverse(couple(g_ref, own, slice(0, R)), couple(g_ref, 1 - own, slice(0, R)))
+
+
+def last_inverse_kernel(own_ref, sib_ref, inv_ref):
+    inv_ref[...] = pair_inverse(own_ref[...], sib_ref[...])
 
 
 def advance(top_own, top_sib, low_own, low_sib, inv):
@@ -139,51 +147,58 @@
     )
 
 
-def update0_kernel(side_ref, inv_ref, g_ref, q_own_ref, q_sib_ref, q_ref, c_ref, send_ref):
-    own, sib = side_ref[0], 1 - side_ref[0]
-    every, whole = slice(0, WB), slice(0, LEVELS * R)
-    c, q = advance(
-        block(g_ref, own, every, whole), block(g_ref, sib, every, whole), q_own_ref[...], q_sib_ref[...], inv_ref[...]
-    )
-    left = q_ref.shape[0]
-    q_ref[...] = q[:left]
-    c_ref[...] = c[:left]
-    send = jnp.concatenate([q[left:], c[left:]], axis=1)
-    send_ref[...] = jnp.broadcast_to(send[None], send_ref.shape)
-
-
-def update1_kernel(side_ref, inv_ref, g_ref, q_own_ref, q_sib_ref, q_ref, c_ref):
-    own, sib = side_ref[0], 1 - side_ref[0]
-    lanes = slice(0, q_own_ref.shape[1])
-    at = lambda side, m: block(g_ref, side, slice((3 - m) * WB, (4 - m) * WB), lanes)
-    low_own = jnp.concatenate([at(own, 2), at(own, 3), q_own_ref[...]], axis=0)
-    low_sib = jnp.concatenate([at(sib, 2), at(sib, 3), q_sib_ref[...]], axis=0)
-    c_ref[...], q_ref[...] = advance(at(own, 1), at(sib, 1), low_own, low_sib, inv_ref[...])
-
-
-def level2_kernel(own_ref, sib_ref, q_ref, c_ref):
-    own, sib = own_ref[...], sib_ref[...]
-    inv = pair_inverse(own[:R, :R], sib[:R, :R])
-    c_ref[...], q_ref[...] = advance(own[:R], sib[:R], own[R:], sib[R:], inv)
-
-
-def total_kernel(side_ref, own_ref, sib_ref, c0_ref, c1_ref, c2_ref, g_ref, k_ref):
-    a_own, a_sib = own_ref[:R], sib_ref[:R]
-    inv = pair_inverse(a_own, a_sib)
-    k3, k3h, _ = coefficients(own_ref[R:], sib_ref[R:], halves(a_own), halves(a_sib), halves(inv))
-    w0 = lambda m: halves(block(g_ref, side_ref[0], slice((3 - m) * WB, (4 - m) * WB), slice(3 * R, 4 * R)))
-    k2 = c2_ref[R:] - mm(k3h, halves(c2_ref[:R]))
+def basis_kernel(side_ref, inv_ref, g_ref, w_own_ref, w_sib_ref, *refs):
+    c_ref, send_ref = refs[-2:]
+    own, whole = side_ref[0], slice(0, g_ref.shape[3])
+    c, w = advance(
+        couple(g_ref, own, whole), couple(g_ref, 1 - own, whole), w_own_ref[...], w_sib_ref[...], inv_ref[...]
+    )
+    c_ref[...] = c
+    left = w.shape[0] - send_ref.shape[1]
+    if left:
+        refs[0][...] = w[:left]
+    send_ref[...] = jnp.broadcast_to(w[left:][None], send_ref.shape)
+
+
+def last_basis_kernel(side_ref, inv_ref, g_ref, a_ref, c_ref):
+    own, whole, first = side_ref[0], slice(0, g_ref.shape[3]), slice(0, WB)
+    c_ref[...], a_ref[...] = advance(
+        couple(g_ref, own, whole),
+        couple(g_ref, 1 - own, whole),
+        block(g_ref, own, first, whole),
+        block(g_ref, 1 - own, first, whole),
+        inv_ref[...],
+    )
+
+
+def targets_kernel(side_ref, inv_ref, g_ref, t_own_ref, t_sib_ref, t_ref, c_ref):
+    own, whole = side_ref[0], slice(0, g_ref.shape[3])
+    c_ref[...], t_ref[...] = advance(
+        couple(g_ref, own, whole), couple(g_ref, 1 - own, whole), t_own_ref[...], t_sib_ref[...], inv_ref[...]
+    )
+
+
+def total_kernel(inv_ref, a_own_ref, a_sib_ref, t_own_ref, t_sib_ref, t0_ref, t1_ref, t2_ref, w2_ref, cw_ref, k_ref):
+    k3, k3h, _ = coefficients(
+        t_own_ref[...], t_sib_ref[...], halves(a_own_ref[...]), halves(a_sib_ref[...]), halves(inv_ref[...])
+    )
+    w = lambda i: halves(cw_ref[:, i * WB : i * WB + WB, :].reshape(GROUPS * WB, R))
+    k2 = t2_ref[...] - mm(k3h, halves(w2_ref[...]))
     k2h = halves(k2)
-    k1 = c1_ref[2 * R :] - (mm(k2h, halves(c1_ref[:R])) + mm(k3h, halves(c1_ref[R : 2 * R])))
+    k1 = t1_ref[...] - (mm(k2h, w(4)) + mm(k3h, w(3)))
     k1h = halves(k1)
-    k0 = c0_ref[...] - (mm(k1h, w0(1)) + mm(k2h, w0(2)) + mm(k3h, w0(3)))
+    k0 = t0_ref[...] - (mm(k1h, w(2)) + mm(k2h, w(1)) + mm(k3h, w(0)))
     for level, k in enumerate((k0, k1, k2, k3)):
         k_ref[:, R * level : R * level + R] = k
 
 
-def final_kernel(core_ref, xt_ref, w_ref, k_own_ref, k_sib_ref, out_ref):
+def final_kernel(core_ref, col_ref, xt_ref, *refs):
+    part_refs, (k_own_ref, k_sib_ref, out_ref, w_ref) = refs[: GROUPS - 1], refs[GROUPS - 1 :]
     tgt, rows = out_ref.shape
-    core = core_ref[0]
+    core, col = core_ref[0], col_ref[0]
+    w_ref[col] = xt_ref[tgt:]
+    for shift, part_ref in zip(RING, part_refs):
+        w_ref[lax.rem(col + (shift + GROUPS), GROUPS)] = part_ref[...]
     own, sib = k_own_ref[...], k_sib_ref[...]
     k = halves(jnp.concatenate([jnp.where(core == 0, own, sib), jnp.where(core == 0, sib, own)], axis=0))
     at = [(LEVELS - 1 - level) * WB for level in range(LEVELS)]
@@ -191,7 +206,7 @@
     out_ref[...] = xt_ref[:tgt] - mm(k, w)
 
 
-def call(kernel, outs, scalars=0):
+def call(kernel, outs, scalars=0, scratch=()):
     shapes = [jax.ShapeDtypeStruct(s, F32) for s in outs]
     single = len(shapes) == 1
     vmem, smem = pl.BlockSpec(memory_space=pltpu.VMEM), pl.BlockSpec(memory_space=pltpu.SMEM)
@@ -202,6 +217,7 @@
             out_shape=shapes[0] if single else shapes,
             in_specs=[smem] * scalars + [vmem] * (len(args) - scalars),
             out_specs=vmem if single else [vmem] * len(shapes),
+            scratch_shapes=[pltpu.VMEM(shape, F32) for shape in scratch],
             compiler_params=pltpu.CompilerParams(vmem_limit_bytes=56 * 2**20),
         )(*args)
 
@@ -239,7 +255,7 @@
     scale = [0.55 / math.sqrt(R * rows * (4 << level)) for level in range(LEVELS)]
     index = lambda axis: lax.axis_index(axis).astype(jnp.int32)[None]
     core = index("core")
-    sides = [index(axis) for axis in ("z2", "z4")]
+    sides = [index(axis) for axis in ("z2", "z4", "x1")]
 
     def project(core_ref, order_ref, x_ref, v_ref, *outs):
         project_kernel(core_ref, order_ref, x_ref, v_ref, scale, *outs)
@@ -251,29 +267,48 @@
 
     q = keep + swap(give, "core")
     w0 = lax.all_to_all(lax.optimization_barrier((w0, q))[0], ("z1", "core"), 0, 0, tiled=True)
+    moved = swap(q, "z1")
+    t, w = q[:half] + moved[:half], q[half:] + moved[half:]
     send = call(leaf_sum_kernel, [(2 * GROUPS, WB, wide)])(w0)
-    g = exchange(send, ("z2", "cols"))
-    q = q + swap(q, "z1")
-    q_sib = swap(q, "z2")
-    basis = lax.all_to_all(
-        jnp.broadcast_to(xt[None, tgt:], (GROUPS, LEVELS * WB, rows)), "cols", 0, 0, tiled=True
-    )
-
-    inv = call(inverse_kernel, [(R, R)], 1)(sides[0], g)
-    q, c0, send = call(
-        update0_kernel, [(half, 3 * R), (half, R), (2 * GROUPS, (LEVELS - 1) * WB, wide)], 1
-    )(sides[0], inv, g, q, q_sib)
-    g = mirror_exchange(send, Z)
-    q_sib = mirror(q, Z)
-
-    inv = call(inverse_kernel, [(R, R)], 1)(sides[1], g)
-    q, c1 = call(update1_kernel, [(2 * R + half, 2 * R), (2 * R + half, R)], 1)(sides[1], inv, g, q, q_sib)
-    q_sib = swap(q, "x1")
-    q, c2 = call(level2_kernel, [(R + half, R), (R + half, R)])(q, q_sib)
-    q_sib = mirror(q, X)
-    k = call(total_kernel, [(half, wide)], 1)(sides[1], q, q_sib, c0, c1, c2, g)
+    g0 = exchange(send, ("z2", "cols"))
+    w_sib = swap(w, "z2")
+    t_sib = swap(t, "z2")
+
+    parts, held = [], {1: xt[tgt:], -1: xt[tgt:]}
+    for shift in RING:
+        way = 1 if shift > 0 else -1
+        held[way] = lax.ppermute(held[way], "cols", [((y + way) % GROUPS, y) for y in range(GROUPS)])
+        parts.append(held[way])
+
+    inv0 = call(inverse_kernel, [(R, R)], 1)(sides[0], g0)
+    w, cw0, send = call(
+        basis_kernel, [(2 * WB, 3 * R), (3 * WB, R), (2 * GROUPS, WB, 3 * R)], 1
+    )(sides[0], inv0, g0, w, w_sib)
+    g1 = mirror_exchange(send, Z)
+    w_sib = mirror(w, Z)
+    t, t0 = call(targets_kernel, [(half, 3 * R), (half, R)], 1)(sides[0], inv0, g0, t, t_sib)
+    t_sib = mirror(t, Z)
+
+    inv1 = call(inverse_kernel, [(R, R)], 1)(sides[1], g1)
+    cw1, send = call(basis_kernel, [(2 * WB, R), (2 * GROUPS, 2 * WB, 2 * R)], 1)(sides[1], inv1, g1, w, w_sib)
+    g2 = exchange(send, ("x1", "cols"))
+    t, t1 = call(targets_kernel, [(half, 2 * R), (half, R)], 1)(sides[1], inv1, g1, t, t_sib)
+    t_sib = swap(t, "x1")
+
+    inv2 = call(inverse_kernel, [(R, R)], 1)(sides[2], g2)
+    a3, cw2 = call(last_basis_kernel, [(R, R), (R, R)], 1)(sides[2], inv2, g2)
+    a3_sib = mirror(a3, X)
+    cw = jnp.concatenate([cw0, cw1], axis=0)
+    cw = lax.all_to_all(jnp.broadcast_to(cw[None], (GROUPS, *cw.shape)), "cols", 0, 0, tiled=True)
+    t, t2 = call(targets_kernel, [(half, R), (half, R)], 1)(sides[2], inv2, g2, t, t_sib)
+    t_sib = mirror(t, X)
+
+    inv3 = call(last_inverse_kernel, [(R, R)])(a3, a3_sib)
+    k = call(total_kernel, [(half, wide)])(inv3, a3, a3_sib, t, t_sib, t0, t1, t2, cw2, cw)
     k_sib = swap(k, "core")
-    return call(final_kernel, [(tgt, rows)], 1)(core, xt, basis, k, k_sib).T
+    return call(final_kernel, [(tgt, rows)], 2, [(GROUPS, LEVELS * WB, rows)])(
+        core, index("cols"), xt, *parts, k, k_sib
+    ).T
 
 
 def solution(mesh):

time: 215 us -> 227 us (1.056); the launches traced: 215 us -> 223 us
  starting transfers between devices: 54.6 us -> 101 us
  waiting for transfers between devices: 81 us -> 35.6 us
  Pallas kernels: 62.6 us -> 68.1 us
    all_to_all x1, waiting for transfers between devices: 39.8 us -> 8.3 us  [mirror_exchange(): lax.all_to_all(v, (*axes, 'cols'), 0, 0, tiled=True, axis_index_groups=pa...]
    ppermute x0 -> x7, starting transfers between devices: none -> 24 us  [sweep(): lax.ppermute(held[way], 'cols', [((y + way) % GROUPS, y) for y in range(G...]
    ppermute x5 -> x6, waiting for transfers between devices: 37.6 us -> 18.1 us  [swap(): return lax.ppermute(v, axis, [(0, 1), (1, 0)])]
    ppermute x5 -> x6, starting transfers between devices: 22.3 us -> 33.6 us  [swap(): return lax.ppermute(v, axis, [(0, 1), (1, 0)])]
    all_to_all x1 -> x2, starting transfers between devices: 5.57 us -> 11.2 us  [exchange(): lax.all_to_all(v, axes, 0, 0, tiled=True).reshape(2, GROUPS, *v.shape[1:])]
    pallas_call x9 -> x14, Pallas kernels: 62.6 us -> 68.1 us  [run(): pl.pallas_call(kernel, out_shape=shapes[0] if single else shapes, in_spec...]
    ppermute x0 -> x7, waiting for transfers between devices: none -> 5.35 us  [sweep(): lax.ppermute(held[way], 'cols', [((y + way) % GROUPS, y) for y in range(G...]
    ppermute x2 -> x4, starting transfers between devices: 9.41 us -> 14.3 us  [mirror(): return lax.ppermute(v, axes, [(i, n - 1 - i) for i in range(n)])]
  transfers between devices with their start and end apart: 10 -> 21, of which waited for: 8 -> 8; matrix products, arithmetic and copies ran while one was open for 0% -> 1% of each run, Pallas kernels for 21% -> 22%
where the time goes in v3:
time: 227 us; the launch traced here: 223 us
  starting transfers between devices  101 us (44%)
  Pallas kernels  68.1 us (30%)
  waiting for transfers between devices  35.6 us (16%)
  local copies, waits for them, and re-layouts  8.83 us (4%)
  blocking collectives  7.96 us (4%)
    pallas_call x14, Pallas kernels, run(): pl.pallas_call(kernel, out_shape=shapes[0] if single else shapes, in_spec...  68.1 us
    ppermute x6, starting transfers between devices, swap(): return lax.ppermute(v, axis, [(0, 1), (1, 0)])  33.6 us
    ppermute x7, starting transfers between devices, sweep(): lax.ppermute(held[way], 'cols', [((y + way) % GROUPS, y) for y in range(G...  24 us
    ppermute x6, waiting for transfers between devices, swap(): return lax.ppermute(v, axis, [(0, 1), (1, 0)])  18.1 us
    ppermute x4, starting transfers between devices, mirror(): return lax.ppermute(v, axes, [(i, n - 1 - i) for i in range(n)])  14.3 us
    all_to_all x1, starting transfers between devices, mirror_exchange(): lax.all_to_all(v, (*axes, 'cols'), 0, 0, tiled=True, axis_index_groups=pa...  12.2 us
    all_to_all x2, starting transfers between devices, exchange(): lax.all_to_all(v, axes, 0, 0, tiled=True).reshape(2, GROUPS, *v.shape[1:])  11.2 us
    all_to_all x1, waiting for transfers between devices, mirror_exchange(): lax.all_to_all(v, (*axes, 'cols'), 0, 0, tiled=True, axis_index_groups=pa...  8.3 us
  transfers between devices with their start and end apart: 21, of which 8 were waited for; matrix products, arithmetic and copies ran while one was open for 1% of the time, Pallas kernels for 22%

profile of v3, /device:TPU:1, one launch (start us, length us, event | category | flops | bytes accessed | tf_op | source)
XLA Modules:
  0.0 222.9 jit_solution(3761407183336566948)
XLA Ops:
  0.0 7.5 %shard_map.37 = (f32[384,1024]{1,0:T(8,128)}, f32[4,16,512]{2,1,0:T(8,128)}, f32[208,512]{1,0:T(8,128)}, f32[208,512]{1,0:T(8,128)}) custom-call(s32[1]{0:T(128)} %bitcast.core_ref, s32[1,1024]{1,0:T(1,128)} %order_ref.1, f32[1024,384]{1,0:T(8,128)} %x_ref.1, f32[4,1024,128]{2,1,0:T(8,128)} %v_ref.1), custom_call_target="tpu_custom_call" | custom-call | tf_op jit(solution)/shard_map/pallas_call | solution.py:215
  7.5 8.7 %collective-permute-start.7 = (f32[208,512]{1,0:T(8,128)}, f32[208,512]{1,0:T(8,128)S(1)}, u32[]{:S(2)}, u32[]{:S(2)}) collective-permute-start(f32[208,512]{1,0:T(8,128)} %get-tuple-element.26), channel_id=1, source_target_pairs={{0,8},{8,0},{1,9},{9,1},{2,10},{10,2},{3,11},{11,3},{4,12},{12,4},... | collective-permute-start | bytes 1277960 | tf_op jit(solution)/shard_map/ppermute | solution.py:228
  16.2 1.6 collective-permute-done.7
  17.8 1.1 add.9
  18.9 8.0 %all_to_all.25.parts_ref = f32[4,16,512]{2,1,0:T(8,128)} all-to-all(f32[4,16,512]{2,1,0:T(8,128)} %get-tuple-element.27), channel_id=1, replica_groups=mesh['x2'=2,'x1'=2,'z4'=2,'z2'=2,'z1'=2,'core'=2,'cols'=8] {'z1','core'}, dimensions={0} | all-to-all | bytes 262144 | tf_op jit(solution)/shard_map/all_to_all | solution.py:269
  26.9 1.8 shard_map.38
  28.6 5.6 %all-to-all-start.1 = ((f32[16,16,512]{2,1,0:T(8,128)}), f32[16,16,512]{2,1,0:T(8,128)S(1)}, u32[]{:S(2)}, u32[]{:S(2)}) async-start(f32[16,16,512]{2,1,0:T(8,128)} %shard_map.38), calls=%async_computation.1 | async-start | bytes 1048576 | tf_op jit(solution)/shard_map/all_to_all | solution.py:237
  34.2 2.1 collective-permute-start.8
  36.3 15.6 %collective-permute-done.8 = f32[208,512]{1,0:T(8,128)S(1)} collective-permute-done((f32[208,512]{1,0:T(8,128)S(1)}, f32[208,512]{1,0:T(8,128)S(1)}, u32[]{:S(2)}, u32[]{:S(2)}) %collective-permute-start.8) | collective-permute-done | bytes 426016 | tf_op jit(solution)/shard_map/ppermute | solution.py:228
  51.9 2.8 %collective-permute-start.9 = (f32[48,512]{1,0:T(8,128)S(1)}, f32[48,512]{1,0:T(8,128)S(1)}, u32[]{:S(2)}, u32[]{:S(2)}) collective-permute-start(f32[48,512]{1,0:T(8,128)S(1)} %slice_add_fusion.1.w_own_ref), channel_id=1, source_target_pairs={{0,32},{32,0},{1,33},{33,1},{2,34},{34,2},{3,35},{35,3},{4,36},{36... | collective-permute-start | bytes 294920 | tf_op jit(solution)/shard_map/ppermute | solution.py:228
  54.7 0.0 copy-start.1
  54.7 0.8 copy-done.1
  55.5 9.0 %shard_map.39.inv_ref = f32[128,128]{1,0:T(8,128)} custom-call(s32[1]{0:T(128)} %bitcast.4.side_ref, f32[2,8,16,512]{3,2,1,0:T(8,128)} %bitcast.12), custom_call_target="tpu_custom_call" | custom-call | tf_op jit(solution)/shard_map/pallas_call | solution.py:215
  64.5 0.0 collective-permute-done.9.w_sib_ref
  64.6 0.6 copy-done.18
  65.2 2.6 %shard_map.40 = (f32[32,384]{1,0:T(8,128)}, f32[48,128]{1,0:T(8,128)}, f32[16,16,384]{2,1,0:T(8,128)}) custom-call(s32[1]{0:T(128)} %bitcast.4.side_ref, f32[128,128]{1,0:T(8,128)} %shard_map.39.inv_ref, f32[2,8,16,512]{3,2,1,0:T(8,128)} %bitcast.13, f32[48,512]{1,0:T(8,128)} %copy-done.5, f32[48,512]{1,0:T(8,128)} %copy-done.18), custom_call_target="tpu_custom_call" | custom-call | tf_op jit(solution)/shard_map/pallas_call | solution.py:215
  67.7 12.2 %all-to-all-start.2 = ((f32[16,16,384]{2,1,0:T(8,128)}), f32[16,16,384]{2,1,0:T(8,128)S(1)}, u32[]{:S(2)}, u32[]{:S(2)}) async-start(f32[16,16,384]{2,1,0:T(8,128)} %get-tuple-element.28), calls=%async_computation.2 | async-start | bytes 786432 | tf_op jit(solution)/shard_map/all_to_all | solution.py:243
  79.9 4.7 %collective-permute-start.10 = (f32[32,384]{1,0:T(8,128)}, f32[32,384]{1,0:T(8,128)S(1)}, u32[]{:S(2)}, u32[]{:S(2)}) collective-permute-start(f32[32,384]{1,0:T(8,128)} %get-tuple-element.29.w_own_ref), channel_id=1, source_target_pairs={{0,112},{16,96},{32,80},{48,64},{64,48},{80,32},{96,16},{112,0},{1... | collective-permute-start | bytes 147464 | tf_op jit(solution)/shard_map/ppermute | solution.py:233
  84.6 8.3 %all-to-all-done.2 = f32[16,16,384]{2,1,0:T(8,128)S(1)} async-done(((f32[16,16,384]{2,1,0:T(8,128)}), f32[16,16,384]{2,1,0:T(8,128)S(1)}, u32[]{:S(2)}, u32[]{:S(2)}) %all-to-all-start.2) | async-done | bytes 393248 | tf_op jit(solution)/shard_map/all_to_all | solution.py:243
  92.9 0.8 copy-done.2
  93.7 9.0 %shard_map.41.inv_ref = f32[128,128]{1,0:T(8,128)} custom-call(s32[1]{0:T(128)} %bitcast.3.side_ref, f32[2,8,16,384]{3,2,1,0:T(8,128)} %bitcast.15), custom_call_target="tpu_custom_call" | custom-call | tf_op jit(solution)/shard_map/pallas_call | solution.py:215
  102.7 0.6 copy-done.20
  103.3 2.5 %shard_map.42 = (f32[32,128]{1,0:T(8,128)}, f32[16,32,256]{2,1,0:T(8,128)}) custom-call(s32[1]{0:T(128)} %bitcast.3.side_ref, f32[128,128]{1,0:T(8,128)} %shard_map.41.inv_ref, f32[2,8,16,384]{3,2,1,0:T(8,128)} %bitcast.16, f32[32,384]{1,0:T(8,128)} %get-tuple-element.29.w_own_ref, f32[32,384]{1,0:T(8,128)} %copy-done.20), custom_call_target="tpu_custom_call" | custom-call | tf_op jit(solution)/shard_map/pallas_call | solution.py:215
  105.7 5.6 %all-to-all-start.3 = ((f32[16,32,256]{2,1,0:T(8,128)}), f32[16,32,256]{2,1,0:T(8,128)S(1)}, u32[]{:S(2)}, u32[]{:S(2)}) async-start(f32[16,32,256]{2,1,0:T(8,128)} %get-tuple-element.30), calls=%async_computation.3 | async-start | bytes 1048576 | tf_op jit(solution)/shard_map/all_to_all | solution.py:237
  111.4 5.0 %collective-permute-start.12 = (f32[160,512]{1,0:T(8,128)S(1)}, f32[160,512]{1,0:T(8,128)S(1)}, u32[]{:S(2)}, u32[]{:S(2)}) collective-permute-start(f32[160,512]{1,0:T(8,128)S(1)} %slice_add_fusion.t_own_ref), channel_id=1, source_target_pairs={{0,32},{32,0},{1,33},{33,1},{2,34},{34,2},{3,35},{35,3},{4,36},{36... | collective-permute-start | bytes 983048 | tf_op jit(solution)/shard_map/ppermute | solution.py:228
  116.4 1.0 slice.16
  117.3 4.5 %collective-permute-start = (f32[64,1024]{1,0:T(8,128)S(1)}, f32[64,1024]{1,0:T(8,128)S(1)}, u32[]{:S(2)}, u32[]{:S(2)}) collective-permute-start(f32[64,1024]{1,0:T(8,128)S(1)} %slice.16), channel_id=1, source_target_pairs={{1,0},{2,1},{3,2},{4,3},{5,4},{6,5},{7,6},{0,7},{9,8},{10,9},{11,1... | collective-permute-start | bytes 786440 | tf_op jit(solution)/shard_map/ppermute | solution.py:280
  121.9 0.9 all-to-all-done.3
  122.8 0.8 broadcast_in_dim.26
  123.6 5.7 %all-to-all-start.4 = ((f32[8,80,128]{2,1,0:T(8,128)}), f32[8,80,128]{2,1,0:T(8,128)S(1)}, u32[]{:S(2)}, u32[]{:S(2)}) async-start(f32[8,80,128]{2,1,0:T(8,128)} %broadcast_in_dim.26), calls=%async_computation.4 | async-start | bytes 655360 | tf_op jit(solution)/shard_map/all_to_all | solution.py:302
  129.3 0.9 collective-permute-done.12.t_sib_ref
  130.2 0.7 copy-done.7
  131.0 2.8 %shard_map.46 = (f32[160,384]{1,0:T(8,128)}, f32[160,128]{1,0:T(8,128)}) custom-call(s32[1]{0:T(128)} %bitcast.4.side_ref, f32[128,128]{1,0:T(8,128)} %shard_map.39.inv_ref, f32[2,8,16,512]{3,2,1,0:T(8,128)} %bitcast.14, f32[160,512]{1,0:T(8,128)} %copy-done.4, f32[160,512]{1,0:T(8,128)} %copy-done.7), custom_call_target="tpu_custom_call" | custom-call | tf_op jit(solution)/shard_map/pallas_call | solution.py:215
  133.7 2.9 %collective-permute-start.13 = (f32[160,384]{1,0:T(8,128)}, f32[160,384]{1,0:T(8,128)S(1)}, u32[]{:S(2)}, u32[]{:S(2)}) collective-permute-start(f32[160,384]{1,0:T(8,128)} %get-tuple-element.32.t_own_ref), channel_id=1, source_target_pairs={{0,112},{16,96},{32,80},{48,64},{64,48},{80,32},{96,16},{112,0},{1... | collective-permute-start | bytes 737288 | tf_op jit(solution)/shard_map/ppermute | solution.py:233
  136.7 3.4 %collective-permute-start.1 = (f32[64,1024]{1,0:T(8,128)S(1)}, f32[64,1024]{1,0:T(8,128)S(1)}, u32[]{:S(2)}, u32[]{:S(2)}) collective-permute-start(f32[64,1024]{1,0:T(8,128)S(1)} %slice.16), channel_id=1, source_target_pairs={{7,0},{0,1},{1,2},{2,3},{3,4},{4,5},{5,6},{6,7},{15,8},{8,9},{9,10... | collective-permute-start | bytes 786440 | tf_op jit(solution)/shard_map/ppermute | solution.py:280
  140.0 0.0 collective-permute-done.refs_0_
  140.1 3.1 %collective-permute-start.2 = (f32[64,1024]{1,0:T(8,128)S(1)}, f32[64,1024]{1,0:T(8,128)S(1)}, u32[]{:S(2)}, u32[]{:S(2)}) collective-permute-start(f32[64,1024]{1,0:T(8,128)S(1)} %collective-permute-done.refs_0_), channel_id=1, source_target_pairs={{1,0},{2,1},{3,2},{4,3},{5,4},{6,5},{7,6},{0,7},{9,8},{10,9},{11,1... | collective-permute-start | bytes 786440 | tf_op jit(solution)/shard_map/ppermute | solution.py:280
  143.2 0.0 copy-start.16
  143.2 0.7 copy-done.16
  143.9 2.7 %shard_map.47 = (f32[160,256]{1,0:T(8,128)}, f32[160,128]{1,0:T(8,128)}) custom-call(s32[1]{0:T(128)} %bitcast.3.side_ref, f32[128,128]{1,0:T(8,128)} %shard_map.41.inv_ref, f32[2,8,16,384]{3,2,1,0:T(8,128)} %bitcast.17, f32[160,384]{1,0:T(8,128)} %get-tuple-element.32.t_own_ref, f32[160,384]{1,0:T(8,128)} %copy-done.16), custom_call_target="tpu_custom_call" | custom-call | tf_op jit(solution)/shard_map/pallas_call | solution.py:215
  146.6 5.2 %collective-permute-start.14 = (f32[160,256]{1,0:T(8,128)}, f32[160,256]{1,0:T(8,128)S(1)}, u32[]{:S(2)}, u32[]{:S(2)}) collective-permute-start(f32[160,256]{1,0:T(8,128)} %get-tuple-element.33.t_own_ref), channel_id=1, source_target_pairs={{0,128},{128,0},{1,129},{129,1},{2,130},{130,2},{3,131},{131,3},{4... | collective-permute-start | bytes 491528 | tf_op jit(solution)/shard_map/ppermute | solution.py:228
  151.8 0.0 collective-permute-done.1.refs_1_
  151.8 1.9 collective-permute-start.3
  153.7 4.6 %collective-permute-start.4 = (f32[64,1024]{1,0:T(8,128)S(1)}, f32[64,1024]{1,0:T(8,128)S(1)}, u32[]{:S(2)}, u32[]{:S(2)}) collective-permute-start(f32[64,1024]{1,0:T(8,128)S(1)} %collective-permute-done.2.refs_2_), channel_id=1, source_target_pairs={{1,0},{2,1},{3,2},{4,3},{5,4},{6,5},{7,6},{0,7},{9,8},{10,9},{11,1... | collective-permute-start | bytes 786440 | tf_op jit(solution)/shard_map/ppermute | solution.py:280
  158.3 9.1 %shard_map.43.inv_ref = f32[128,128]{1,0:T(8,128)} custom-call(s32[1]{0:T(128)} %bitcast.2.side_ref, f32[2,8,32,256]{3,2,1,0:T(8,128)} %bitcast.9), custom_call_target="tpu_custom_call" | custom-call | tf_op jit(solution)/shard_map/pallas_call | solution.py:215
  167.4 0.7 copy-done.17
  168.1 2.5 %shard_map.48 = (f32[160,128]{1,0:T(8,128)}, f32[160,128]{1,0:T(8,128)}) custom-call(s32[1]{0:T(128)} %bitcast.2.side_ref, f32[128,128]{1,0:T(8,128)} %shard_map.43.inv_ref, f32[2,8,32,256]{3,2,1,0:T(8,128)} %bitcast.10, f32[160,256]{1,0:T(8,128)} %get-tuple-element.33.t_own_ref, f32[160,256]{1,0:T(8,128)} %copy-done.17), custom_call_target="tpu_custom_call" | custom-call | tf_op jit(solution)/shard_map/pallas_call | solution.py:215
  170.5 3.2 %collective-permute-start.15 = (f32[160,128]{1,0:T(8,128)}, f32[160,128]{1,0:T(8,128)S(1)}, u32[]{:S(2)}, u32[]{:S(2)}) collective-permute-start(f32[160,128]{1,0:T(8,128)} %get-tuple-element.34.t_own_ref), channel_id=1, source_target_pairs={{0,384},{128,256},{256,128},{384,0},{1,385},{129,257},{257,129},{3... | collective-permute-start | bytes 245768 | tf_op jit(solution)/shard_map/ppermute | solution.py:233
  173.7 2.4 %shard_map.44 = (f32[128,128]{1,0:T(8,128)}, f32[128,128]{1,0:T(8,128)}) custom-call(s32[1]{0:T(128)} %bitcast.2.side_ref, f32[128,128]{1,0:T(8,128)} %shard_map.43.inv_ref, f32[2,8,32,256]{3,2,1,0:T(8,128)} %bitcast.11), custom_call_target="tpu_custom_call" | custom-call | tf_op jit(solution)/shard_map/pallas_call | solution.py:215
  176.1 3.5 %collective-permute-start.11 = (f32[128,128]{1,0:T(8,128)}, f32[128,128]{1,0:T(8,128)S(1)}, u32[]{:S(2)}, u32[]{:S(2)}) collective-permute-start(f32[128,128]{1,0:T(8,128)} %get-tuple-element.31.own_ref.a_own_ref), channel_id=1, source_target_pairs={{0,384},{128,256},{256,128},{384,0},{1,385},{129,257},{257,129},{3... | collective-permute-start | bytes 196616 | tf_op jit(solution)/shard_map/ppermute | solution.py:233
  179.6 2.9 %collective-permute-done.11.sib_ref.a_sib_ref = f32[128,128]{1,0:T(8,128)S(1)} collective-permute-done((f32[128,128]{1,0:T(8,128)}, f32[128,128]{1,0:T(8,128)S(1)}, u32[]{:S(2)}, u32[]{:S(2)}) %collective-permute-start.11) | collective-permute-done | bytes 65568 | tf_op jit(solution)/shard_map/ppermute | solution.py:233
  182.5 0.6 copy-done.15
  183.1 8.9 %shard_map.45.inv_ref = f32[128,128]{1,0:T(8,128)} custom-call(f32[128,128]{1,0:T(8,128)} %get-tuple-element.31.own_ref.a_own_ref, f32[128,128]{1,0:T(8,128)} %copy-done.15), custom_call_target="tpu_custom_call" | custom-call | tf_op jit(solution)/shard_map/pallas_call | solution.py:215
  192.1 0.7 copy-done.3
  192.8 0.0 copy-done.19
  192.8 3.0 %shard_map.49.refs_7_ = f32[160,512]{1,0:T(8,128)} custom-call(f32[128,128]{1,0:T(8,128)} %shard_map.45.inv_ref, f32[128,128]{1,0:T(8,128)} %get-tuple-element.31.own_ref.a_own_ref, f32[128,128]{1,0:T(8,128)} %copy-done.15, f32[160,128]{1,0:T(8,128)} %get-tuple-element.34.t_own_ref, f32[160,128]{1,0:T(8,128)} %copy-done.19, ...), custom_call_target="tpu_custom_call" | custom-call | tf_op jit(solution)/shard_map/pallas_call | solution.py:215
  195.8 9.8 %collective-permute-start.16 = (f32[160,512]{1,0:T(8,128)}, f32[160,512]{1,0:T(8,128)S(1)}, u32[]{:S(2)}, u32[]{:S(2)}) collective-permute-start(f32[160,512]{1,0:T(8,128)} %shard_map.49.refs_7_), channel_id=1, source_target_pairs={{0,8},{8,0},{1,9},{9,1},{2,10},{10,2},{3,11},{11,3},{4,12},{12,4},... | collective-permute-start | bytes 983048 | tf_op jit(solution)/shard_map/ppermute | solution.py:228
  205.6 1.9 collective-permute-start.5
  207.6 4.6 %collective-permute-start.6 = (f32[64,1024]{1,0:T(8,128)S(1)}, f32[64,1024]{1,0:T(8,128)S(1)}, u32[]{:S(2)}, u32[]{:S(2)}) collective-permute-start(f32[64,1024]{1,0:T(8,128)S(1)} %collective-permute-done.4.refs_4_), channel_id=1, source_target_pairs={{1,0},{2,1},{3,2},{4,3},{5,4},{6,5},{7,6},{0,7},{9,8},{10,9},{11,1... | collective-permute-start | bytes 786440 | tf_op jit(solution)/shard_map/ppermute | solution.py:280
  212.2 4.4 %collective-permute-done.5.refs_5_ = f32[64,1024]{1,0:T(8,128)S(1)} collective-permute-done((f32[64,1024]{1,0:T(8,128)S(1)}, f32[64,1024]{1,0:T(8,128)S(1)}, u32[]{:S(2)}, u32[]{:S(2)}) %collective-permute-start.5) | collective-permute-done | bytes 262176 | tf_op jit(solution)/shard_map/ppermute | solution.py:280
  216.6 0.9 collective-permute-done.6.refs_6_
  217.6 0.7 copy-done.14
  218.2 0.1 copy-done.6
  218.3 4.5 %shard_map.50 = f32[320,1024]{1,0:T(8,128)} custom-call(s32[1]{0:T(128)} %bitcast.core_ref, s32[1]{0:T(128)} %bitcast.1.col_ref, f32[384,1024]{1,0:T(8,128)} %get-tuple-element.23.xt_ref, f32[64,1024]{1,0:T(8,128)} %copy-done.8, f32[64,1024]{1,0:T(8,128)} %copy-done.9, f32[64,1024]{1,0:T(8,128)} %copy-done.10, f32[64,1024]{1,0:T(8,128)} %copy-done.11, ...), custom_call_target="tpu_custom_call" | custom-call | tf_op jit(solution)/shard_map/pallas_call | solution.py:215
  (45 shorter events, 0.2 us)
Async XLA Ops:
  7.5 10.3 %collective-permute-start.7 = (f32[208,512]{1,0:T(8,128)}, f32[208,512]{1,0:T(8,128)S(1)}, u32[]{:S(2)}, u32[]{:S(2)}) collective-permute-start(f32[208,512]{1,0:T(8,128)} %get-tuple-element.26), channel_id=1, source_target_pairs={{0,8},{8,0},{1,9},{9,1},{2,10},{10,2},{3,11},{11,3},{4,12},{12,4},... | collective-permute-start | bytes 1277960 | tf_op jit(solution)/shard_map/ppermute | solution.py:228
  28.6 26.1 %all-to-all-start.1 = ((f32[16,16,512]{2,1,0:T(8,128)}), f32[16,16,512]{2,1,0:T(8,128)S(1)}, u32[]{:S(2)}, u32[]{:S(2)}) async-start(f32[16,16,512]{2,1,0:T(8,128)} %shard_map.38), calls=%async_computation.1 | async-start | bytes 1048576 | tf_op jit(solution)/shard_map/all_to_all | solution.py:237
  34.2 17.7 %collective-permute-start.8 = (f32[208,512]{1,0:T(8,128)S(1)}, f32[208,512]{1,0:T(8,128)S(1)}, u32[]{:S(2)}, u32[]{:S(2)}) collective-permute-start(f32[208,512]{1,0:T(8,128)S(1)} %add.9), channel_id=1, source_target_pairs={{0,16},{16,0},{1,17},{17,1},{2,18},{18,2},{3,19},{19,3},{4,20},{20... | collective-permute-start | bytes 1277960 | tf_op jit(solution)/shard_map/ppermute | solution.py:228
  51.9 12.7 %copy-start.5 = (f32[48,512]{1,0:T(8,128)}, f32[48,512]{1,0:T(8,128)S(1)}, u32[]{:S(2)}) copy-start(f32[48,512]{1,0:T(8,128)S(1)} %slice_add_fusion.1.w_own_ref) | copy-start | bytes 294916
  51.9 12.7 %collective-permute-start.9 = (f32[48,512]{1,0:T(8,128)S(1)}, f32[48,512]{1,0:T(8,128)S(1)}, u32[]{:S(2)}, u32[]{:S(2)}) collective-permute-start(f32[48,512]{1,0:T(8,128)S(1)} %slice_add_fusion.1.w_own_ref), channel_id=1, source_target_pairs={{0,32},{32,0},{1,33},{33,1},{2,34},{34,2},{3,35},{35,3},{4,36},{36... | collective-permute-start | bytes 294920 | tf_op jit(solution)/shard_map/ppermute | solution.py:228
  54.7 0.8 copy-start.1
  64.5 0.6 copy-start.18
  67.7 25.1 %all-to-all-start.2 = ((f32[16,16,384]{2,1,0:T(8,128)}), f32[16,16,384]{2,1,0:T(8,128)S(1)}, u32[]{:S(2)}, u32[]{:S(2)}) async-start(f32[16,16,384]{2,1,0:T(8,128)} %get-tuple-element.28), calls=%async_computation.2 | async-start | bytes 786432 | tf_op jit(solution)/shard_map/all_to_all | solution.py:243
  79.9 22.7 %collective-permute-start.10 = (f32[32,384]{1,0:T(8,128)}, f32[32,384]{1,0:T(8,128)S(1)}, u32[]{:S(2)}, u32[]{:S(2)}) collective-permute-start(f32[32,384]{1,0:T(8,128)} %get-tuple-element.29.w_own_ref), channel_id=1, source_target_pairs={{0,112},{16,96},{32,80},{48,64},{64,48},{80,32},{96,16},{112,0},{1... | collective-permute-start | bytes 147464 | tf_op jit(solution)/shard_map/ppermute | solution.py:233
  92.9 0.8 copy-start.2
  102.7 19.2 %copy-start.21 = (f32[48,128]{1,0:T(8,128)S(1)}, f32[48,128]{1,0:T(8,128)}, u32[]{:S(2)}) copy-start(f32[48,128]{1,0:T(8,128)} %get-tuple-element.39) | copy-start | bytes 73732
  102.7 0.6 copy-start.20
  105.7 16.1 %copy-start.22 = (f32[32,128]{1,0:T(8,128)S(1)}, f32[32,128]{1,0:T(8,128)}, u32[]{:S(2)}) copy-start(f32[32,128]{1,0:T(8,128)} %get-tuple-element.40) | copy-start | bytes 49156
  105.7 17.1 %all-to-all-start.3 = ((f32[16,32,256]{2,1,0:T(8,128)}), f32[16,32,256]{2,1,0:T(8,128)S(1)}, u32[]{:S(2)}, u32[]{:S(2)}) async-start(f32[16,32,256]{2,1,0:T(8,128)} %get-tuple-element.30), calls=%async_computation.3 | async-start | bytes 1048576 | tf_op jit(solution)/shard_map/all_to_all | solution.py:237
  111.4 18.9 %copy-start.4 = (f32[160,512]{1,0:T(8,128)}, f32[160,512]{1,0:T(8,128)S(1)}, u32[]{:S(2)}) copy-start(f32[160,512]{1,0:T(8,128)S(1)} %slice_add_fusion.t_own_ref) | copy-start | bytes 983044
  111.4 18.8 %collective-permute-start.12 = (f32[160,512]{1,0:T(8,128)S(1)}, f32[160,512]{1,0:T(8,128)S(1)}, u32[]{:S(2)}, u32[]{:S(2)}) collective-permute-start(f32[160,512]{1,0:T(8,128)S(1)} %slice_add_fusion.t_own_ref), channel_id=1, source_target_pairs={{0,32},{32,0},{1,33},{33,1},{2,34},{34,2},{3,35},{35,3},{4,36},{36... | collective-permute-start | bytes 983048 | tf_op jit(solution)/shard_map/ppermute | solution.py:228
  117.3 22.7 %collective-permute-start = (f32[64,1024]{1,0:T(8,128)S(1)}, f32[64,1024]{1,0:T(8,128)S(1)}, u32[]{:S(2)}, u32[]{:S(2)}) collective-permute-start(f32[64,1024]{1,0:T(8,128)S(1)} %slice.16), channel_id=1, source_target_pairs={{1,0},{2,1},{3,2},{4,3},{5,4},{6,5},{7,6},{0,7},{9,8},{10,9},{11,1... | collective-permute-start | bytes 786440 | tf_op jit(solution)/shard_map/ppermute | solution.py:280
  122.8 23.8 %copy-start = (f32[16,32,256]{2,1,0:T(8,128)}, f32[16,32,256]{2,1,0:T(8,128)S(1)}, u32[]{:S(2)}) copy-start(f32[16,32,256]{2,1,0:T(8,128)S(1)} %all-to-all-done.3) | copy-start | bytes 1572868
  123.6 68.4 %all-to-all-start.4 = ((f32[8,80,128]{2,1,0:T(8,128)}), f32[8,80,128]{2,1,0:T(8,128)S(1)}, u32[]{:S(2)}, u32[]{:S(2)}) async-start(f32[8,80,128]{2,1,0:T(8,128)} %broadcast_in_dim.26), calls=%async_computation.4 | async-start | bytes 655360 | tf_op jit(solution)/shard_map/all_to_all | solution.py:302
  130.2 0.7 copy-start.7
  133.7 9.5 %collective-permute-start.13 = (f32[160,384]{1,0:T(8,128)}, f32[160,384]{1,0:T(8,128)S(1)}, u32[]{:S(2)}, u32[]{:S(2)}) collective-permute-start(f32[160,384]{1,0:T(8,128)} %get-tuple-element.32.t_own_ref), channel_id=1, source_target_pairs={{0,112},{16,96},{32,80},{48,64},{64,48},{80,32},{96,16},{112,0},{1... | collective-permute-start | bytes 737288 | tf_op jit(solution)/shard_map/ppermute | solution.py:233
  136.7 15.1 %collective-permute-start.1 = (f32[64,1024]{1,0:T(8,128)S(1)}, f32[64,1024]{1,0:T(8,128)S(1)}, u32[]{:S(2)}, u32[]{:S(2)}) collective-permute-start(f32[64,1024]{1,0:T(8,128)S(1)} %slice.16), channel_id=1, source_target_pairs={{7,0},{0,1},{1,2},{2,3},{3,4},{4,5},{5,6},{6,7},{15,8},{8,9},{9,10... | collective-permute-start | bytes 786440 | tf_op jit(solution)/shard_map/ppermute | solution.py:280
  140.0 52.0 %copy-start.8 = (f32[64,1024]{1,0:T(8,128)}, f32[64,1024]{1,0:T(8,128)S(1)}, u32[]{:S(2)}) copy-start(f32[64,1024]{1,0:T(8,128)S(1)} %collective-permute-done.refs_0_) | copy-start | bytes 786436
  140.1 13.7 %collective-permute-start.2 = (f32[64,1024]{1,0:T(8,128)S(1)}, f32[64,1024]{1,0:T(8,128)S(1)}, u32[]{:S(2)}, u32[]{:S(2)}) collective-permute-start(f32[64,1024]{1,0:T(8,128)S(1)} %collective-permute-done.refs_0_), channel_id=1, source_target_pairs={{1,0},{2,1},{3,2},{4,3},{5,4},{6,5},{7,6},{0,7},{9,8},{10,9},{11,1... | collective-permute-start | bytes 786440 | tf_op jit(solution)/shard_map/ppermute | solution.py:280
  143.2 0.7 copy-start.16
  146.6 20.8 %collective-permute-start.14 = (f32[160,256]{1,0:T(8,128)}, f32[160,256]{1,0:T(8,128)S(1)}, u32[]{:S(2)}, u32[]{:S(2)}) collective-permute-start(f32[160,256]{1,0:T(8,128)} %get-tuple-element.33.t_own_ref), channel_id=1, source_target_pairs={{0,128},{128,0},{1,129},{129,1},{2,130},{130,2},{3,131},{131,3},{4... | collective-permute-start | bytes 491528 | tf_op jit(solution)/shard_map/ppermute | solution.py:228
  151.8 44.0 %copy-start.9 = (f32[64,1024]{1,0:T(8,128)}, f32[64,1024]{1,0:T(8,128)S(1)}, u32[]{:S(2)}) copy-start(f32[64,1024]{1,0:T(8,128)S(1)} %collective-permute-done.1.refs_1_) | copy-start | bytes 786436
  151.8 53.8 %collective-permute-start.3 = (f32[64,1024]{1,0:T(8,128)S(1)}, f32[64,1024]{1,0:T(8,128)S(1)}, u32[]{:S(2)}, u32[]{:S(2)}) collective-permute-start(f32[64,1024]{1,0:T(8,128)S(1)} %collective-permute-done.1.refs_1_), channel_id=1, source_target_pairs={{7,0},{0,1},{1,2},{2,3},{3,4},{4,5},{5,6},{6,7},{15,8},{8,9},{9,10... | collective-permute-start | bytes 786440 | tf_op jit(solution)/shard_map/ppermute | solution.py:280
  153.7 42.1 %copy-start.10 = (f32[64,1024]{1,0:T(8,128)}, f32[64,1024]{1,0:T(8,128)S(1)}, u32[]{:S(2)}) copy-start(f32[64,1024]{1,0:T(8,128)S(1)} %collective-permute-done.2.refs_2_) | copy-start | bytes 786436
  153.7 53.8 %collective-permute-start.4 = (f32[64,1024]{1,0:T(8,128)S(1)}, f32[64,1024]{1,0:T(8,128)S(1)}, u32[]{:S(2)}, u32[]{:S(2)}) collective-permute-start(f32[64,1024]{1,0:T(8,128)S(1)} %collective-permute-done.2.refs_2_), channel_id=1, source_target_pairs={{1,0},{2,1},{3,2},{4,3},{5,4},{6,5},{7,6},{0,7},{9,8},{10,9},{11,1... | collective-permute-start | bytes 786440 | tf_op jit(solution)/shard_map/ppermute | solution.py:280
  167.4 0.7 copy-start.17
  170.5 21.5 %collective-permute-start.15 = (f32[160,128]{1,0:T(8,128)}, f32[160,128]{1,0:T(8,128)S(1)}, u32[]{:S(2)}, u32[]{:S(2)}) collective-permute-start(f32[160,128]{1,0:T(8,128)} %get-tuple-element.34.t_own_ref), channel_id=1, source_target_pairs={{0,384},{128,256},{256,128},{384,0},{1,385},{129,257},{257,129},{3... | collective-permute-start | bytes 245768 | tf_op jit(solution)/shard_map/ppermute | solution.py:233
  176.1 6.4 %collective-permute-start.11 = (f32[128,128]{1,0:T(8,128)}, f32[128,128]{1,0:T(8,128)S(1)}, u32[]{:S(2)}, u32[]{:S(2)}) collective-permute-start(f32[128,128]{1,0:T(8,128)} %get-tuple-element.31.own_ref.a_own_ref), channel_id=1, source_target_pairs={{0,384},{128,256},{256,128},{384,0},{1,385},{129,257},{257,129},{3... | collective-permute-start | bytes 196616 | tf_op jit(solution)/shard_map/ppermute | solution.py:233
  182.5 0.6 copy-start.15
  192.0 0.7 copy-start.3
  192.0 0.7 copy-start.19
  195.8 21.7 %collective-permute-start.16 = (f32[160,512]{1,0:T(8,128)}, f32[160,512]{1,0:T(8,128)S(1)}, u32[]{:S(2)}, u32[]{:S(2)}) collective-permute-start(f32[160,512]{1,0:T(8,128)} %shard_map.49.refs_7_), channel_id=1, source_target_pairs={{0,8},{8,0},{1,9},{9,1},{2,10},{10,2},{3,11},{11,3},{4,12},{12,4},... | collective-permute-start | bytes 983048 | tf_op jit(solution)/shard_map/ppermute | solution.py:228
  205.6 11.9 %copy-start.11 = (f32[64,1024]{1,0:T(8,128)}, f32[64,1024]{1,0:T(8,128)S(1)}, u32[]{:S(2)}) copy-start(f32[64,1024]{1,0:T(8,128)S(1)} %collective-permute-done.3.refs_3_) | copy-start | bytes 786436
  205.6 11.0 %collective-permute-start.5 = (f32[64,1024]{1,0:T(8,128)S(1)}, f32[64,1024]{1,0:T(8,128)S(1)}, u32[]{:S(2)}, u32[]{:S(2)}) collective-permute-start(f32[64,1024]{1,0:T(8,128)S(1)} %collective-permute-done.3.refs_3_), channel_id=1, source_target_pairs={{7,0},{0,1},{1,2},{2,3},{3,4},{4,5},{5,6},{6,7},{15,8},{8,9},{9,10... | collective-permute-start | bytes 786440 | tf_op jit(solution)/shard_map/ppermute | solution.py:280
  207.6 10.0 %copy-start.12 = (f32[64,1024]{1,0:T(8,128)}, f32[64,1024]{1,0:T(8,128)S(1)}, u32[]{:S(2)}) copy-start(f32[64,1024]{1,0:T(8,128)S(1)} %collective-permute-done.4.refs_4_) | copy-start | bytes 786436
  207.6 9.9 %collective-permute-start.6 = (f32[64,1024]{1,0:T(8,128)S(1)}, f32[64,1024]{1,0:T(8,128)S(1)}, u32[]{:S(2)}, u32[]{:S(2)}) collective-permute-start(f32[64,1024]{1,0:T(8,128)S(1)} %collective-permute-done.4.refs_4_), channel_id=1, source_target_pairs={{1,0},{2,1},{3,2},{4,3},{5,4},{6,5},{7,6},{0,7},{9,8},{10,9},{11,1... | collective-permute-start | bytes 786440 | tf_op jit(solution)/shard_map/ppermute | solution.py:280
  216.6 0.9 copy-start.13
  217.5 0.7 copy-start.14
  217.5 0.8 copy-start.6

commit v4 on v3

v4 whole, which is shorter than its diff:
```python
import functools
import math

import jax
import jax.numpy as jnp
from jax import lax
from jax.experimental import pallas as pl
from jax.experimental.pallas import tpu as pltpu
from jax.sharding import Mesh, PartitionSpec as P


R = 128
LEVELS = 4
WB = 16
GROUPS = 8
RING = (1, -1, 2, -2, 3, -3, 4)
ROW_AXES = ("x2", "x1", "z4", "z2", "z1", "core")
HIGH = lax.Precision.HIGHEST
F32 = jnp.float32
BF16 = jnp.bfloat16


def halves(x):
    hi = x.astype(BF16)
    return hi, (x - hi.astype(F32)).astype(BF16)


def mm(a, b):
    dot = functools.partial(jnp.dot, preferred_element_type=F32)
    return dot(a[0], b[0]) + (dot(a[0], b[1]) + dot(a[1], b[0]))


def exact(a, b, dims):
    return lax.dot_general(a, b, ((dims[0], dims[1]), ((), ())), precision=HIGH, preferred_element_type=F32)


def spd_inverse(g):
    lane = lax.broadcasted_iota(jnp.int32, (8, R), 1)
    sub = lax.broadcasted_iota(jnp.int32, (8, R), 0)
    n = R // 8
    tiles = [g[8 * i : 8 * i + 8, :] for i in range(n)]
    full = lambda v: jnp.broadcast_to(v, (8, R))
    row = lambda v, i: full(v[i : i + 1, :])
    for p in range(n):
        k = 8 * p
        cols = [[full(tiles[i][:, k + j : k + j + 1]) for i in range(n)] for j in range(8)]
        panel = (lane >= k) & (lane < k + 8)
        rows = jnp.where(panel, jnp.where(lane == sub + k, 1.0, 0.0), tiles[p])
        d = [cols[j][p] for j in range(8)]
        for s in range(0, 8, 2):
            a, b, c, e = row(d[s], s), row(d[s + 1], s), row(d[s], s + 1), row(d[s + 1], s + 1)
            r = 1.0 / (a * e - b * c)
            p00, p01, p10, p11 = e * r, -b * r, -c * r, a * r
            f0, f1 = d[s], d[s + 1]

            def step(v):
                b0, b1 = row(v, s), row(v, s + 1)
                n0, n1 = p00 * b0 + p01 * b1, p10 * b0 + p11 * b1
                return jnp.where(sub == s, n0, jnp.where(sub == s + 1, n1, v - f0 * n0 - f1 * n1))

            for j in range(s + 2, 8):
                d[j] = step(d[j])
            rows = step(rows)
        new = [row(rows, j) for j in range(8)]
        for i in range(n):
            if i != p:
                t = jnp.where(panel, 0.0, tiles[i])
                for j in range(8):
                    t = t - cols[j][i] * new[j]
                tiles[i] = t
        tiles[p] = rows
    return jnp.concatenate(tiles, axis=0)


def pair_inverse(own, sib):
    i = lax.broadcasted_iota(jnp.int32, (R, R), 0)
    j = lax.broadcasted_iota(jnp.int32, (R, R), 1)
    m = jnp.where(i == j, 1.0, 0.0) - exact(own, sib, ((1,), (0,)))
    return exact(spd_inverse(exact(m, m, ((0,), (0,)))), m, ((1,), (1,)))


def coefficients(p_own, p_sib, a_own, a_sib, inv):
    c_own = mm(halves(p_sib - mm(halves(p_own), a_sib)), inv)
    c_own_h = halves(c_own)
    c_sib_h = halves(p_own - mm(c_own_h, a_own))
    return c_own, c_own_h, c_sib_h


def project_kernel(core_ref, order_hbm, x_hbm, v_hbm, scale, xt_hbm, wt_ref, w0_ref, keep_ref, give_ref, *scratch):
    order_ref, x_ref, v_ref, xt_ref, sems = scratch
    copies = [
        pltpu.make_async_copy(order_hbm, order_ref, sems.at[0]),
        pltpu.make_async_copy(x_hbm, x_ref, sems.at[1]),
    ] + [pltpu.make_async_copy(v_hbm.at[i], v_ref.at[i], sems.at[2 + i]) for i in range(LEVELS)]
    out = pltpu.make_async_copy(xt_ref, xt_hbm, sems.at[2 + LEVELS])
    copies[0].start()
    copies[1].start()
    rows, width = x_ref.shape
    tgt = width - LEVELS * WB
    half = tgt // 2
    core = core_ref[0]
    copies[0].wait()
    at = lax.broadcasted_iota(jnp.int32, (rows, rows), 0)
    onehot = jnp.where(at == order_ref[...], 1.0, 0.0).astype(BF16)
    copies[1].wait()
    for copy in copies[2:]:
        copy.start()
    xt = x_ref[...].T
    xt_ref[...] = xt[:tgt]
    out.start()
    wt_ref[...] = xt[tgt:]
    hi, lo = halves(xt)
    hi = jnp.dot(hi, onehot, preferred_element_type=F32).astype(BF16)
    lo = jnp.dot(lo, onehot, preferred_element_type=F32).astype(BF16)
    later = slice(tgt, width - WB)
    for level in range(LEVELS):
        lanes = slice(R * level, R * level + R)
        copies[2 + level].wait()
        h = mm((hi, lo), halves(v_ref[level])) * scale[level]
        keep_ref[:half, lanes] = jnp.where(core == 0, h[:half], h[half:tgt])
        give_ref[:half, lanes] = jnp.where(core == 0, h[half:tgt], h[:half])
        keep_ref[half:, lanes] = h[later]
        give_ref[half:, lanes] = h[later]
        w0_ref[:, :, lanes] = jnp.broadcast_to(h[width - WB :][None], (w0_ref.shape[0], WB, R))
    out.wait()


def leaf_sum_kernel(parts_ref, out_ref):
    total = (parts_ref[0] + parts_ref[1]) + (parts_ref[2] + parts_ref[3])
    out_ref[...] = jnp.broadcast_to(total[None], out_ref.shape)


def block(ref, side, rows, lanes):
    part = ref[side, :, rows, lanes]
    return part.reshape(GROUPS * WB, part.shape[-1])


def couple(g_ref, side, lanes):
    rows = g_ref.shape[2]
    return block(g_ref, side, slice(rows - WB, rows), lanes)


def inverse_kernel(side_ref, g_ref, inv_ref):
    own = side_ref[0]
    inv_ref[...] = pair_inverse(couple(g_ref, own, slice(0, R)), couple(g_ref, 1 - own, slice(0, R)))


def last_inverse_kernel(own_ref, sib_ref, inv_ref):
    inv_ref[...] = pair_inverse(own_ref[...], sib_ref[...])


def advance(top_own, top_sib, low_own, low_sib, inv):
    a_own, a_sib = halves(top_own[:, :R]), halves(top_sib[:, :R])
    c, c_own, c_sib = coefficients(low_own[:, :R], low_sib[:, :R], a_own, a_sib, halves(inv))
    return c, (low_own[:, R:] + low_sib[:, R:]) - (
        mm(c_own, halves(top_own[:, R:])) + mm(c_sib, halves(top_sib[:, R:]))
    )


def basis0_kernel(side_ref, inv_ref, g_ref, w_own_ref, w_sib_ref, w_ref, c_hbm, send_ref, c_ref, sems):
    own, whole = side_ref[0], slice(0, g_ref.shape[3])
    c_ref[...], w = advance(
        couple(g_ref, own, whole), couple(g_ref, 1 - own, whole), w_own_ref[...], w_sib_ref[...], inv_ref[...]
    )
    out = pltpu.make_async_copy(c_ref, c_hbm, sems.at[0])
    out.start()
    left = w_ref.shape[0]
    w_ref[...] = w[:left]
    send_ref[...] = jnp.broadcast_to(w[left:][None], send_ref.shape)
    out.wait()


def basis1_kernel(side_ref, inv_ref, g_ref, w_own_ref, w_sib_ref, c0_hbm, c_ref, send_ref, c0_ref, sems):
    earlier = pltpu.make_async_copy(c0_hbm, c0_ref, sems.at[0])
    earlier.start()
    own, whole = side_ref[0], slice(0, g_ref.shape[3])
    c, w = advance(
        couple(g_ref, own, whole), couple(g_ref, 1 - own, whole), w_own_ref[...], w_sib_ref[...], inv_ref[...]
    )
    send_ref[...] = jnp.broadcast_to(w[None], send_ref.shape)
    earlier.wait()
    first = c0_ref.shape[0]
    c_ref[:, :first, :] = jnp.broadcast_to(c0_ref[...][None], (GROUPS, first, R))
    c_ref[:, first:, :] = jnp.broadcast_to(c[None], (GROUPS, *c.shape))


def last_basis_kernel(side_ref, inv_ref, g_ref, a_ref, c_hbm, c_ref, sems):
    own, whole, first = side_ref[0], slice(0, g_ref.shape[3]), slice(0, WB)
    c_ref[...], a_ref[...] = advance(
        couple(g_ref, own, whole),
        couple(g_ref, 1 - own, whole),
        block(g_ref, own, first, whole),
        block(g_ref, 1 - own, first, whole),
        inv_ref[...],
    )
    out = pltpu.make_async_copy(c_ref, c_hbm, sems.at[0])
    out.start()
    out.wait()


def targets_kernel(side_ref, inv_ref, g_ref, t_own_ref, t_sib_ref, t_ref, c_hbm, c_ref, sems):
    own, whole = side_ref[0], slice(0, g_ref.shape[3])
    c_ref[...], t = advance(
        couple(g_ref, own, whole), couple(g_ref, 1 - own, whole), t_own_ref[...], t_sib_ref[...], inv_ref[...]
    )
    out = pltpu.make_async_copy(c_ref, c_hbm, sems.at[0])
    out.start()
    t_ref[...] = t
    out.wait()


def split_sum_kernel(q_ref, moved_ref, t_ref, w_ref):
    half = t_ref.shape[0]
    t_ref[...] = q_ref[:half] + moved_ref[:half]
    w_ref[...] = q_ref[half:] + moved_ref[half:]


def total_kernel(inv_ref, a_own_ref, a_sib_ref, t_own_ref, t_sib_ref, *refs):
    far, (cw_ref, k_ref), near, sems = refs[:4], refs[4:6], refs[6:10], refs[10]
    copies = [pltpu.make_async_copy(a, b, sems.at[i]) for i, (a, b) in enumerate(zip(far, near))]
    for copy in copies:
        copy.start()
    t0_ref, t1_ref, t2_ref, w2_ref = near
    k3, k3h, _ = coefficients(
        t_own_ref[...], t_sib_ref[...], halves(a_own_ref[...]), halves(a_sib_ref[...]), halves(inv_ref[...])
    )
    for copy in copies:
        copy.wait()
    w = lambda i: halves(cw_ref[:, i * WB : i * WB + WB, :].reshape(GROUPS * WB, R))
    k2 = t2_ref[...] - mm(k3h, halves(w2_ref[...]))
    k2h = halves(k2)
    k1 = t1_ref[...] - (mm(k2h, w(4)) + mm(k3h, w(3)))
    k1h = halves(k1)
    k0 = t0_ref[...] - (mm(k1h, w(2)) + mm(k2h, w(1)) + mm(k3h, w(0)))
    for level, k in enumerate((k0, k1, k2, k3)):
        k_ref[:, R * level : R * level + R] = k


def final_kernel(core_ref, col_ref, xt_ref, wt_ref, *refs):
    part_refs, (k_own_ref, k_sib_ref, out_hbm, w_ref, out_ref, near_ref, sems) = refs[: GROUPS - 1], refs[GROUPS - 1 :]
    near = pltpu.make_async_copy(xt_ref, near_ref, sems.at[1])
    near.start()
    tgt, rows = out_ref.shape
    core, col = core_ref[0], col_ref[0]
    w_ref[col] = wt_ref[...]
    for shift, part_ref in zip(RING, part_refs):
        w_ref[lax.rem(col + (shift + GROUPS), GROUPS)] = part_ref[...]
    own, sib = k_own_ref[...], k_sib_ref[...]
    k = halves(jnp.concatenate([jnp.where(core == 0, own, sib), jnp.where(core == 0, sib, own)], axis=0))
    at = [(LEVELS - 1 - level) * WB for level in range(LEVELS)]
    w = halves(jnp.concatenate([w_ref[:, a : a + WB, :].reshape(GROUPS * WB, rows) for a in at], axis=0))
    half = tgt // 2
    outs = []
    for i in range(2):
        part = slice(i * half, i * half + half)
        total = mm((k[0][part], k[1][part]), w)
        if i == 0:
            near.wait()
        out_ref[part] = near_ref[part] - total
        outs.append(pltpu.make_async_copy(out_ref.at[part], out_hbm.at[part], sems.at[2 * i]))
        outs[-1].start()
    for out in outs:
        out.wait()


def call(kernel, outs, scalars=0, scratch=(), far=(), from_hbm=(), limit=16):
    shapes = [pltpu.HBM(s, F32) if i in far else pltpu.VMEM(s, F32) for i, s in enumerate(outs)]
    single = len(shapes) == 1
    vmem, smem = pl.BlockSpec(memory_space=pltpu.VMEM), pl.BlockSpec(memory_space=pltpu.SMEM)
    hbm = pl.BlockSpec(memory_space=pltpu.HBM)

    def run(*args):
        spaces = [None if i < scalars else pltpu.HBM if i in from_hbm else pltpu.VMEM for i in range(len(args))]
        specs = [smem if m is None else hbm if m is pltpu.HBM else vmem for m in spaces]
        through = [outs[i] for i in far] + [args[i].shape for i in from_hbm]
        return pl.pallas_call(
            kernel,
            out_shape=shapes[0] if single else shapes,
            in_specs=specs,
            out_specs=(hbm if far else vmem) if single else [hbm if i in far else vmem for i in range(len(outs))],
            scratch_shapes=[pltpu.VMEM(shape, F32) for shape in (*scratch, *through)]
            + ([pltpu.SemaphoreType.DMA((len(through) + 1,))] if through else []),
            compiler_params=pltpu.CompilerParams(vmem_limit_bytes=limit * 2**20),
        )(*(a if m is None else pltpu.with_memory_space_constraint(a, m) for a, m in zip(args, spaces)))

    return run


def swap(v, axis):
    return lax.ppermute(v, axis, [(0, 1), (1, 0)])


def mirror(v, axes):
    n = lax.axis_size(axes)
    return lax.ppermute(v, axes, [(i, n - 1 - i) for i in range(n)])


def exchange(v, axes):
    return lax.all_to_all(v, axes, 0, 0, tiled=True).reshape(2, GROUPS, *v.shape[1:])


def mirror_exchange(v, axes):
    n = lax.axis_size(axes)
    pairs = [[p * GROUPS + y for p in (a, n - 1 - a) for y in range(GROUPS)] for a in range(n // 2)]
    out = lax.all_to_all(v, (*axes, "cols"), 0, 0, tiled=True, axis_index_groups=pairs)
    return out.reshape(2, GROUPS, *v.shape[1:])


Z, X = ("z4", "z2", "z1"), ("x2", "x1")


def sweep(columns, row_bases, order):
    rows, width = columns.shape
    tgt = width - LEVELS * WB
    half = tgt // 2
    wide = LEVELS * R
    scale = [0.55 / math.sqrt(R * rows * (4 << level)) for level in range(LEVELS)]
    index = lambda axis: lax.axis_index(axis).astype(jnp.int32)[None]
    core = index("core")
    sides = [index(axis) for axis in ("z2", "z4", "x1")]

    def project(core_ref, order_hbm, x_hbm, v_hbm, *refs):
        project_kernel(core_ref, order_hbm, x_hbm, v_hbm, scale, *refs)

    early = half + (LEVELS - 1) * WB
    hbm, vmem = pl.BlockSpec(memory_space=pltpu.HBM), pl.BlockSpec(memory_space=pltpu.VMEM)
    xt, wt, w0, keep, give = pl.pallas_call(
        project,
        out_shape=[pltpu.HBM((tgt, rows), F32)]
        + [pltpu.VMEM(s, F32) for s in ((LEVELS * WB, rows), (4, WB, wide), (early, wide), (early, wide))],
        in_specs=[pl.BlockSpec(memory_space=pltpu.SMEM), hbm, hbm, hbm],
        out_specs=[hbm] + [vmem] * 4,
        scratch_shapes=[
            pltpu.VMEM(order.shape, jnp.int32),
            pltpu.VMEM(columns.shape, F32),
            pltpu.VMEM(row_bases.shape, F32),
            pltpu.VMEM((tgt, rows), F32),
            pltpu.SemaphoreType.DMA((3 + LEVELS,)),
        ],
        name="project",
        compiler_params=pltpu.CompilerParams(vmem_limit_bytes=40 * 2**20),
    )(core, *(pltpu.with_memory_space_constraint(v, pltpu.HBM) for v in (order, columns, row_bases)))

    q = keep + swap(give, "core")
    w0 = lax.all_to_all(lax.optimization_barrier((w0, q))[0], ("z1", "core"), 0, 0, tiled=True)
    moved = swap(q, "z1")
    t, w = call(split_sum_kernel, [(half, wide), (early - half, wide)])(q, moved)
    send = call(leaf_sum_kernel, [(2 * GROUPS, WB, wide)])(w0)
    g0 = exchange(send, ("z2", "cols"))
    w_sib = swap(w, "z2")
    t_sib = swap(t, "z2")

    parts, held = [], {1: wt, -1: wt}
    for shift in RING:
        way = 1 if shift > 0 else -1
        held[way] = lax.ppermute(held[way], "cols", [((y + way) % GROUPS, y) for y in range(GROUPS)])
        parts.append(held[way])

    inv0 = call(inverse_kernel, [(R, R)], 1)(sides[0], g0)
    w, cw0, send = call(
        basis0_kernel, [(2 * WB, 3 * R), (3 * WB, R), (2 * GROUPS, WB, 3 * R)], 1, far=(1,)
    )(sides[0], inv0, g0, w, w_sib)
    g1 = mirror_exchange(send, Z)
    w_sib = mirror(w, Z)
    t, t0 = call(targets_kernel, [(half, 3 * R), (half, R)], 1, far=(1,))(sides[0], inv0, g0, t, t_sib)
    t_sib = mirror(t, Z)

    inv1 = call(inverse_kernel, [(R, R)], 1)(sides[1], g1)
    cw, send = call(
        basis1_kernel, [(GROUPS, 5 * WB, R), (2 * GROUPS, 2 * WB, 2 * R)], 1, from_hbm=(5,)
    )(sides[1], inv1, g1, w, w_sib, cw0)
    g2 = exchange(send, ("x1", "cols"))
    t, t1 = call(targets_kernel, [(half, 2 * R), (half, R)], 1, far=(1,))(sides[1], inv1, g1, t, t_sib)
    t_sib = swap(t, "x1")

    inv2 = call(inverse_kernel, [(R, R)], 1)(sides[2], g2)
    a3, cw2 = call(last_basis_kernel, [(R, R), (R, R)], 1, far=(1,))(sides[2], inv2, g2)
    a3_sib = mirror(a3, X)
    cw = lax.all_to_all(cw, "cols", 0, 0, tiled=True)
    t, t2 = call(targets_kernel, [(half, R), (half, R)], 1, far=(1,))(sides[2], inv2, g2, t, t_sib)
    t_sib = mirror(t, X)

    inv3 = call(last_inverse_kernel, [(R, R)])(a3, a3_sib)
    k = call(total_kernel, [(half, wide)], from_hbm=(5, 6, 7, 8))(inv3, a3, a3_sib, t, t_sib, t0, t1, t2, cw2, cw)
    k_sib = swap(k, "core")
    return call(final_kernel, [(tgt, rows)], 2, [(GROUPS, LEVELS * WB, rows)], (0,), (2,), 24)(
        core, index("cols"), xt, wt, *parts, k, k_sib
    ).T


def solution(mesh):
    fine = Mesh(mesh.devices.reshape(2, 2, 2, 2, 2, 2, GROUPS), (*ROW_AXES, "cols"))
    placed = (P(ROW_AXES, "cols"), P(None, ROW_AXES, None), P(ROW_AXES, None))
    return jax.shard_map(sweep, mesh=fine, in_specs=placed, out_specs=P(ROW_AXES, "cols"), check_vma=False)
```

time: 227 us -> 195 us (0.86)
  Pallas kernels: 68.1 us -> 46.3 us
  local copies, waits for them, and re-layouts: 8.83 us -> 0 us
  waiting for transfers between devices: 35.6 us -> 40.2 us
  starting transfers between devices: 101 us -> 97.4 us
    pallas_call x14, Pallas kernels: 68.1 us -> 37.5 us  [run(): pl.pallas_call(kernel, out_shape=shapes[0] if single else shapes, in_spec...]
    pallas_call x0 -> x1, Pallas kernels: none -> 8.84 us  [sweep(): pl.pallas_call(project, out_shape=[pltpu.HBM((tgt, rows), F32)] + [pltpu....]
    unnamed x46 -> x0, local copies, waits for them, and re-layouts: 7.04 us -> none
    ppermute x4, waiting for transfers between devices: 2.92 us -> 5.51 us  [mirror(): return lax.ppermute(v, axes, [(i, n - 1 - i) for i in range(n)])]
  transfers between devices with their start and end apart: 21 -> 21, of which waited for: 8 -> 9; matrix products, arithmetic and copies ran while one was open for 1% -> 0% of each run, Pallas kernels for 22% -> 16%
where the time goes in v4:
time: 195 us; the launch traced here: 191 us
  starting transfers between devices  97.4 us (50%)
  Pallas kernels  46.3 us (24%)
  waiting for transfers between devices  40.2 us (21%)
  blocking collectives  6.32 us (3%)
    pallas_call x14, Pallas kernels, run(): pl.pallas_call(kernel, out_shape=shapes[0] if single else shapes, in_spec...  37.5 us
    ppermute x6, starting transfers between devices, swap(): return lax.ppermute(v, axis, [(0, 1), (1, 0)])  31.5 us
    ppermute x7, starting transfers between devices, sweep(): lax.ppermute(held[way], 'cols', [((y + way) % GROUPS, y) for y in range(G...  24 us
    ppermute x6, waiting for transfers between devices, swap(): return lax.ppermute(v, axis, [(0, 1), (1, 0)])  18.8 us
    ppermute x4, starting transfers between devices, mirror(): return lax.ppermute(v, axes, [(i, n - 1 - i) for i in range(n)])  13.8 us
    all_to_all x2, starting transfers between devices, exchange(): lax.all_to_all(v, axes, 0, 0, tiled=True).reshape(2, GROUPS, *v.shape[1:])  11.7 us
    all_to_all x1, starting transfers between devices, mirror_exchange(): lax.all_to_all(v, (*axes, 'cols'), 0, 0, tiled=True, axis_index_groups=pa...  11.5 us
    pallas_call x1, Pallas kernels, sweep(): pl.pallas_call(project, out_shape=[pltpu.HBM((tgt, rows), F32)] + [pltpu....  8.84 us
  transfers between devices with their start and end apart: 21, of which 9 were waited for; matrix products, arithmetic and copies ran while one was open for 0% of the time, Pallas kernels for 16%

profile of v4, /device:TPU:1, one launch (start us, length us, event | category | flops | bytes accessed | tf_op | source)
XLA Modules:
  0.0 190.8 jit_solution(2440887111233187213)
XLA Ops:
  0.0 8.8 %project.1 = (f32[320,1024]{1,0:T(8,128)}, f32[64,1024]{1,0:T(8,128)S(1)}, f32[4,16,512]{2,1,0:T(8,128)S(1)}, f32[208,512]{1,0:T(8,128)S(1)}, f32[208,512]{1,0:T(8,128)S(1)}) custom-call(s32[1]{0:T(128)} %bitcast.core_ref, s32[1,1024]{1,0:T(1,128)} %order_hbm.1, f32[1024,384]{1,0:T(8,128)} %x_hbm.1, f32[4,1024,128]{2,1,0:T(8,128)} %v_hbm.1), custom_call_target="tpu_custom_call" | custom-call | tf_op jit(solution)/shard_map/project/pallas_call | solution.py:327
  8.8 8.7 %collective-permute-start.7 = (f32[208,512]{1,0:T(8,128)S(1)}, f32[208,512]{1,0:T(8,128)S(1)}, u32[]{:S(2)}, u32[]{:S(2)}) collective-permute-start(f32[208,512]{1,0:T(8,128)S(1)} %get-tuple-element.30), channel_id=1, source_target_pairs={{0,8},{8,0},{1,9},{9,1},{2,10},{10,2},{3,11},{11,3},{4,12},{12,4},... | collective-permute-start | bytes 1277960 | tf_op jit(solution)/shard_map/ppermute | solution.py:290
  17.6 1.4 collective-permute-done.7
  19.0 0.1 add.3.q_ref
  19.0 6.3 %all_to_all.25.parts_ref = f32[4,16,512]{2,1,0:T(8,128)S(1)} all-to-all(f32[4,16,512]{2,1,0:T(8,128)S(1)} %get-tuple-element.31), channel_id=1, replica_groups=mesh['x2'=2,'x1'=2,'z4'=2,'z2'=2,'z1'=2,'core'=2,'cols'=8] {'z1','core'}, dimensions={0} | all-to-all | bytes 262144 | tf_op jit(solution)/shard_map/all_to_all | solution.py:345
  25.4 0.8 shard_map.37
  26.2 6.3 %all-to-all-start.1 = ((f32[16,16,512]{2,1,0:T(8,128)}), f32[16,16,512]{2,1,0:T(8,128)S(1)}, u32[]{:S(2)}, u32[]{:S(2)}) async-start(f32[16,16,512]{2,1,0:T(8,128)} %shard_map.37), calls=%async_computation.1 | async-start | bytes 1048576 | tf_op jit(solution)/shard_map/all_to_all | solution.py:299
  32.5 2.5 %collective-permute-start.8 = (f32[208,512]{1,0:T(8,128)S(1)}, f32[208,512]{1,0:T(8,128)S(1)}, u32[]{:S(2)}, u32[]{:S(2)}) collective-permute-start(f32[208,512]{1,0:T(8,128)S(1)} %add.3.q_ref), channel_id=1, source_target_pairs={{0,16},{16,0},{1,17},{17,1},{2,18},{18,2},{3,19},{19,3},{4,20},{20... | collective-permute-start | bytes 1277960 | tf_op jit(solution)/shard_map/ppermute | solution.py:290
  35.0 15.2 %collective-permute-done.8.moved_ref = f32[208,512]{1,0:T(8,128)S(1)} collective-permute-done((f32[208,512]{1,0:T(8,128)S(1)}, f32[208,512]{1,0:T(8,128)S(1)}, u32[]{:S(2)}, u32[]{:S(2)}) %collective-permute-start.8) | collective-permute-done | bytes 426016 | tf_op jit(solution)/shard_map/ppermute | solution.py:290
  50.2 3.0 %collective-permute-start.9 = (f32[48,512]{1,0:T(8,128)S(1)}, f32[48,512]{1,0:T(8,128)S(1)}, u32[]{:S(2)}, u32[]{:S(2)}) collective-permute-start(f32[48,512]{1,0:T(8,128)S(1)} %get-tuple-element.32.w_own_ref), channel_id=1, source_target_pairs={{0,32},{32,0},{1,33},{33,1},{2,34},{34,2},{3,35},{35,3},{4,36},{36... | collective-permute-start | bytes 294920 | tf_op jit(solution)/shard_map/ppermute | solution.py:290
  53.2 0.0 all-to-all-done.1
  53.2 6.0 %shard_map.38.inv_ref = f32[128,128]{1,0:T(8,128)S(1)} custom-call(s32[1]{0:T(128)} %bitcast.4.side_ref, f32[2,8,16,512]{3,2,1,0:T(8,128)S(1)} %bitcast.9), custom_call_target="tpu_custom_call" | custom-call | tf_op jit(solution)/shard_map/pallas_call | solution.py:276
  59.2 0.0 collective-permute-done.9.w_sib_ref
  59.2 1.7 shard_map.40
  60.9 11.5 %all-to-all-start.2 = ((f32[16,16,384]{2,1,0:T(8,128)}), f32[16,16,384]{2,1,0:T(8,128)S(1)}, u32[]{:S(2)}, u32[]{:S(2)}) async-start(f32[16,16,384]{2,1,0:T(8,128)} %get-tuple-element.33), calls=%async_computation.2 | async-start | bytes 786432 | tf_op jit(solution)/shard_map/all_to_all | solution.py:305
  72.4 4.7 %collective-permute-start.10 = (f32[32,384]{1,0:T(8,128)S(1)}, f32[32,384]{1,0:T(8,128)S(1)}, u32[]{:S(2)}, u32[]{:S(2)}) collective-permute-start(f32[32,384]{1,0:T(8,128)S(1)} %get-tuple-element.34.w_own_ref), channel_id=1, source_target_pairs={{0,112},{16,96},{32,80},{48,64},{64,48},{80,32},{96,16},{112,0},{1... | collective-permute-start | bytes 147464 | tf_op jit(solution)/shard_map/ppermute | solution.py:295
  77.1 8.3 %all-to-all-done.2 = f32[16,16,384]{2,1,0:T(8,128)S(1)} async-done(((f32[16,16,384]{2,1,0:T(8,128)}), f32[16,16,384]{2,1,0:T(8,128)S(1)}, u32[]{:S(2)}, u32[]{:S(2)}) %all-to-all-start.2) | async-done | bytes 393248 | tf_op jit(solution)/shard_map/all_to_all | solution.py:305
  85.4 6.0 %shard_map.41.inv_ref = f32[128,128]{1,0:T(8,128)S(1)} custom-call(s32[1]{0:T(128)} %bitcast.3.side_ref, f32[2,8,16,384]{3,2,1,0:T(8,128)S(1)} %bitcast.15), custom_call_target="tpu_custom_call" | custom-call | tf_op jit(solution)/shard_map/pallas_call | solution.py:276
  91.3 0.0 collective-permute-done.10.w_sib_ref
  91.3 1.7 shard_map.42
  93.0 5.5 %all-to-all-start.3 = ((f32[16,32,256]{2,1,0:T(8,128)}), f32[16,32,256]{2,1,0:T(8,128)S(1)}, u32[]{:S(2)}, u32[]{:S(2)}) async-start(f32[16,32,256]{2,1,0:T(8,128)} %get-tuple-element.36), calls=%async_computation.3 | async-start | bytes 1048576 | tf_op jit(solution)/shard_map/all_to_all | solution.py:299
  98.5 4.8 %collective-permute-start.12 = (f32[160,512]{1,0:T(8,128)S(1)}, f32[160,512]{1,0:T(8,128)S(1)}, u32[]{:S(2)}, u32[]{:S(2)}) collective-permute-start(f32[160,512]{1,0:T(8,128)S(1)} %get-tuple-element.38.t_own_ref), channel_id=1, source_target_pairs={{0,32},{32,0},{1,33},{33,1},{2,34},{34,2},{3,35},{35,3},{4,36},{36... | collective-permute-start | bytes 983048 | tf_op jit(solution)/shard_map/ppermute | solution.py:290
  103.3 4.5 %collective-permute-start = (f32[64,1024]{1,0:T(8,128)S(1)}, f32[64,1024]{1,0:T(8,128)S(1)}, u32[]{:S(2)}, u32[]{:S(2)}) collective-permute-start(f32[64,1024]{1,0:T(8,128)S(1)} %get-tuple-element.27.wt_ref), channel_id=1, source_target_pairs={{1,0},{2,1},{3,2},{4,3},{5,4},{6,5},{7,6},{0,7},{9,8},{10,9},{11,1... | collective-permute-start | bytes 786440 | tf_op jit(solution)/shard_map/ppermute | solution.py:356
  107.8 2.2 %all-to-all-done.3 = f32[16,32,256]{2,1,0:T(8,128)S(1)} async-done(((f32[16,32,256]{2,1,0:T(8,128)}), f32[16,32,256]{2,1,0:T(8,128)S(1)}, u32[]{:S(2)}, u32[]{:S(2)}) %all-to-all-start.3) | async-done | bytes 524320 | tf_op jit(solution)/shard_map/all_to_all | solution.py:299
  109.9 4.8 %all-to-all-start.4 = ((f32[8,80,128]{2,1,0:T(8,128)}), f32[8,80,128]{2,1,0:T(8,128)S(1)}, u32[]{:S(2)}, u32[]{:S(2)}) async-start(f32[8,80,128]{2,1,0:T(8,128)} %get-tuple-element.46), calls=%async_computation.4 | async-start | bytes 655360 | tf_op jit(solution)/shard_map/all_to_all | solution.py:379
  114.8 2.3 %collective-permute-done.12.t_sib_ref = f32[160,512]{1,0:T(8,128)S(1)} collective-permute-done((f32[160,512]{1,0:T(8,128)S(1)}, f32[160,512]{1,0:T(8,128)S(1)}, u32[]{:S(2)}, u32[]{:S(2)}) %collective-permute-start.12) | collective-permute-done | bytes 327712 | tf_op jit(solution)/shard_map/ppermute | solution.py:290
  117.1 1.2 shard_map.46
  118.3 2.4 %collective-permute-start.13 = (f32[160,384]{1,0:T(8,128)S(1)}, f32[160,384]{1,0:T(8,128)S(1)}, u32[]{:S(2)}, u32[]{:S(2)}) collective-permute-start(f32[160,384]{1,0:T(8,128)S(1)} %get-tuple-element.39.t_own_ref), channel_id=1, source_target_pairs={{0,112},{16,96},{32,80},{48,64},{64,48},{80,32},{96,16},{112,0},{1... | collective-permute-start | bytes 737288 | tf_op jit(solution)/shard_map/ppermute | solution.py:295
  120.7 3.4 %collective-permute-start.1 = (f32[64,1024]{1,0:T(8,128)S(1)}, f32[64,1024]{1,0:T(8,128)S(1)}, u32[]{:S(2)}, u32[]{:S(2)}) collective-permute-start(f32[64,1024]{1,0:T(8,128)S(1)} %get-tuple-element.27.wt_ref), channel_id=1, source_target_pairs={{7,0},{0,1},{1,2},{2,3},{3,4},{4,5},{5,6},{6,7},{15,8},{8,9},{9,10... | collective-permute-start | bytes 786440 | tf_op jit(solution)/shard_map/ppermute | solution.py:356
  124.1 0.0 collective-permute-done.refs_0_
  124.1 3.1 %collective-permute-start.2 = (f32[64,1024]{1,0:T(8,128)S(1)}, f32[64,1024]{1,0:T(8,128)S(1)}, u32[]{:S(2)}, u32[]{:S(2)}) collective-permute-start(f32[64,1024]{1,0:T(8,128)S(1)} %collective-permute-done.refs_0_), channel_id=1, source_target_pairs={{1,0},{2,1},{3,2},{4,3},{5,4},{6,5},{7,6},{0,7},{9,8},{10,9},{11,1... | collective-permute-start | bytes 786440 | tf_op jit(solution)/shard_map/ppermute | solution.py:356
  127.3 2.8 %collective-permute-done.13.t_sib_ref = f32[160,384]{1,0:T(8,128)S(1)} collective-permute-done((f32[160,384]{1,0:T(8,128)S(1)}, f32[160,384]{1,0:T(8,128)S(1)}, u32[]{:S(2)}, u32[]{:S(2)}) %collective-permute-start.13) | collective-permute-done | bytes 245792 | tf_op jit(solution)/shard_map/ppermute | solution.py:295
  130.0 1.0 shard_map.47
  131.1 3.3 %collective-permute-start.14 = (f32[160,256]{1,0:T(8,128)S(1)}, f32[160,256]{1,0:T(8,128)S(1)}, u32[]{:S(2)}, u32[]{:S(2)}) collective-permute-start(f32[160,256]{1,0:T(8,128)S(1)} %get-tuple-element.40.t_own_ref), channel_id=1, source_target_pairs={{0,128},{128,0},{1,129},{129,1},{2,130},{130,2},{3,131},{131,3},{4... | collective-permute-start | bytes 491528 | tf_op jit(solution)/shard_map/ppermute | solution.py:290
  134.4 0.0 collective-permute-done.1.refs_1_
  134.4 2.8 %collective-permute-start.3 = (f32[64,1024]{1,0:T(8,128)S(1)}, f32[64,1024]{1,0:T(8,128)S(1)}, u32[]{:S(2)}, u32[]{:S(2)}) collective-permute-start(f32[64,1024]{1,0:T(8,128)S(1)} %collective-permute-done.1.refs_1_), channel_id=1, source_target_pairs={{7,0},{0,1},{1,2},{2,3},{3,4},{4,5},{5,6},{6,7},{15,8},{8,9},{9,10... | collective-permute-start | bytes 786440 | tf_op jit(solution)/shard_map/ppermute | solution.py:356
  137.2 0.0 collective-permute-done.2.refs_2_
  137.3 3.7 %collective-permute-start.4 = (f32[64,1024]{1,0:T(8,128)S(1)}, f32[64,1024]{1,0:T(8,128)S(1)}, u32[]{:S(2)}, u32[]{:S(2)}) collective-permute-start(f32[64,1024]{1,0:T(8,128)S(1)} %collective-permute-done.2.refs_2_), channel_id=1, source_target_pairs={{1,0},{2,1},{3,2},{4,3},{5,4},{6,5},{7,6},{0,7},{9,8},{10,9},{11,1... | collective-permute-start | bytes 786440 | tf_op jit(solution)/shard_map/ppermute | solution.py:356
  140.9 6.0 %shard_map.43.inv_ref = f32[128,128]{1,0:T(8,128)S(1)} custom-call(s32[1]{0:T(128)} %bitcast.2.side_ref, f32[2,8,32,256]{3,2,1,0:T(8,128)S(1)} %bitcast.12), custom_call_target="tpu_custom_call" | custom-call | tf_op jit(solution)/shard_map/pallas_call | solution.py:276
  146.9 0.0 collective-permute-done.14.t_sib_ref
  146.9 1.0 shard_map.48
  147.9 3.2 %collective-permute-start.15 = (f32[160,128]{1,0:T(8,128)S(1)}, f32[160,128]{1,0:T(8,128)S(1)}, u32[]{:S(2)}, u32[]{:S(2)}) collective-permute-start(f32[160,128]{1,0:T(8,128)S(1)} %get-tuple-element.41.t_own_ref), channel_id=1, source_target_pairs={{0,384},{128,256},{256,128},{384,0},{1,385},{129,257},{257,129},{3... | collective-permute-start | bytes 245768 | tf_op jit(solution)/shard_map/ppermute | solution.py:295
  151.2 1.0 shard_map.44
  152.2 3.5 %collective-permute-start.11 = (f32[128,128]{1,0:T(8,128)S(1)}, f32[128,128]{1,0:T(8,128)S(1)}, u32[]{:S(2)}, u32[]{:S(2)}) collective-permute-start(f32[128,128]{1,0:T(8,128)S(1)} %get-tuple-element.37.own_ref.a_own_ref), channel_id=1, source_target_pairs={{0,384},{128,256},{256,128},{384,0},{1,385},{129,257},{257,129},{3... | collective-permute-start | bytes 196616 | tf_op jit(solution)/shard_map/ppermute | solution.py:295
  155.7 2.7 %collective-permute-done.11.sib_ref.a_sib_ref = f32[128,128]{1,0:T(8,128)S(1)} collective-permute-done((f32[128,128]{1,0:T(8,128)S(1)}, f32[128,128]{1,0:T(8,128)S(1)}, u32[]{:S(2)}, u32[]{:S(2)}) %collective-permute-start.11) | collective-permute-done | bytes 65568 | tf_op jit(solution)/shard_map/ppermute | solution.py:295
  158.4 6.0 %shard_map.45.inv_ref = f32[128,128]{1,0:T(8,128)S(1)} custom-call(f32[128,128]{1,0:T(8,128)S(1)} %get-tuple-element.37.own_ref.a_own_ref, f32[128,128]{1,0:T(8,128)S(1)} %collective-permute-done.11.sib_ref.a_sib_ref), custom_call_target="tpu_custom_call" | custom-call | tf_op jit(solution)/shard_map/pallas_call | solution.py:276
  164.4 0.0 all-to-all-done.4.refs_4_
  164.4 0.0 collective-permute-done.15.t_sib_ref
  164.4 1.9 %shard_map.49.refs_7_ = f32[160,512]{1,0:T(8,128)S(1)} custom-call(f32[128,128]{1,0:T(8,128)S(1)} %shard_map.45.inv_ref, f32[128,128]{1,0:T(8,128)S(1)} %get-tuple-element.37.own_ref.a_own_ref, f32[128,128]{1,0:T(8,128)S(1)} %collective-permute-done.11.sib_ref.a_sib_ref, f32[160,128]{1,0:T(8,128)S(1)} %get-tuple-element.41.t_own_ref, ...), custom_call_target="tpu_custom_call" | custom-call | tf_op jit(solution)/shard_map/pallas_call | solution.py:276
  166.3 9.2 %collective-permute-start.16 = (f32[160,512]{1,0:T(8,128)S(1)}, f32[160,512]{1,0:T(8,128)S(1)}, u32[]{:S(2)}, u32[]{:S(2)}) collective-permute-start(f32[160,512]{1,0:T(8,128)S(1)} %shard_map.49.refs_7_), channel_id=1, source_target_pairs={{0,8},{8,0},{1,9},{9,1},{2,10},{10,2},{3,11},{11,3},{4,12},{12,4},... | collective-permute-start | bytes 983048 | tf_op jit(solution)/shard_map/ppermute | solution.py:290
  175.5 0.0 collective-permute-done.3.refs_3_
  175.5 2.1 %collective-permute-start.5 = (f32[64,1024]{1,0:T(8,128)S(1)}, f32[64,1024]{1,0:T(8,128)S(1)}, u32[]{:S(2)}, u32[]{:S(2)}) collective-permute-start(f32[64,1024]{1,0:T(8,128)S(1)} %collective-permute-done.3.refs_3_), channel_id=1, source_target_pairs={{7,0},{0,1},{1,2},{2,3},{3,4},{4,5},{5,6},{6,7},{15,8},{8,9},{9,10... | collective-permute-start | bytes 786440 | tf_op jit(solution)/shard_map/ppermute | solution.py:356
  177.5 0.0 collective-permute-done.4.refs_4_
  177.6 4.4 %collective-permute-start.6 = (f32[64,1024]{1,0:T(8,128)S(1)}, f32[64,1024]{1,0:T(8,128)S(1)}, u32[]{:S(2)}, u32[]{:S(2)}) collective-permute-start(f32[64,1024]{1,0:T(8,128)S(1)} %collective-permute-done.4.refs_4_), channel_id=1, source_target_pairs={{1,0},{2,1},{3,2},{4,3},{5,4},{6,5},{7,6},{0,7},{9,8},{10,9},{11,1... | collective-permute-start | bytes 786440 | tf_op jit(solution)/shard_map/ppermute | solution.py:356
  182.0 4.4 %collective-permute-done.5.refs_5_ = f32[64,1024]{1,0:T(8,128)S(1)} collective-permute-done((f32[64,1024]{1,0:T(8,128)S(1)}, f32[64,1024]{1,0:T(8,128)S(1)}, u32[]{:S(2)}, u32[]{:S(2)}) %collective-permute-start.5) | collective-permute-done | bytes 262176 | tf_op jit(solution)/shard_map/ppermute | solution.py:356
  186.4 0.9 collective-permute-done.6.refs_6_
  187.3 0.0 collective-permute-done.16.refs_8_
  187.4 3.2 %shard_map.50 = f32[320,1024]{1,0:T(8,128)} custom-call(s32[1]{0:T(128)} %bitcast.core_ref, s32[1]{0:T(128)} %bitcast.1.col_ref, f32[320,1024]{1,0:T(8,128)} %get-tuple-element.26.xt_ref, f32[64,1024]{1,0:T(8,128)S(1)} %get-tuple-element.27.wt_ref, f32[64,1024]{1,0:T(8,128)S(1)} %collective-permute-done.refs_0_, ...), custom_call_target="tpu_custom_call" | custom-call | tf_op jit(solution)/shard_map/pallas_call | solution.py:276
  (1 shorter events, 0.0 us)
Async XLA Ops:
  8.8 10.1 %collective-permute-start.7 = (f32[208,512]{1,0:T(8,128)S(1)}, f32[208,512]{1,0:T(8,128)S(1)}, u32[]{:S(2)}, u32[]{:S(2)}) collective-permute-start(f32[208,512]{1,0:T(8,128)S(1)} %get-tuple-element.30), channel_id=1, source_target_pairs={{0,8},{8,0},{1,9},{9,1},{2,10},{10,2},{3,11},{11,3},{4,12},{12,4},... | collective-permute-start | bytes 1277960 | tf_op jit(solution)/shard_map/ppermute | solution.py:290
  26.2 27.0 %all-to-all-start.1 = ((f32[16,16,512]{2,1,0:T(8,128)}), f32[16,16,512]{2,1,0:T(8,128)S(1)}, u32[]{:S(2)}, u32[]{:S(2)}) async-start(f32[16,16,512]{2,1,0:T(8,128)} %shard_map.37), calls=%async_computation.1 | async-start | bytes 1048576 | tf_op jit(solution)/shard_map/all_to_all | solution.py:299
  32.5 17.7 %collective-permute-start.8 = (f32[208,512]{1,0:T(8,128)S(1)}, f32[208,512]{1,0:T(8,128)S(1)}, u32[]{:S(2)}, u32[]{:S(2)}) collective-permute-start(f32[208,512]{1,0:T(8,128)S(1)} %add.3.q_ref), channel_id=1, source_target_pairs={{0,16},{16,0},{1,17},{17,1},{2,18},{18,2},{3,19},{19,3},{4,20},{20... | collective-permute-start | bytes 1277960 | tf_op jit(solution)/shard_map/ppermute | solution.py:290
  50.2 9.0 %collective-permute-start.9 = (f32[48,512]{1,0:T(8,128)S(1)}, f32[48,512]{1,0:T(8,128)S(1)}, u32[]{:S(2)}, u32[]{:S(2)}) collective-permute-start(f32[48,512]{1,0:T(8,128)S(1)} %get-tuple-element.32.w_own_ref), channel_id=1, source_target_pairs={{0,32},{32,0},{1,33},{33,1},{2,34},{34,2},{3,35},{35,3},{4,36},{36... | collective-permute-start | bytes 294920 | tf_op jit(solution)/shard_map/ppermute | solution.py:290
  60.9 24.5 %all-to-all-start.2 = ((f32[16,16,384]{2,1,0:T(8,128)}), f32[16,16,384]{2,1,0:T(8,128)S(1)}, u32[]{:S(2)}, u32[]{:S(2)}) async-start(f32[16,16,384]{2,1,0:T(8,128)} %get-tuple-element.33), calls=%async_computation.2 | async-start | bytes 786432 | tf_op jit(solution)/shard_map/all_to_all | solution.py:305
  72.4 18.9 %collective-permute-start.10 = (f32[32,384]{1,0:T(8,128)S(1)}, f32[32,384]{1,0:T(8,128)S(1)}, u32[]{:S(2)}, u32[]{:S(2)}) collective-permute-start(f32[32,384]{1,0:T(8,128)S(1)} %get-tuple-element.34.w_own_ref), channel_id=1, source_target_pairs={{0,112},{16,96},{32,80},{48,64},{64,48},{80,32},{96,16},{112,0},{1... | collective-permute-start | bytes 147464 | tf_op jit(solution)/shard_map/ppermute | solution.py:295
  93.0 16.9 %all-to-all-start.3 = ((f32[16,32,256]{2,1,0:T(8,128)}), f32[16,32,256]{2,1,0:T(8,128)S(1)}, u32[]{:S(2)}, u32[]{:S(2)}) async-start(f32[16,32,256]{2,1,0:T(8,128)} %get-tuple-element.36), calls=%async_computation.3 | async-start | bytes 1048576 | tf_op jit(solution)/shard_map/all_to_all | solution.py:299
  98.5 18.6 %collective-permute-start.12 = (f32[160,512]{1,0:T(8,128)S(1)}, f32[160,512]{1,0:T(8,128)S(1)}, u32[]{:S(2)}, u32[]{:S(2)}) collective-permute-start(f32[160,512]{1,0:T(8,128)S(1)} %get-tuple-element.38.t_own_ref), channel_id=1, source_target_pairs={{0,32},{32,0},{1,33},{33,1},{2,34},{34,2},{3,35},{35,3},{4,36},{36... | collective-permute-start | bytes 983048 | tf_op jit(solution)/shard_map/ppermute | solution.py:290
  103.3 20.8 %collective-permute-start = (f32[64,1024]{1,0:T(8,128)S(1)}, f32[64,1024]{1,0:T(8,128)S(1)}, u32[]{:S(2)}, u32[]{:S(2)}) collective-permute-start(f32[64,1024]{1,0:T(8,128)S(1)} %get-tuple-element.27.wt_ref), channel_id=1, source_target_pairs={{1,0},{2,1},{3,2},{4,3},{5,4},{6,5},{7,6},{0,7},{9,8},{10,9},{11,1... | collective-permute-start | bytes 786440 | tf_op jit(solution)/shard_map/ppermute | solution.py:356
  109.9 54.4 %all-to-all-start.4 = ((f32[8,80,128]{2,1,0:T(8,128)}), f32[8,80,128]{2,1,0:T(8,128)S(1)}, u32[]{:S(2)}, u32[]{:S(2)}) async-start(f32[8,80,128]{2,1,0:T(8,128)} %get-tuple-element.46), calls=%async_computation.4 | async-start | bytes 655360 | tf_op jit(solution)/shard_map/all_to_all | solution.py:379
  118.3 11.7 %collective-permute-start.13 = (f32[160,384]{1,0:T(8,128)S(1)}, f32[160,384]{1,0:T(8,128)S(1)}, u32[]{:S(2)}, u32[]{:S(2)}) collective-permute-start(f32[160,384]{1,0:T(8,128)S(1)} %get-tuple-element.39.t_own_ref), channel_id=1, source_target_pairs={{0,112},{16,96},{32,80},{48,64},{64,48},{80,32},{96,16},{112,0},{1... | collective-permute-start | bytes 737288 | tf_op jit(solution)/shard_map/ppermute | solution.py:295
  120.7 13.7 %collective-permute-start.1 = (f32[64,1024]{1,0:T(8,128)S(1)}, f32[64,1024]{1,0:T(8,128)S(1)}, u32[]{:S(2)}, u32[]{:S(2)}) collective-permute-start(f32[64,1024]{1,0:T(8,128)S(1)} %get-tuple-element.27.wt_ref), channel_id=1, source_target_pairs={{7,0},{0,1},{1,2},{2,3},{3,4},{4,5},{5,6},{6,7},{15,8},{8,9},{9,10... | collective-permute-start | bytes 786440 | tf_op jit(solution)/shard_map/ppermute | solution.py:356
  124.1 13.1 %collective-permute-start.2 = (f32[64,1024]{1,0:T(8,128)S(1)}, f32[64,1024]{1,0:T(8,128)S(1)}, u32[]{:S(2)}, u32[]{:S(2)}) collective-permute-start(f32[64,1024]{1,0:T(8,128)S(1)} %collective-permute-done.refs_0_), channel_id=1, source_target_pairs={{1,0},{2,1},{3,2},{4,3},{5,4},{6,5},{7,6},{0,7},{9,8},{10,9},{11,1... | collective-permute-start | bytes 786440 | tf_op jit(solution)/shard_map/ppermute | solution.py:356
  131.1 15.9 %collective-permute-start.14 = (f32[160,256]{1,0:T(8,128)S(1)}, f32[160,256]{1,0:T(8,128)S(1)}, u32[]{:S(2)}, u32[]{:S(2)}) collective-permute-start(f32[160,256]{1,0:T(8,128)S(1)} %get-tuple-element.40.t_own_ref), channel_id=1, source_target_pairs={{0,128},{128,0},{1,129},{129,1},{2,130},{130,2},{3,131},{131,3},{4... | collective-permute-start | bytes 491528 | tf_op jit(solution)/shard_map/ppermute | solution.py:290
  134.4 41.1 %collective-permute-start.3 = (f32[64,1024]{1,0:T(8,128)S(1)}, f32[64,1024]{1,0:T(8,128)S(1)}, u32[]{:S(2)}, u32[]{:S(2)}) collective-permute-start(f32[64,1024]{1,0:T(8,128)S(1)} %collective-permute-done.1.refs_1_), channel_id=1, source_target_pairs={{7,0},{0,1},{1,2},{2,3},{3,4},{4,5},{5,6},{6,7},{15,8},{8,9},{9,10... | collective-permute-start | bytes 786440 | tf_op jit(solution)/shard_map/ppermute | solution.py:356
  137.3 40.3 %collective-permute-start.4 = (f32[64,1024]{1,0:T(8,128)S(1)}, f32[64,1024]{1,0:T(8,128)S(1)}, u32[]{:S(2)}, u32[]{:S(2)}) collective-permute-start(f32[64,1024]{1,0:T(8,128)S(1)} %collective-permute-done.2.refs_2_), channel_id=1, source_target_pairs={{1,0},{2,1},{3,2},{4,3},{5,4},{6,5},{7,6},{0,7},{9,8},{10,9},{11,1... | collective-permute-start | bytes 786440 | tf_op jit(solution)/shard_map/ppermute | solution.py:356
  147.9 16.4 %collective-permute-start.15 = (f32[160,128]{1,0:T(8,128)S(1)}, f32[160,128]{1,0:T(8,128)S(1)}, u32[]{:S(2)}, u32[]{:S(2)}) collective-permute-start(f32[160,128]{1,0:T(8,128)S(1)} %get-tuple-element.41.t_own_ref), channel_id=1, source_target_pairs={{0,384},{128,256},{256,128},{384,0},{1,385},{129,257},{257,129},{3... | collective-permute-start | bytes 245768 | tf_op jit(solution)/shard_map/ppermute | solution.py:295
  152.2 6.2 %collective-permute-start.11 = (f32[128,128]{1,0:T(8,128)S(1)}, f32[128,128]{1,0:T(8,128)S(1)}, u32[]{:S(2)}, u32[]{:S(2)}) collective-permute-start(f32[128,128]{1,0:T(8,128)S(1)} %get-tuple-element.37.own_ref.a_own_ref), channel_id=1, source_target_pairs={{0,384},{128,256},{256,128},{384,0},{1,385},{129,257},{257,129},{3... | collective-permute-start | bytes 196616 | tf_op jit(solution)/shard_map/ppermute | solution.py:295
  166.3 21.0 %collective-permute-start.16 = (f32[160,512]{1,0:T(8,128)S(1)}, f32[160,512]{1,0:T(8,128)S(1)}, u32[]{:S(2)}, u32[]{:S(2)}) collective-permute-start(f32[160,512]{1,0:T(8,128)S(1)} %shard_map.49.refs_7_), channel_id=1, source_target_pairs={{0,8},{8,0},{1,9},{9,1},{2,10},{10,2},{3,11},{11,3},{4,12},{12,4},... | collective-permute-start | bytes 983048 | tf_op jit(solution)/shard_map/ppermute | solution.py:290
  175.5 11.0 %collective-permute-start.5 = (f32[64,1024]{1,0:T(8,128)S(1)}, f32[64,1024]{1,0:T(8,128)S(1)}, u32[]{:S(2)}, u32[]{:S(2)}) collective-permute-start(f32[64,1024]{1,0:T(8,128)S(1)} %collective-permute-done.3.refs_3_), channel_id=1, source_target_pairs={{7,0},{0,1},{1,2},{2,3},{3,4},{4,5},{5,6},{6,7},{15,8},{8,9},{9,10... | collective-permute-start | bytes 786440 | tf_op jit(solution)/shard_map/ppermute | solution.py:356
  177.6 9.8 %collective-permute-start.6 = (f32[64,1024]{1,0:T(8,128)S(1)}, f32[64,1024]{1,0:T(8,128)S(1)}, u32[]{:S(2)}, u32[]{:S(2)}) collective-permute-start(f32[64,1024]{1,0:T(8,128)S(1)} %collective-permute-done.4.refs_4_), channel_id=1, source_target_pairs={{1,0},{2,1},{3,2},{4,3},{5,4},{6,5},{7,6},{0,7},{9,8},{10,9},{11,1... | collective-permute-start | bytes 786440 | tf_op jit(solution)/shard_map/ppermute | solution.py:356

commit v5 on v4

--- a/solution.py
+++ b/solution.py
@@ -13,7 +13,6 @@
 LEVELS = 4
 WB = 16
 GROUPS = 8
-RING = (1, -1, 2, -2, 3, -3, 4)
 ROW_AXES = ("x2", "x1", "z4", "z2", "z1", "core")
 HIGH = lax.Precision.HIGHEST
 F32 = jnp.float32
@@ -209,6 +208,13 @@
     out.wait()
 
 
+def pair_kernel(own_ref, up_ref, down_ref, up_pair_ref, down_pair_ref):
+    share = own_ref.shape[0]
+    for pair_ref, next_ref in ((up_pair_ref, up_ref), (down_pair_ref, down_ref)):
+        pair_ref[:share] = own_ref[...]
+        pair_ref[share:] = next_ref[...]
+
+
 def split_sum_kernel(q_ref, moved_ref, t_ref, w_ref):
     half = t_ref.shape[0]
     t_ref[...] = q_ref[:half] + moved_ref[:half]
@@ -237,14 +243,16 @@
 
 
 def final_kernel(core_ref, col_ref, xt_ref, wt_ref, *refs):
-    part_refs, (k_own_ref, k_sib_ref, out_hbm, w_ref, out_ref, near_ref, sems) = refs[: GROUPS - 1], refs[GROUPS - 1 :]
+    part_refs, (k_own_ref, k_sib_ref, out_hbm, w_ref, out_ref, near_ref, sems) = refs[:5], refs[5:]
     near = pltpu.make_async_copy(xt_ref, near_ref, sems.at[1])
     near.start()
     tgt, rows = out_ref.shape
     core, col = core_ref[0], col_ref[0]
     w_ref[col] = wt_ref[...]
-    for shift, part_ref in zip(RING, part_refs):
-        w_ref[lax.rem(col + (shift + GROUPS), GROUPS)] = part_ref[...]
+    share = wt_ref.shape[0]
+    for shifts, part_ref in zip(((1,), (-1,), (2, 3), (-2, -3), (4,)), part_refs):
+        for i, shift in enumerate(shifts):
+            w_ref[lax.rem(col + (shift + GROUPS), GROUPS)] = part_ref[i * share : i * share + share]
     own, sib = k_own_ref[...], k_sib_ref[...]
     k = halves(jnp.concatenate([jnp.where(core == 0, own, sib), jnp.where(core == 0, sib, own)], axis=0))
     at = [(LEVELS - 1 - level) * WB for level in range(LEVELS)]
@@ -350,11 +358,14 @@
     w_sib = swap(w, "z2")
     t_sib = swap(t, "z2")
 
-    parts, held = [], {1: wt, -1: wt}
-    for shift in RING:
-        way = 1 if shift > 0 else -1
-        held[way] = lax.ppermute(held[way], "cols", [((y + way) % GROUPS, y) for y in range(GROUPS)])
-        parts.append(held[way])
+    def ring(v, shift):
+        return lax.ppermute(v, "cols", [((y + shift) % GROUPS, y) for y in range(GROUPS)])
+
+    up, down = ring(wt, 1), ring(wt, -1)
+    share = LEVELS * WB
+    pairs = call(pair_kernel, [(2 * share, rows), (2 * share, rows)])(wt, up, down)
+    up2, down2 = ring(pairs[0], 2), ring(pairs[1], -2)
+    parts = (up, down, up2, down2, ring(up2[share:], 1))
 
     inv0 = call(inverse_kernel, [(R, R)], 1)(sides[0], g0)
     w, cw0, send = call(

time: 195 us -> 189 us (0.969); the launches traced: 191 us -> 187 us
  starting transfers between devices: 97.4 us -> 94.1 us
  waiting for transfers between devices: 40.2 us -> 37.6 us
  Pallas kernels: 46.3 us -> 48.4 us
    ppermute x7 -> x5, starting transfers between devices: 24 us -> 19.1 us  [ring(): lax.ppermute(v, 'cols', [((y + shift) % GROUPS, y) for y in range(GROUPS)])]
    pallas_call x14 -> x15, Pallas kernels: 37.5 us -> 39.6 us  [run(): pl.pallas_call(kernel, out_shape=shapes[0] if single else shapes, in_spec...]
    all_to_all x2, waiting for transfers between devices: 2.16 us -> 0.13 us  [exchange(): lax.all_to_all(v, axes, 0, 0, tiled=True).reshape(2, GROUPS, *v.shape[1:])]
    ppermute x7 -> x5, waiting for transfers between devices: 5.36 us -> 6.33 us  [ring(): lax.ppermute(v, 'cols', [((y + shift) % GROUPS, y) for y in range(GROUPS)])]
  transfers between devices with their start and end apart: 21 -> 19, of which waited for: 9 -> 8; matrix products, arithmetic and copies ran while one was open for 0% -> 0% of each run, Pallas kernels for 16% -> 17%
where the time goes in v5:
time: 189 us; the launch traced here: 187 us
  starting transfers between devices  94.1 us (50%)
  Pallas kernels  48.4 us (26%)
  waiting for transfers between devices  37.6 us (20%)
  blocking collectives  6.32 us (3%)
    pallas_call x15, Pallas kernels, run(): pl.pallas_call(kernel, out_shape=shapes[0] if single else shapes, in_spec...  39.6 us
    ppermute x6, starting transfers between devices, swap(): return lax.ppermute(v, axis, [(0, 1), (1, 0)])  31.6 us
    ppermute x5, starting transfers between devices, ring(): lax.ppermute(v, 'cols', [((y + shift) % GROUPS, y) for y in range(GROUPS)])  19.1 us
    ppermute x6, waiting for transfers between devices, swap(): return lax.ppermute(v, axis, [(0, 1), (1, 0)])  17.2 us
    ppermute x4, starting transfers between devices, mirror(): return lax.ppermute(v, axes, [(i, n - 1 - i) for i in range(n)])  13.8 us
    all_to_all x2, starting transfers between devices, exchange(): lax.all_to_all(v, axes, 0, 0, tiled=True).reshape(2, GROUPS, *v.shape[1:])  11.7 us
    all_to_all x1, starting transfers between devices, mirror_exchange(): lax.all_to_all(v, (*axes, 'cols'), 0, 0, tiled=True, axis_index_groups=pa...  11.5 us
    pallas_call x1, Pallas kernels, sweep(): pl.pallas_call(project, out_shape=[pltpu.HBM((tgt, rows), F32)] + [pltpu....  8.84 us
  transfers between devices with their start and end apart: 19, of which 8 were waited for; matrix products, arithmetic and copies ran while one was open for 0% of the time, Pallas kernels for 17%

profile of v5, /device:TPU:1, one launch (start us, length us, event | category | flops | bytes accessed | tf_op | source)
XLA Modules:
  0.0 187.1 jit_solution(4556877154630233232)
XLA Ops:
  0.0 8.8 %project.1 = (f32[320,1024]{1,0:T(8,128)}, f32[64,1024]{1,0:T(8,128)S(1)}, f32[4,16,512]{2,1,0:T(8,128)S(1)}, f32[208,512]{1,0:T(8,128)S(1)}, f32[208,512]{1,0:T(8,128)S(1)}) custom-call(s32[1]{0:T(128)} %bitcast.core_ref, s32[1,1024]{1,0:T(1,128)} %order_hbm.1, f32[1024,384]{1,0:T(8,128)} %x_hbm.1, f32[4,1024,128]{2,1,0:T(8,128)} %v_hbm.1), custom_call_target="tpu_custom_call" | custom-call | tf_op jit(solution)/shard_map/project/pallas_call | solution.py:335
  8.8 8.7 %collective-permute-start.5 = (f32[208,512]{1,0:T(8,128)S(1)}, f32[208,512]{1,0:T(8,128)S(1)}, u32[]{:S(2)}, u32[]{:S(2)}) collective-permute-start(f32[208,512]{1,0:T(8,128)S(1)} %get-tuple-element.34), channel_id=1, source_target_pairs={{0,8},{8,0},{1,9},{9,1},{2,10},{10,2},{3,11},{11,3},{4,12},{12,4},... | collective-permute-start | bytes 1277960 | tf_op jit(solution)/shard_map/ppermute | solution.py:298
  17.6 1.4 collective-permute-done.5
  19.0 0.1 add.3.q_ref
  19.0 6.3 %all_to_all.25.parts_ref = f32[4,16,512]{2,1,0:T(8,128)S(1)} all-to-all(f32[4,16,512]{2,1,0:T(8,128)S(1)} %get-tuple-element.35), channel_id=1, replica_groups=mesh['x2'=2,'x1'=2,'z4'=2,'z2'=2,'z1'=2,'core'=2,'cols'=8] {'z1','core'}, dimensions={0} | all-to-all | bytes 262144 | tf_op jit(solution)/shard_map/all_to_all | solution.py:353
  25.4 0.8 shard_map.38
  26.2 6.3 %all-to-all-start.1 = ((f32[16,16,512]{2,1,0:T(8,128)}), f32[16,16,512]{2,1,0:T(8,128)S(1)}, u32[]{:S(2)}, u32[]{:S(2)}) async-start(f32[16,16,512]{2,1,0:T(8,128)} %shard_map.38), calls=%async_computation.1 | async-start | bytes 1048576 | tf_op jit(solution)/shard_map/all_to_all | solution.py:307
  32.5 2.5 %collective-permute-start.6 = (f32[208,512]{1,0:T(8,128)S(1)}, f32[208,512]{1,0:T(8,128)S(1)}, u32[]{:S(2)}, u32[]{:S(2)}) collective-permute-start(f32[208,512]{1,0:T(8,128)S(1)} %add.3.q_ref), channel_id=1, source_target_pairs={{0,16},{16,0},{1,17},{17,1},{2,18},{18,2},{3,19},{19,3},{4,20},{20... | collective-permute-start | bytes 1277960 | tf_op jit(solution)/shard_map/ppermute | solution.py:298
  35.0 15.2 %collective-permute-done.6.moved_ref = f32[208,512]{1,0:T(8,128)S(1)} collective-permute-done((f32[208,512]{1,0:T(8,128)S(1)}, f32[208,512]{1,0:T(8,128)S(1)}, u32[]{:S(2)}, u32[]{:S(2)}) %collective-permute-start.6) | collective-permute-done | bytes 426016 | tf_op jit(solution)/shard_map/ppermute | solution.py:298
  50.2 3.0 %collective-permute-start.7 = (f32[48,512]{1,0:T(8,128)S(1)}, f32[48,512]{1,0:T(8,128)S(1)}, u32[]{:S(2)}, u32[]{:S(2)}) collective-permute-start(f32[48,512]{1,0:T(8,128)S(1)} %get-tuple-element.36.w_own_ref), channel_id=1, source_target_pairs={{0,32},{32,0},{1,33},{33,1},{2,34},{34,2},{3,35},{35,3},{4,36},{36... | collective-permute-start | bytes 294920 | tf_op jit(solution)/shard_map/ppermute | solution.py:298
  53.2 0.0 all-to-all-done.1
  53.2 6.0 %shard_map.39.inv_ref = f32[128,128]{1,0:T(8,128)S(1)} custom-call(s32[1]{0:T(128)} %bitcast.4.side_ref, f32[2,8,16,512]{3,2,1,0:T(8,128)S(1)} %bitcast.9), custom_call_target="tpu_custom_call" | custom-call | tf_op jit(solution)/shard_map/pallas_call | solution.py:284
  59.2 0.0 collective-permute-done.7.w_sib_ref
  59.2 1.7 shard_map.41
  60.9 11.5 %all-to-all-start.2 = ((f32[16,16,384]{2,1,0:T(8,128)}), f32[16,16,384]{2,1,0:T(8,128)S(1)}, u32[]{:S(2)}, u32[]{:S(2)}) async-start(f32[16,16,384]{2,1,0:T(8,128)} %get-tuple-element.37), calls=%async_computation.2 | async-start | bytes 786432 | tf_op jit(solution)/shard_map/all_to_all | solution.py:313
  72.4 4.7 %collective-permute-start.8 = (f32[32,384]{1,0:T(8,128)S(1)}, f32[32,384]{1,0:T(8,128)S(1)}, u32[]{:S(2)}, u32[]{:S(2)}) collective-permute-start(f32[32,384]{1,0:T(8,128)S(1)} %get-tuple-element.38.w_own_ref), channel_id=1, source_target_pairs={{0,112},{16,96},{32,80},{48,64},{64,48},{80,32},{96,16},{112,0},{1... | collective-permute-start | bytes 147464 | tf_op jit(solution)/shard_map/ppermute | solution.py:303
  77.0 8.3 %all-to-all-done.2 = f32[16,16,384]{2,1,0:T(8,128)S(1)} async-done(((f32[16,16,384]{2,1,0:T(8,128)}), f32[16,16,384]{2,1,0:T(8,128)S(1)}, u32[]{:S(2)}, u32[]{:S(2)}) %all-to-all-start.2) | async-done | bytes 393248 | tf_op jit(solution)/shard_map/all_to_all | solution.py:313
  85.3 6.0 %shard_map.42.inv_ref = f32[128,128]{1,0:T(8,128)S(1)} custom-call(s32[1]{0:T(128)} %bitcast.3.side_ref, f32[2,8,16,384]{3,2,1,0:T(8,128)S(1)} %bitcast.15), custom_call_target="tpu_custom_call" | custom-call | tf_op jit(solution)/shard_map/pallas_call | solution.py:284
  91.3 0.0 collective-permute-done.8.w_sib_ref
  91.3 1.7 shard_map.43
  93.0 5.5 %all-to-all-start.3 = ((f32[16,32,256]{2,1,0:T(8,128)}), f32[16,32,256]{2,1,0:T(8,128)S(1)}, u32[]{:S(2)}, u32[]{:S(2)}) async-start(f32[16,32,256]{2,1,0:T(8,128)} %get-tuple-element.40), calls=%async_computation.3 | async-start | bytes 1048576 | tf_op jit(solution)/shard_map/all_to_all | solution.py:307
  98.5 4.8 %collective-permute-start.10 = (f32[160,512]{1,0:T(8,128)S(1)}, f32[160,512]{1,0:T(8,128)S(1)}, u32[]{:S(2)}, u32[]{:S(2)}) collective-permute-start(f32[160,512]{1,0:T(8,128)S(1)} %get-tuple-element.42.t_own_ref), channel_id=1, source_target_pairs={{0,32},{32,0},{1,33},{33,1},{2,34},{34,2},{3,35},{35,3},{4,36},{36... | collective-permute-start | bytes 983048 | tf_op jit(solution)/shard_map/ppermute | solution.py:298
  103.3 3.3 %collective-permute-start.1 = (f32[64,1024]{1,0:T(8,128)S(1)}, f32[64,1024]{1,0:T(8,128)S(1)}, u32[]{:S(2)}, u32[]{:S(2)}) collective-permute-start(f32[64,1024]{1,0:T(8,128)S(1)} %get-tuple-element.29.own_ref.wt_ref), channel_id=1, source_target_pairs={{7,0},{0,1},{1,2},{2,3},{3,4},{4,5},{5,6},{6,7},{15,8},{8,9},{9,10... | collective-permute-start | bytes 786440 | tf_op jit(solution)/shard_map/ppermute | solution.py:362
  106.6 3.2 %collective-permute-start = (f32[64,1024]{1,0:T(8,128)S(1)}, f32[64,1024]{1,0:T(8,128)S(1)}, u32[]{:S(2)}, u32[]{:S(2)}) collective-permute-start(f32[64,1024]{1,0:T(8,128)S(1)} %get-tuple-element.29.own_ref.wt_ref), channel_id=1, source_target_pairs={{1,0},{2,1},{3,2},{4,3},{5,4},{6,5},{7,6},{0,7},{9,8},{10,9},{11,1... | collective-permute-start | bytes 786440 | tf_op jit(solution)/shard_map/ppermute | solution.py:362
  109.8 0.1 all-to-all-done.3
  110.0 6.4 %all-to-all-start.4 = ((f32[8,80,128]{2,1,0:T(8,128)}), f32[8,80,128]{2,1,0:T(8,128)S(1)}, u32[]{:S(2)}, u32[]{:S(2)}) async-start(f32[8,80,128]{2,1,0:T(8,128)} %get-tuple-element.50), calls=%async_computation.4 | async-start | bytes 655360 | tf_op jit(solution)/shard_map/all_to_all | solution.py:390
  116.4 0.7 collective-permute-done.10.t_sib_ref
  117.1 1.2 shard_map.47
  118.3 2.4 %collective-permute-start.11 = (f32[160,384]{1,0:T(8,128)S(1)}, f32[160,384]{1,0:T(8,128)S(1)}, u32[]{:S(2)}, u32[]{:S(2)}) collective-permute-start(f32[160,384]{1,0:T(8,128)S(1)} %get-tuple-element.43.t_own_ref), channel_id=1, source_target_pairs={{0,112},{16,96},{32,80},{48,64},{64,48},{80,32},{96,16},{112,0},{1... | collective-permute-start | bytes 737288 | tf_op jit(solution)/shard_map/ppermute | solution.py:303
  120.7 0.0 collective-permute-done.1.down_ref.refs_1_
  120.8 0.0 collective-permute-done.up_ref.refs_0_
  120.8 1.0 shard_map.37
  121.8 5.5 %collective-permute-start.2 = (f32[128,1024]{1,0:T(8,128)}, f32[128,1024]{1,0:T(8,128)S(1)}, u32[]{:S(2)}, u32[]{:S(2)}) collective-permute-start(f32[128,1024]{1,0:T(8,128)} %get-tuple-element.30), channel_id=1, source_target_pairs={{2,0},{3,1},{4,2},{5,3},{6,4},{7,5},{0,6},{1,7},{10,8},{11,9},{12,... | collective-permute-start | bytes 1572872 | tf_op jit(solution)/shard_map/ppermute | solution.py:362
  127.3 2.4 %collective-permute-done.11.t_sib_ref = f32[160,384]{1,0:T(8,128)S(1)} collective-permute-done((f32[160,384]{1,0:T(8,128)S(1)}, f32[160,384]{1,0:T(8,128)S(1)}, u32[]{:S(2)}, u32[]{:S(2)}) %collective-permute-start.11) | collective-permute-done | bytes 245792 | tf_op jit(solution)/shard_map/ppermute | solution.py:303
  129.7 1.0 shard_map.48
  130.7 3.7 %collective-permute-start.12 = (f32[160,256]{1,0:T(8,128)S(1)}, f32[160,256]{1,0:T(8,128)S(1)}, u32[]{:S(2)}, u32[]{:S(2)}) collective-permute-start(f32[160,256]{1,0:T(8,128)S(1)} %get-tuple-element.44.t_own_ref), channel_id=1, source_target_pairs={{0,128},{128,0},{1,129},{129,1},{2,130},{130,2},{3,131},{131,3},{4... | collective-permute-start | bytes 491528 | tf_op jit(solution)/shard_map/ppermute | solution.py:298
  134.4 3.7 %collective-permute-start.3 = (f32[128,1024]{1,0:T(8,128)}, f32[128,1024]{1,0:T(8,128)}, u32[]{:S(2)}, u32[]{:S(2)}) collective-permute-start(f32[128,1024]{1,0:T(8,128)} %get-tuple-element.31), channel_id=1, source_target_pairs={{6,0},{7,1},{0,2},{1,3},{2,4},{3,5},{4,6},{5,7},{14,8},{15,9},{8,1... | collective-permute-start | bytes 1572872 | tf_op jit(solution)/shard_map/ppermute | solution.py:362
  138.1 6.0 %shard_map.44.inv_ref = f32[128,128]{1,0:T(8,128)S(1)} custom-call(s32[1]{0:T(128)} %bitcast.2.side_ref, f32[2,8,32,256]{3,2,1,0:T(8,128)S(1)} %bitcast.12), custom_call_target="tpu_custom_call" | custom-call | tf_op jit(solution)/shard_map/pallas_call | solution.py:284
  144.1 0.0 collective-permute-done.12.t_sib_ref
  144.1 1.0 shard_map.49
  145.1 3.3 %collective-permute-start.13 = (f32[160,128]{1,0:T(8,128)S(1)}, f32[160,128]{1,0:T(8,128)S(1)}, u32[]{:S(2)}, u32[]{:S(2)}) collective-permute-start(f32[160,128]{1,0:T(8,128)S(1)} %get-tuple-element.45.t_own_ref), channel_id=1, source_target_pairs={{0,384},{128,256},{256,128},{384,0},{1,385},{129,257},{257,129},{3... | collective-permute-start | bytes 245768 | tf_op jit(solution)/shard_map/ppermute | solution.py:303
  148.4 1.0 shard_map.45
  149.4 3.4 %collective-permute-start.9 = (f32[128,128]{1,0:T(8,128)S(1)}, f32[128,128]{1,0:T(8,128)S(1)}, u32[]{:S(2)}, u32[]{:S(2)}) collective-permute-start(f32[128,128]{1,0:T(8,128)S(1)} %get-tuple-element.41.own_ref.a_own_ref), channel_id=1, source_target_pairs={{0,384},{128,256},{256,128},{384,0},{1,385},{129,257},{257,129},{3... | collective-permute-start | bytes 196616 | tf_op jit(solution)/shard_map/ppermute | solution.py:303
  152.9 3.2 %collective-permute-done.9.sib_ref.a_sib_ref = f32[128,128]{1,0:T(8,128)S(1)} collective-permute-done((f32[128,128]{1,0:T(8,128)S(1)}, f32[128,128]{1,0:T(8,128)S(1)}, u32[]{:S(2)}, u32[]{:S(2)}) %collective-permute-start.9) | collective-permute-done | bytes 65568 | tf_op jit(solution)/shard_map/ppermute | solution.py:303
  156.0 6.0 %shard_map.46.inv_ref = f32[128,128]{1,0:T(8,128)S(1)} custom-call(f32[128,128]{1,0:T(8,128)S(1)} %get-tuple-element.41.own_ref.a_own_ref, f32[128,128]{1,0:T(8,128)S(1)} %collective-permute-done.9.sib_ref.a_sib_ref), custom_call_target="tpu_custom_call" | custom-call | tf_op jit(solution)/shard_map/pallas_call | solution.py:284
  162.0 0.0 all-to-all-done.4.refs_4_
  162.0 0.0 collective-permute-done.13.t_sib_ref
  162.0 1.9 %shard_map.50.refs_5_ = f32[160,512]{1,0:T(8,128)S(1)} custom-call(f32[128,128]{1,0:T(8,128)S(1)} %shard_map.46.inv_ref, f32[128,128]{1,0:T(8,128)S(1)} %get-tuple-element.41.own_ref.a_own_ref, f32[128,128]{1,0:T(8,128)S(1)} %collective-permute-done.9.sib_ref.a_sib_ref, f32[160,128]{1,0:T(8,128)S(1)} %get-tuple-element.45.t_own_ref, ...), custom_call_target="tpu_custom_call" | custom-call | tf_op jit(solution)/shard_map/pallas_call | solution.py:284
  163.9 8.9 %collective-permute-start.14 = (f32[160,512]{1,0:T(8,128)S(1)}, f32[160,512]{1,0:T(8,128)S(1)}, u32[]{:S(2)}, u32[]{:S(2)}) collective-permute-start(f32[160,512]{1,0:T(8,128)S(1)} %shard_map.50.refs_5_), channel_id=1, source_target_pairs={{0,8},{8,0},{1,9},{9,1},{2,10},{10,2},{3,11},{11,3},{4,12},{12,4},... | collective-permute-start | bytes 983048 | tf_op jit(solution)/shard_map/ppermute | solution.py:298
  172.9 0.0 collective-permute-done.2.refs_2_
  172.9 3.4 %collective-permute-start.4 = (f32[64,1024]{1,0:T(8,128)S(1)}, f32[64,1024]{1,0:T(8,128)S(1)}, u32[]{:S(2)}, u32[]{:S(2)}) collective-permute-start(f32[64,1024]{1,0:T(8,128)S(1)} %slice.4), channel_id=1, source_target_pairs={{1,0},{2,1},{3,2},{4,3},{5,4},{6,5},{7,6},{0,7},{9,8},{10,9},{11,1... | collective-permute-start | bytes 786440 | tf_op jit(solution)/shard_map/ppermute | solution.py:362
  176.3 0.0 collective-permute-done.3.refs_3_
  176.3 6.3 %collective-permute-done.4.refs_4_ = f32[64,1024]{1,0:T(8,128)S(1)} collective-permute-done((f32[64,1024]{1,0:T(8,128)S(1)}, f32[64,1024]{1,0:T(8,128)S(1)}, u32[]{:S(2)}, u32[]{:S(2)}) %collective-permute-start.4) | collective-permute-done | bytes 262176 | tf_op jit(solution)/shard_map/ppermute | solution.py:362
  182.6 0.0 collective-permute-done.14.refs_6_
  182.6 4.3 %shard_map.51 = f32[320,1024]{1,0:T(8,128)} custom-call(s32[1]{0:T(128)} %bitcast.core_ref, s32[1]{0:T(128)} %bitcast.1.col_ref, f32[320,1024]{1,0:T(8,128)} %get-tuple-element.28.xt_ref, f32[64,1024]{1,0:T(8,128)S(1)} %get-tuple-element.29.own_ref.wt_ref, f32[64,1024]{1,0:T(8,128)S(1)} %collective-permute-done.up_ref.refs_0_, ...), custom_call_target="tpu_custom_call" | custom-call | tf_op jit(solution)/shard_map/pallas_call | solution.py:284
  (2 shorter events, 0.1 us)
Async XLA Ops:
  8.8 10.1 %collective-permute-start.5 = (f32[208,512]{1,0:T(8,128)S(1)}, f32[208,512]{1,0:T(8,128)S(1)}, u32[]{:S(2)}, u32[]{:S(2)}) collective-permute-start(f32[208,512]{1,0:T(8,128)S(1)} %get-tuple-element.34), channel_id=1, source_target_pairs={{0,8},{8,0},{1,9},{9,1},{2,10},{10,2},{3,11},{11,3},{4,12},{12,4},... | collective-permute-start | bytes 1277960 | tf_op jit(solution)/shard_map/ppermute | solution.py:298
  26.2 27.0 %all-to-all-start.1 = ((f32[16,16,512]{2,1,0:T(8,128)}), f32[16,16,512]{2,1,0:T(8,128)S(1)}, u32[]{:S(2)}, u32[]{:S(2)}) async-start(f32[16,16,512]{2,1,0:T(8,128)} %shard_map.38), calls=%async_computation.1 | async-start | bytes 1048576 | tf_op jit(solution)/shard_map/all_to_all | solution.py:307
  32.5 17.7 %collective-permute-start.6 = (f32[208,512]{1,0:T(8,128)S(1)}, f32[208,512]{1,0:T(8,128)S(1)}, u32[]{:S(2)}, u32[]{:S(2)}) collective-permute-start(f32[208,512]{1,0:T(8,128)S(1)} %add.3.q_ref), channel_id=1, source_target_pairs={{0,16},{16,0},{1,17},{17,1},{2,18},{18,2},{3,19},{19,3},{4,20},{20... | collective-permute-start | bytes 1277960 | tf_op jit(solution)/shard_map/ppermute | solution.py:298
  50.2 9.0 %collective-permute-start.7 = (f32[48,512]{1,0:T(8,128)S(1)}, f32[48,512]{1,0:T(8,128)S(1)}, u32[]{:S(2)}, u32[]{:S(2)}) collective-permute-start(f32[48,512]{1,0:T(8,128)S(1)} %get-tuple-element.36.w_own_ref), channel_id=1, source_target_pairs={{0,32},{32,0},{1,33},{33,1},{2,34},{34,2},{3,35},{35,3},{4,36},{36... | collective-permute-start | bytes 294920 | tf_op jit(solution)/shard_map/ppermute | solution.py:298
  60.9 24.5 %all-to-all-start.2 = ((f32[16,16,384]{2,1,0:T(8,128)}), f32[16,16,384]{2,1,0:T(8,128)S(1)}, u32[]{:S(2)}, u32[]{:S(2)}) async-start(f32[16,16,384]{2,1,0:T(8,128)} %get-tuple-element.37), calls=%async_computation.2 | async-start | bytes 786432 | tf_op jit(solution)/shard_map/all_to_all | solution.py:313
  72.4 18.9 %collective-permute-start.8 = (f32[32,384]{1,0:T(8,128)S(1)}, f32[32,384]{1,0:T(8,128)S(1)}, u32[]{:S(2)}, u32[]{:S(2)}) collective-permute-start(f32[32,384]{1,0:T(8,128)S(1)} %get-tuple-element.38.w_own_ref), channel_id=1, source_target_pairs={{0,112},{16,96},{32,80},{48,64},{64,48},{80,32},{96,16},{112,0},{1... | collective-permute-start | bytes 147464 | tf_op jit(solution)/shard_map/ppermute | solution.py:303
  93.0 16.9 %all-to-all-start.3 = ((f32[16,32,256]{2,1,0:T(8,128)}), f32[16,32,256]{2,1,0:T(8,128)S(1)}, u32[]{:S(2)}, u32[]{:S(2)}) async-start(f32[16,32,256]{2,1,0:T(8,128)} %get-tuple-element.40), calls=%async_computation.3 | async-start | bytes 1048576 | tf_op jit(solution)/shard_map/all_to_all | solution.py:307
  98.5 18.6 %collective-permute-start.10 = (f32[160,512]{1,0:T(8,128)S(1)}, f32[160,512]{1,0:T(8,128)S(1)}, u32[]{:S(2)}, u32[]{:S(2)}) collective-permute-start(f32[160,512]{1,0:T(8,128)S(1)} %get-tuple-element.42.t_own_ref), channel_id=1, source_target_pairs={{0,32},{32,0},{1,33},{33,1},{2,34},{34,2},{3,35},{35,3},{4,36},{36... | collective-permute-start | bytes 983048 | tf_op jit(solution)/shard_map/ppermute | solution.py:298
  103.3 17.4 %collective-permute-start.1 = (f32[64,1024]{1,0:T(8,128)S(1)}, f32[64,1024]{1,0:T(8,128)S(1)}, u32[]{:S(2)}, u32[]{:S(2)}) collective-permute-start(f32[64,1024]{1,0:T(8,128)S(1)} %get-tuple-element.29.own_ref.wt_ref), channel_id=1, source_target_pairs={{7,0},{0,1},{1,2},{2,3},{3,4},{4,5},{5,6},{6,7},{15,8},{8,9},{9,10... | collective-permute-start | bytes 786440 | tf_op jit(solution)/shard_map/ppermute | solution.py:362
  106.6 14.2 %collective-permute-start = (f32[64,1024]{1,0:T(8,128)S(1)}, f32[64,1024]{1,0:T(8,128)S(1)}, u32[]{:S(2)}, u32[]{:S(2)}) collective-permute-start(f32[64,1024]{1,0:T(8,128)S(1)} %get-tuple-element.29.own_ref.wt_ref), channel_id=1, source_target_pairs={{1,0},{2,1},{3,2},{4,3},{5,4},{6,5},{7,6},{0,7},{9,8},{10,9},{11,1... | collective-permute-start | bytes 786440 | tf_op jit(solution)/shard_map/ppermute | solution.py:362
  110.0 52.0 %all-to-all-start.4 = ((f32[8,80,128]{2,1,0:T(8,128)}), f32[8,80,128]{2,1,0:T(8,128)S(1)}, u32[]{:S(2)}, u32[]{:S(2)}) async-start(f32[8,80,128]{2,1,0:T(8,128)} %get-tuple-element.50), calls=%async_computation.4 | async-start | bytes 655360 | tf_op jit(solution)/shard_map/all_to_all | solution.py:390
  118.3 11.4 %collective-permute-start.11 = (f32[160,384]{1,0:T(8,128)S(1)}, f32[160,384]{1,0:T(8,128)S(1)}, u32[]{:S(2)}, u32[]{:S(2)}) collective-permute-start(f32[160,384]{1,0:T(8,128)S(1)} %get-tuple-element.43.t_own_ref), channel_id=1, source_target_pairs={{0,112},{16,96},{32,80},{48,64},{64,48},{80,32},{96,16},{112,0},{1... | collective-permute-start | bytes 737288 | tf_op jit(solution)/shard_map/ppermute | solution.py:303
  121.8 51.1 %collective-permute-start.2 = (f32[128,1024]{1,0:T(8,128)}, f32[128,1024]{1,0:T(8,128)S(1)}, u32[]{:S(2)}, u32[]{:S(2)}) collective-permute-start(f32[128,1024]{1,0:T(8,128)} %get-tuple-element.30), channel_id=1, source_target_pairs={{2,0},{3,1},{4,2},{5,3},{6,4},{7,5},{0,6},{1,7},{10,8},{11,9},{12,... | collective-permute-start | bytes 1572872 | tf_op jit(solution)/shard_map/ppermute | solution.py:362
  130.7 13.4 %collective-permute-start.12 = (f32[160,256]{1,0:T(8,128)S(1)}, f32[160,256]{1,0:T(8,128)S(1)}, u32[]{:S(2)}, u32[]{:S(2)}) collective-permute-start(f32[160,256]{1,0:T(8,128)S(1)} %get-tuple-element.44.t_own_ref), channel_id=1, source_target_pairs={{0,128},{128,0},{1,129},{129,1},{2,130},{130,2},{3,131},{131,3},{4... | collective-permute-start | bytes 491528 | tf_op jit(solution)/shard_map/ppermute | solution.py:298
  134.4 41.9 %collective-permute-start.3 = (f32[128,1024]{1,0:T(8,128)}, f32[128,1024]{1,0:T(8,128)}, u32[]{:S(2)}, u32[]{:S(2)}) collective-permute-start(f32[128,1024]{1,0:T(8,128)} %get-tuple-element.31), channel_id=1, source_target_pairs={{6,0},{7,1},{0,2},{1,3},{2,4},{3,5},{4,6},{5,7},{14,8},{15,9},{8,1... | collective-permute-start | bytes 1572872 | tf_op jit(solution)/shard_map/ppermute | solution.py:362
  145.1 16.9 %collective-permute-start.13 = (f32[160,128]{1,0:T(8,128)S(1)}, f32[160,128]{1,0:T(8,128)S(1)}, u32[]{:S(2)}, u32[]{:S(2)}) collective-permute-start(f32[160,128]{1,0:T(8,128)S(1)} %get-tuple-element.45.t_own_ref), channel_id=1, source_target_pairs={{0,384},{128,256},{256,128},{384,0},{1,385},{129,257},{257,129},{3... | collective-permute-start | bytes 245768 | tf_op jit(solution)/shard_map/ppermute | solution.py:303
  149.4 6.6 %collective-permute-start.9 = (f32[128,128]{1,0:T(8,128)S(1)}, f32[128,128]{1,0:T(8,128)S(1)}, u32[]{:S(2)}, u32[]{:S(2)}) collective-permute-start(f32[128,128]{1,0:T(8,128)S(1)} %get-tuple-element.41.own_ref.a_own_ref), channel_id=1, source_target_pairs={{0,384},{128,256},{256,128},{384,0},{1,385},{129,257},{257,129},{3... | collective-permute-start | bytes 196616 | tf_op jit(solution)/shard_map/ppermute | solution.py:303
  163.9 18.7 %collective-permute-start.14 = (f32[160,512]{1,0:T(8,128)S(1)}, f32[160,512]{1,0:T(8,128)S(1)}, u32[]{:S(2)}, u32[]{:S(2)}) collective-permute-start(f32[160,512]{1,0:T(8,128)S(1)} %shard_map.50.refs_5_), channel_id=1, source_target_pairs={{0,8},{8,0},{1,9},{9,1},{2,10},{10,2},{3,11},{11,3},{4,12},{12,4},... | collective-permute-start | bytes 983048 | tf_op jit(solution)/shard_map/ppermute | solution.py:298
  172.9 9.7 %collective-permute-start.4 = (f32[64,1024]{1,0:T(8,128)S(1)}, f32[64,1024]{1,0:T(8,128)S(1)}, u32[]{:S(2)}, u32[]{:S(2)}) collective-permute-start(f32[64,1024]{1,0:T(8,128)S(1)} %slice.4), channel_id=1, source_target_pairs={{1,0},{2,1},{3,2},{4,3},{5,4},{6,5},{7,6},{0,7},{9,8},{10,9},{11,1... | collective-permute-start | bytes 786440 | tf_op jit(solution)/shard_map/ppermute | solution.py:362
